TPU v7x, 256 devices: a whole 4x4x8 slice. The times are simulated.
256 devices in a mesh: box: 16 (over z, core), agg: 16 (over y, x).
Axes of the slice: x: 4, y: 4, z: 8, core: 2. Of those that a mesh axis runs over, the one named last changes fastest.
Arguments:
- source: float32 [512, 512, 128], P('box', 'agg'), may hold values from -6 to 6
- guess: float32 [512, 512, 128], P('box', 'agg'), may hold values from -6 to 6
- reaction: float32 [512, 512, 128], P('box', 'agg'), may hold values from 0.001 to 0.02
- flags: int32 [16, 16, 4], P('box', 'agg'), may hold values from 0 to 1, as said below
Outputs:
- iterate: float32 [512, 512, 128], P('box', 'agg')
- level_one: float32 [256, 256, 64], P('box', 'agg')
- level_two: float32 [128, 128, 32], P('box', 'agg')
- level_three: float32 [64, 64, 16], P('box', 'agg')
- level_four: float32 [32, 32, 8], P('box', 'agg')
- bottom_residual: float32 [32, 32, 8], P('box', 'agg')
Inputs may be any that keep to these rules, and one draw needn't show every extreme that they name: `flags`: flags are 0 or 1; the share of refined boxes differs from device block to device block, and some blocks have none.
All inputs are finite; a program needn't handle non-finite values.
Results may differ from a plain program's by a relative error of at most 0.00018.
Values sent between devices are 32-bit elements; how exact they have to be, the bound alone decides.
No kernel may reach another device: no remote copies, remote signals or barrier semaphores. Data moves between devices by JAX's collectives and lax.ppermute only.
A program may use at most 128 MiB of HBM per device.

v0:
```python
import jax
import jax.numpy as jnp
from jax import lax
from jax.sharding import PartitionSpec as P

LEVELS = 4


def passed_along(block, axis, distance):
    devices = range(lax.axis_size(axis))
    route = [(i - distance, i) for i in devices if i - distance in devices]
    return lax.ppermute(block, axis, route)


def extended(block, sides, width):
    for axis, dim in sides:
        count = lax.axis_size(axis)
        forward = [(i, i + 1) for i in range(count - 1)]
        backward = [(target, source) for source, target in forward]
        low = lax.ppermute(
            lax.slice_in_dim(block, block.shape[dim] - width, None, axis=dim), axis, forward
        )
        high = lax.ppermute(lax.slice_in_dim(block, 0, width, axis=dim), axis, backward)
        block = jnp.concatenate([low, block, high], axis=dim)
    return block


def swapped(block, axis, bit):
    count = lax.axis_size(axis)
    route = []
    for low in range(count):
        high = low | 1 << bit
        if high != low and high < count:
            route += [(low, high), (high, low)]
    return lax.ppermute(block, axis, route)


def neighbours(padded):
    count_x = padded.shape[0] - 2
    count_y = padded.shape[1] - 2
    count_z = padded.shape[2] - 2
    face_sum = jnp.zeros((count_x, count_y, count_z), jnp.float32)
    edge_sum = jnp.zeros((count_x, count_y, count_z), jnp.float32)
    corner_sum = jnp.zeros((count_x, count_y, count_z), jnp.float32)
    for step_x in (-1, 0, 1):
        for step_y in (-1, 0, 1):
            for step_z in (-1, 0, 1):
                moved = abs(step_x) + abs(step_y) + abs(step_z)
                if moved == 0:
                    continue
                window = padded[
                    1 + step_x : 1 + step_x + count_x,
                    1 + step_y : 1 + step_y + count_y,
                    1 + step_z : 1 + step_z + count_z,
                ]
                if moved == 1:
                    face_sum = face_sum + window
                elif moved == 2:
                    edge_sum = edge_sum + window
                else:
                    corner_sum = corner_sum + window
    return (face_sum + 0.5 * edge_sum + 0.25 * corner_sum) / 14.0


def padded_field(values, stride):
    top_plane = values[:, -1:, :]
    bottom_plane = values[:, :1, :]
    if stride < lax.axis_size("agg"):
        from_below = passed_along(top_plane, "agg", stride)
        from_above = passed_along(bottom_plane, "agg", -stride)
    else:
        from_below = jnp.zeros_like(top_plane)
        from_above = jnp.zeros_like(bottom_plane)
    padded_y = jnp.concatenate([from_below, values, from_above], axis=1)
    padded_xy = extended(padded_y, (("box", 0),), 1)
    return jnp.pad(padded_xy, ((0, 0), (0, 0), (1, 1)))


def operate(values, coefficient, stride):
    padded = padded_field(values, stride)
    return values - neighbours(padded) + coefficient * values


def restrict(values):
    size_a, size_b, size_c = values.shape
    return values.reshape(size_a // 2, 2, size_b // 2, 2, size_c // 2, 2).sum(axis=(1, 3, 5)) * 0.5


def cell_mask(flags, shape):
    boxes_x, boxes_y, boxes_z = flags.shape
    spread = jnp.broadcast_to(
        flags.astype(jnp.float32)[:, None, :, None, :, None],
        (boxes_x, shape[0] // boxes_x, boxes_y, shape[1] // boxes_y, boxes_z, shape[2] // boxes_z),
    )
    return spread.reshape(shape)


def coefficients(level_index):
    upper_edge = 1.1 * (2.0 + 0.02 * 4.0**level_index)
    lower_edge = upper_edge / 8.0
    midpoint = (upper_edge + lower_edge) / 2.0
    half_span = (upper_edge - lower_edge) / 2.0
    sigma_value = midpoint / half_span
    rho_first = 1.0 / sigma_value
    rho_second = 1.0 / (2.0 * sigma_value - rho_first)
    return (midpoint, rho_second * rho_first, 2.0 * rho_second / half_span)


def merge_pairs(coarse_source, coarse_reaction, stride, position):
    theirs_source, theirs_reaction = swapped(
        (coarse_source, coarse_reaction), "agg", stride.bit_length() - 1
    )
    upper_half = position // stride % 2 == 1
    merged_source = jnp.where(
        upper_half,
        jnp.concatenate([theirs_source, coarse_source], axis=1),
        jnp.concatenate([coarse_source, theirs_source], axis=1),
    )
    merged_reaction = jnp.where(
        upper_half,
        jnp.concatenate([theirs_reaction, coarse_reaction], axis=1),
        jnp.concatenate([coarse_reaction, theirs_reaction], axis=1),
    )
    return (merged_source, merged_reaction)


def per_device(source, guess, reaction, flags):
    position = lax.axis_index("agg")
    fine_rows = source.shape[1]
    refined = cell_mask(flags, source.shape)
    midpoint, factor_one, factor_two = coefficients(0)
    first_residual = refined * (source - operate(guess, reaction, 1))
    first_step = first_residual / midpoint
    current = guess + first_step
    mid_residual = refined * (source - operate(current, reaction, 1))
    second_step = factor_one * first_step + factor_two * mid_residual
    current = current + second_step
    residual = refined * (source - operate(current, reaction, 1))
    results = [current]
    coarse_reaction = reaction
    stride = 1
    extent = fine_rows
    for level_index in range(1, LEVELS + 1):
        coarse_source = restrict(residual)
        coarse_reaction = restrict(coarse_reaction)
        extent = extent // 2
        coarse_source, coarse_reaction = merge_pairs(
            coarse_source, coarse_reaction, stride, position
        )
        stride = stride * 2
        extent = extent * 2
        midpoint, factor_one, factor_two = coefficients(level_index)
        first_step = coarse_source / midpoint
        mid_residual = coarse_source - operate(first_step, coarse_reaction, stride)
        second_step = factor_one * first_step + factor_two * mid_residual
        correction = first_step + second_step
        residual = coarse_source - operate(correction, coarse_reaction, stride)
        own_rows = fine_rows >> level_index
        local_start = position * own_rows - position // stride * extent
        results.append(lax.dynamic_slice_in_dim(correction, local_start, own_rows, 1))
        if level_index == LEVELS:
            bottom_residual = lax.dynamic_slice_in_dim(residual, local_start, own_rows, 1)
    return (results[0], results[1], results[2], results[3], results[4], bottom_residual)


def solution(mesh):
    in_specs = (
        P("box", "agg", None),
        P("box", "agg", None),
        P("box", "agg", None),
        P("box", "agg", None),
    )
    out_specs = (
        P("box", "agg", None),
        P("box", "agg", None),
        P("box", "agg", None),
        P("box", "agg", None),
        P("box", "agg", None),
        P("box", "agg", None),
    )
    return jax.shard_map(
        per_device, mesh=mesh, in_specs=in_specs, out_specs=out_specs, check_vma=False
    )
```

profile of v0, /device:TPU:97, one launch (start us, length us, event | category | flops | bytes accessed | tf_op | source)
XLA Modules:
  0.0 348.4 jit_solution(18303555956371934038)
XLA Ops:
  10.1 6.7 %collective-permute-start.2 = (f32[1,34,128]{2,1,0:T(8,128)S(1)}, f32[1,34,128]{2,1,0:T(8,128)S(1)}, u32[]{:S(2)}, u32[]{:S(2)}) collective-permute-start(f32[1,34,128]{2,1,0:T(8,128)S(1)} %get-tuple-element.40), channel_id=1, source_target_pairs={{0,16},{16,32},{32,48},{48,64},{64,80},{80,96},{96,112},{112,128},... | collective-permute-start | bytes 52232 | tf_op jit(solution)/shard_map/ppermute | solution.py:20
  19.5 3.6 %collective-permute-done.3 = f32[1,34,128]{2,1,0:T(8,128)S(1)} collective-permute-done((f32[1,34,128]{2,1,0:T(8,128)S(1)}, f32[1,34,128]{2,1,0:T(8,128)S(1)}, u32[]{:S(2)}, u32[]{:S(2)}) %collective-permute-start.3) | collective-permute-done | bytes 17440 | tf_op jit(solution)/shard_map/ppermute | solution.py:23
  34.8 3.4 collective-permute-start.6
  40.1 4.4 %collective-permute-done.7 = f32[1,34,128]{2,1,0:T(8,128)S(1)} collective-permute-done((f32[1,34,128]{2,1,0:T(8,128)S(1)}, f32[1,34,128]{2,1,0:T(8,128)S(1)}, u32[]{:S(2)}, u32[]{:S(2)}) %collective-permute-start.7) | collective-permute-done | bytes 17440 | tf_op jit(solution)/shard_map/ppermute | solution.py:23
  46.6 4.4 %collective-permute-start.8 = (f32[32,1,128]{2,1,0:T(1,128)S(1)}, f32[32,1,128]{2,1,0:T(1,128)S(1)}, u32[]{:S(2)}, u32[]{:S(2)}) collective-permute-start(f32[32,1,128]{2,1,0:T(1,128)S(1)} %get-tuple-element.42), channel_id=1, source_target_pairs={{0,1},{1,2},{2,3},{3,4},{4,5},{5,6},{6,7},{7,8},{8,9},{9,10},{10,1... | collective-permute-start | bytes 49160 | tf_op jit(solution)/shard_map/ppermute | solution.py:12
  52.3 3.5 collective-permute-done.9
  60.8 4.4 %collective-permute-done.11 = f32[1,34,128]{2,1,0:T(8,128)S(1)} collective-permute-done((f32[1,34,128]{2,1,0:T(8,128)S(1)}, f32[1,34,128]{2,1,0:T(8,128)S(1)}, u32[]{:S(2)}, u32[]{:S(2)}) %collective-permute-start.11) | collective-permute-done | bytes 17440 | tf_op jit(solution)/shard_map/ppermute | solution.py:23
  67.3 34.8 %reshape.47 = f32[16,2,16,2,64,2]{5,4,3,2,1,0:T(8,128)} reshape(f32[32,32,128]{2,1,0:T(8,128)S(1)} %fusion.7) | data formatting | bytes 1048576 | tf_op jit(solution)/shard_map/reshape | solution.py:86
  102.1 12.2 %reduce_sum.72 = f32[16,16,64]{2,1,0:T(8,128)S(1)} reduce(f32[16,2,16,2,64,2]{5,4,3,2,1,0:T(8,128)} %reshape.47, f32[]{:T(128)} %constant.137.clone.1), dimensions={1,3,5}, to_apply=%region_0.1 | reduce | flops 114688 | bytes 589828 | tf_op jit(solution)/shard_map/reduce_sum | solution.py:86
  118.7 5.8 %collective-permute-start.13 = (f32[16,1,64]{2,1,0:T(1,128)S(1)}, f32[16,1,64]{2,1,0:T(1,128)S(1)}, u32[]{:S(2)}, u32[]{:S(2)}) collective-permute-start(f32[16,1,64]{2,1,0:T(1,128)S(1)} %get-tuple-element.58), channel_id=1, source_target_pairs={{0,2},{1,3},{2,4},{3,5},{4,6},{5,7},{6,8},{7,9},{8,10},{9,11},{10,... | collective-permute-start | bytes 12296 | tf_op jit(solution)/shard_map/ppermute | solution.py:12
  125.8 34.8 %reshape.48 = f32[16,2,16,2,64,2]{5,4,3,2,1,0:T(8,128)} reshape(f32[32,32,128]{2,1,0:T(8,128)S(1)} %copy-done.2) | data formatting | bytes 1048576 | tf_op jit(solution)/shard_map/reshape | solution.py:86
  160.7 12.2 %reduce_sum.73 = f32[16,16,64]{2,1,0:T(8,128)S(1)} reduce(f32[16,2,16,2,64,2]{5,4,3,2,1,0:T(8,128)} %reshape.48, f32[]{:T(128)} %constant.137.clone.1), dimensions={1,3,5}, to_apply=%region_1.2 | reduce | flops 114688 | bytes 589828 | tf_op jit(solution)/shard_map/reduce_sum | solution.py:86
  184.1 5.4 %collective-permute-start.18 = (f32[16,1,64]{2,1,0:T(1,128)S(1)}, f32[16,1,64]{2,1,0:T(1,128)S(1)}, u32[]{:S(2)}, u32[]{:S(2)}) collective-permute-start(f32[16,1,64]{2,1,0:T(1,128)S(1)} %get-tuple-element.56), channel_id=1, source_target_pairs={{0,2},{1,3},{2,4},{3,5},{4,6},{5,7},{6,8},{7,9},{8,10},{9,11},{10,... | collective-permute-start | bytes 12296 | tf_op jit(solution)/shard_map/ppermute | solution.py:12
  190.9 4.6 %collective-permute-done.19 = f32[16,1,64]{2,1,0:T(1,128)S(1)} collective-permute-done((f32[16,1,64]{2,1,0:T(1,128)S(1)}, f32[16,1,64]{2,1,0:T(1,128)S(1)}, u32[]{:S(2)}, u32[]{:S(2)}) %collective-permute-start.19) | collective-permute-done | bytes 4128 | tf_op jit(solution)/shard_map/ppermute | solution.py:12
  195.5 6.6 %collective-permute-start.20 = (f32[1,34,64]{2,1,0:T(8,128)S(1)}, f32[1,34,64]{2,1,0:T(8,128)S(1)}, u32[]{:S(2)}, u32[]{:S(2)}) collective-permute-start(f32[1,34,64]{2,1,0:T(8,128)S(1)} %get-tuple-element.50), channel_id=1, source_target_pairs={{0,16},{16,32},{32,48},{48,64},{64,80},{80,96},{96,112},{112,128},... | collective-permute-start | bytes 26120 | tf_op jit(solution)/shard_map/ppermute | solution.py:20
  204.0 4.4 %collective-permute-done.21 = f32[1,34,64]{2,1,0:T(8,128)S(1)} collective-permute-done((f32[1,34,64]{2,1,0:T(8,128)S(1)}, f32[1,34,64]{2,1,0:T(8,128)S(1)}, u32[]{:S(2)}, u32[]{:S(2)}) %collective-permute-start.21) | collective-permute-done | bytes 8736 | tf_op jit(solution)/shard_map/ppermute | solution.py:23
  209.4 10.1 %reshape.49 = f32[8,2,16,2,32,2]{5,4,3,2,1,0:T(8,128)} reshape(f32[16,32,64]{2,1,0:T(8,128)S(1)} %fusion.43) | data formatting | bytes 262144 | tf_op jit(solution)/shard_map/reshape | solution.py:86
  219.5 4.1 %reduce_sum.74 = f32[8,16,32]{2,1,0:T(8,128)S(1)} reduce(f32[8,2,16,2,32,2]{5,4,3,2,1,0:T(8,128)} %reshape.49, f32[]{:T(128)} %constant.137.clone.1), dimensions={1,3,5}, to_apply=%region_2.3 | reduce | flops 28672 | bytes 147460 | tf_op jit(solution)/shard_map/reduce_sum | solution.py:86
  232.8 10.1 %select_n.118 = f32[8,2,16,2,32,2]{5,4,3,2,1,0:T(8,128)} reshape(f32[16,32,64]{2,1,0:T(8,128)S(1)} %maximum_select_fusion.1) | data formatting | bytes 262144 | tf_op jit(solution)/shard_map/jit(_where)/select_n | solution.py:119
  242.9 4.1 %reduce_sum.75 = f32[8,16,32]{2,1,0:T(8,128)S(1)} reduce(f32[8,2,16,2,32,2]{5,4,3,2,1,0:T(8,128)} %select_n.118, f32[]{:T(128)} %constant.137.clone.1), dimensions={1,3,5}, to_apply=%region_3.4 | reduce | flops 28672 | bytes 147460 | tf_op jit(solution)/shard_map/reduce_sum | solution.py:86
  247.0 3.4 collective-permute-start.25
  257.7 4.0 %collective-permute-start.28 = (f32[8,1,32]{2,1,0:T(1,128)S(1)}, f32[8,1,32]{2,1,0:T(1,128)S(1)}, u32[]{:S(2)}, u32[]{:S(2)}) collective-permute-start(f32[8,1,32]{2,1,0:T(1,128)S(1)} %get-tuple-element.68), channel_id=1, source_target_pairs={{0,4},{1,5},{2,6},{3,7},{4,8},{5,9},{6,10},{7,11},{8,12},{9,13},{1... | collective-permute-start | bytes 3080 | tf_op jit(solution)/shard_map/ppermute | solution.py:12
  266.1 7.4 %collective-permute-start.30 = (f32[1,34,32]{2,1,0:T(8,128)S(1)}, f32[1,34,32]{2,1,0:T(8,128)S(1)}, u32[]{:S(2)}, u32[]{:S(2)}) collective-permute-start(f32[1,34,32]{2,1,0:T(8,128)S(1)} %get-tuple-element.62), channel_id=1, source_target_pairs={{0,16},{16,32},{32,48},{48,64},{64,80},{80,96},{96,112},{112,128},... | collective-permute-start | bytes 13064 | tf_op jit(solution)/shard_map/ppermute | solution.py:20
  275.6 4.3 %collective-permute-done.31 = f32[1,34,32]{2,1,0:T(8,128)S(1)} collective-permute-done((f32[1,34,32]{2,1,0:T(8,128)S(1)}, f32[1,34,32]{2,1,0:T(8,128)S(1)}, u32[]{:S(2)}, u32[]{:S(2)}) %collective-permute-start.31) | collective-permute-done | bytes 4384 | tf_op jit(solution)/shard_map/ppermute | solution.py:23
  289.3 4.2 %collective-permute-done.34 = f32[4,1,16]{2,1,0:T(1,128)S(1)} collective-permute-done((f32[4,1,16]{2,1,0:T(1,128)S(1)}, f32[4,1,16]{2,1,0:T(1,128)S(1)}, u32[]{:S(2)}, u32[]{:S(2)}) %collective-permute-start.34) | collective-permute-done | bytes 288 | tf_op jit(solution)/shard_map/ppermute | solution.py:12
  293.7 4.5 %collective-permute-start.35 = (f32[1,34,16]{1,2,0:T(8,128)S(1)}, f32[1,34,16]{1,2,0:T(8,128)S(1)}, u32[]{:S(2)}, u32[]{:S(2)}) collective-permute-start(f32[1,34,16]{1,2,0:T(8,128)S(1)} %get-tuple-element.78), channel_id=1, source_target_pairs={{0,16},{16,32},{32,48},{48,64},{64,80},{80,96},{96,112},{112,128},... | collective-permute-start | bytes 6536 | tf_op jit(solution)/shard_map/ppermute | solution.py:20
  300.5 4.1 %collective-permute-done.36 = f32[1,34,16]{1,2,0:T(8,128)S(1)} collective-permute-done((f32[1,34,16]{1,2,0:T(8,128)S(1)}, f32[1,34,16]{1,2,0:T(8,128)S(1)}, u32[]{:S(2)}, u32[]{:S(2)}) %collective-permute-start.36) | collective-permute-done | bytes 2208 | tf_op jit(solution)/shard_map/ppermute | solution.py:23
  309.2 3.9 %collective-permute-done.39 = f32[4,1,16]{2,1,0:T(1,128)S(1)} collective-permute-done((f32[4,1,16]{2,1,0:T(1,128)S(1)}, f32[4,1,16]{2,1,0:T(1,128)S(1)}, u32[]{:S(2)}, u32[]{:S(2)}) %collective-permute-start.39) | collective-permute-done | bytes 288 | tf_op jit(solution)/shard_map/ppermute | solution.py:12
  313.3 3.4 collective-permute-start.40
  318.8 4.1 %collective-permute-done.41 = f32[1,34,16]{1,2,0:T(8,128)S(1)} collective-permute-done((f32[1,34,16]{1,2,0:T(8,128)S(1)}, f32[1,34,16]{1,2,0:T(8,128)S(1)}, u32[]{:S(2)}, u32[]{:S(2)}) %collective-permute-start.41) | collective-permute-done | bytes 2208 | tf_op jit(solution)/shard_map/ppermute | solution.py:23
  325.6 3.3 collective-permute-done.42
  334.7 3.6 %collective-permute-done.44 = f32[1,34,8]{1,2,0:T(8,128)S(1)} collective-permute-done((f32[1,34,8]{1,2,0:T(8,128)S(1)}, f32[1,34,8]{1,2,0:T(8,128)S(1)}, u32[]{:S(2)}, u32[]{:S(2)}) %collective-permute-start.44) | collective-permute-done | bytes 1120 | tf_op jit(solution)/shard_map/ppermute | solution.py:23
  (193 shorter events, 117.0 us)
Async XLA Ops:
  10.1 9.5 %collective-permute-start.2 = (f32[1,34,128]{2,1,0:T(8,128)S(1)}, f32[1,34,128]{2,1,0:T(8,128)S(1)}, u32[]{:S(2)}, u32[]{:S(2)}) collective-permute-start(f32[1,34,128]{2,1,0:T(8,128)S(1)} %get-tuple-element.40), channel_id=1, source_target_pairs={{0,16},{16,32},{32,48},{48,64},{64,80},{80,96},{96,112},{112,128},... | collective-permute-start | bytes 52232 | tf_op jit(solution)/shard_map/ppermute | solution.py:20
  16.8 6.3 %collective-permute-start.3 = (f32[1,34,128]{2,1,0:T(8,128)S(1)}, f32[1,34,128]{2,1,0:T(8,128)S(1)}, u32[]{:S(2)}, u32[]{:S(2)}) collective-permute-start(f32[1,34,128]{2,1,0:T(8,128)S(1)} %get-tuple-element.41), channel_id=1, source_target_pairs={{16,0},{32,16},{48,32},{64,48},{80,64},{96,80},{112,96},{128,112},... | collective-permute-start | bytes 52232 | tf_op jit(solution)/shard_map/ppermute | solution.py:23
  38.2 6.3 %collective-permute-start.7 = (f32[1,34,128]{2,1,0:T(8,128)S(1)}, f32[1,34,128]{2,1,0:T(8,128)S(1)}, u32[]{:S(2)}, u32[]{:S(2)}) collective-permute-start(f32[1,34,128]{2,1,0:T(8,128)S(1)} %get-tuple-element.37), channel_id=1, source_target_pairs={{16,0},{32,16},{48,32},{64,48},{80,64},{96,80},{112,96},{128,112},... | collective-permute-start | bytes 52232 | tf_op jit(solution)/shard_map/ppermute | solution.py:23
  46.6 5.7 %collective-permute-start.8 = (f32[32,1,128]{2,1,0:T(1,128)S(1)}, f32[32,1,128]{2,1,0:T(1,128)S(1)}, u32[]{:S(2)}, u32[]{:S(2)}) collective-permute-start(f32[32,1,128]{2,1,0:T(1,128)S(1)} %get-tuple-element.42), channel_id=1, source_target_pairs={{0,1},{1,2},{2,3},{3,4},{4,5},{5,6},{6,7},{7,8},{8,9},{9,10},{10,1... | collective-permute-start | bytes 49160 | tf_op jit(solution)/shard_map/ppermute | solution.py:12
  58.9 6.3 %collective-permute-start.11 = (f32[1,34,128]{2,1,0:T(8,128)S(1)}, f32[1,34,128]{2,1,0:T(8,128)S(1)}, u32[]{:S(2)}, u32[]{:S(2)}) collective-permute-start(f32[1,34,128]{2,1,0:T(8,128)S(1)} %get-tuple-element.33), channel_id=1, source_target_pairs={{16,0},{32,16},{48,32},{64,48},{80,64},{96,80},{112,96},{128,112},... | collective-permute-start | bytes 52232 | tf_op jit(solution)/shard_map/ppermute | solution.py:23
  118.7 54.2 %collective-permute-start.13 = (f32[16,1,64]{2,1,0:T(1,128)S(1)}, f32[16,1,64]{2,1,0:T(1,128)S(1)}, u32[]{:S(2)}, u32[]{:S(2)}) collective-permute-start(f32[16,1,64]{2,1,0:T(1,128)S(1)} %get-tuple-element.58), channel_id=1, source_target_pairs={{0,2},{1,3},{2,4},{3,5},{4,6},{5,7},{6,8},{7,9},{8,10},{9,11},{10,... | collective-permute-start | bytes 12296 | tf_op jit(solution)/shard_map/ppermute | solution.py:12
  124.5 48.4 %collective-permute-start.14 = (f32[16,1,64]{2,1,0:T(1,128)S(1)}, f32[16,1,64]{2,1,0:T(1,128)S(1)}, u32[]{:S(2)}, u32[]{:S(2)}) collective-permute-start(f32[16,1,64]{2,1,0:T(1,128)S(1)} %get-tuple-element.59), channel_id=1, source_target_pairs={{2,0},{3,1},{4,2},{5,3},{6,4},{7,5},{8,6},{9,7},{10,8},{11,9},{12,... | collective-permute-start | bytes 12296 | tf_op jit(solution)/shard_map/ppermute | solution.py:12
  172.9 6.5 %collective-permute-start.15 = (f32[1,34,64]{2,1,0:T(8,128)S(1)}, f32[1,34,64]{2,1,0:T(8,128)S(1)}, u32[]{:S(2)}, u32[]{:S(2)}) collective-permute-start(f32[1,34,64]{2,1,0:T(8,128)S(1)} %get-tuple-element.54), channel_id=1, source_target_pairs={{0,16},{16,32},{32,48},{48,64},{64,80},{80,96},{96,112},{112,128},... | collective-permute-start | bytes 26120 | tf_op jit(solution)/shard_map/ppermute | solution.py:20
  176.0 6.3 %collective-permute-start.16 = (f32[1,34,64]{2,1,0:T(8,128)S(1)}, f32[1,34,64]{2,1,0:T(8,128)S(1)}, u32[]{:S(2)}, u32[]{:S(2)}) collective-permute-start(f32[1,34,64]{2,1,0:T(8,128)S(1)} %get-tuple-element.55), channel_id=1, source_target_pairs={{16,0},{32,16},{48,32},{64,48},{80,64},{96,80},{112,96},{128,112},... | collective-permute-start | bytes 26120 | tf_op jit(solution)/shard_map/ppermute | solution.py:23
  178.0 5.4 %collective-permute-start.17 = (f32[16,16,64]{2,1,0:T(8,128)S(1)}, f32[16,16,64]{2,1,0:T(8,128)S(1)}, u32[]{:S(2)}, u32[]{:S(2)}) collective-permute-start(f32[16,16,64]{2,1,0:T(8,128)S(1)} %broadcast_multiply_fusion.2), channel_id=1, source_target_pairs={{0,1},{1,0},{2,3},{3,2},{4,5},{5,4},{6,7},{7,6},{8,9},{9,8},{10,11... | collective-permute-start | bytes 196616 | tf_op jit(solution)/shard_map/ppermute | solution.py:35
  184.1 6.7 %collective-permute-start.18 = (f32[16,1,64]{2,1,0:T(1,128)S(1)}, f32[16,1,64]{2,1,0:T(1,128)S(1)}, u32[]{:S(2)}, u32[]{:S(2)}) collective-permute-start(f32[16,1,64]{2,1,0:T(1,128)S(1)} %get-tuple-element.56), channel_id=1, source_target_pairs={{0,2},{1,3},{2,4},{3,5},{4,6},{5,7},{6,8},{7,9},{8,10},{9,11},{10,... | collective-permute-start | bytes 12296 | tf_op jit(solution)/shard_map/ppermute | solution.py:12
  189.5 5.9 %collective-permute-start.19 = (f32[16,1,64]{2,1,0:T(1,128)S(1)}, f32[16,1,64]{2,1,0:T(1,128)S(1)}, u32[]{:S(2)}, u32[]{:S(2)}) collective-permute-start(f32[16,1,64]{2,1,0:T(1,128)S(1)} %get-tuple-element.57), channel_id=1, source_target_pairs={{2,0},{3,1},{4,2},{5,3},{6,4},{7,5},{8,6},{9,7},{10,8},{11,9},{12,... | collective-permute-start | bytes 12296 | tf_op jit(solution)/shard_map/ppermute | solution.py:12
  195.5 8.5 %collective-permute-start.20 = (f32[1,34,64]{2,1,0:T(8,128)S(1)}, f32[1,34,64]{2,1,0:T(8,128)S(1)}, u32[]{:S(2)}, u32[]{:S(2)}) collective-permute-start(f32[1,34,64]{2,1,0:T(8,128)S(1)} %get-tuple-element.50), channel_id=1, source_target_pairs={{0,16},{16,32},{32,48},{48,64},{64,80},{80,96},{96,112},{112,128},... | collective-permute-start | bytes 26120 | tf_op jit(solution)/shard_map/ppermute | solution.py:20
  202.1 6.3 %collective-permute-start.21 = (f32[1,34,64]{2,1,0:T(8,128)S(1)}, f32[1,34,64]{2,1,0:T(8,128)S(1)}, u32[]{:S(2)}, u32[]{:S(2)}) collective-permute-start(f32[1,34,64]{2,1,0:T(8,128)S(1)} %get-tuple-element.51), channel_id=1, source_target_pairs={{16,0},{32,16},{48,32},{64,48},{80,64},{96,80},{112,96},{128,112},... | collective-permute-start | bytes 26120 | tf_op jit(solution)/shard_map/ppermute | solution.py:23
  228.3 18.7 %collective-permute-start.23 = (f32[8,1,32]{2,1,0:T(1,128)S(1)}, f32[8,1,32]{2,1,0:T(1,128)S(1)}, u32[]{:S(2)}, u32[]{:S(2)}) collective-permute-start(f32[8,1,32]{2,1,0:T(1,128)S(1)} %get-tuple-element.70), channel_id=1, source_target_pairs={{0,4},{1,5},{2,6},{3,7},{4,8},{5,9},{6,10},{7,11},{8,12},{9,13},{1... | collective-permute-start | bytes 3080 | tf_op jit(solution)/shard_map/ppermute | solution.py:12
  231.5 15.5 %collective-permute-start.24 = (f32[8,1,32]{2,1,0:T(1,128)S(1)}, f32[8,1,32]{2,1,0:T(1,128)S(1)}, u32[]{:S(2)}, u32[]{:S(2)}) collective-permute-start(f32[8,1,32]{2,1,0:T(1,128)S(1)} %get-tuple-element.71), channel_id=1, source_target_pairs={{4,0},{5,1},{6,2},{7,3},{8,4},{9,5},{10,6},{11,7},{12,8},{13,9},{1... | collective-permute-start | bytes 3080 | tf_op jit(solution)/shard_map/ppermute | solution.py:12
  247.0 7.4 %collective-permute-start.25 = (f32[1,34,32]{2,1,0:T(8,128)S(1)}, f32[1,34,32]{2,1,0:T(8,128)S(1)}, u32[]{:S(2)}, u32[]{:S(2)}) collective-permute-start(f32[1,34,32]{2,1,0:T(8,128)S(1)} %get-tuple-element.66), channel_id=1, source_target_pairs={{0,16},{16,32},{32,48},{48,64},{64,80},{80,96},{96,112},{112,128},... | collective-permute-start | bytes 13064 | tf_op jit(solution)/shard_map/ppermute | solution.py:20
  250.4 6.6 %collective-permute-start.26 = (f32[1,34,32]{2,1,0:T(8,128)S(1)}, f32[1,34,32]{2,1,0:T(8,128)S(1)}, u32[]{:S(2)}, u32[]{:S(2)}) collective-permute-start(f32[1,34,32]{2,1,0:T(8,128)S(1)} %get-tuple-element.67), channel_id=1, source_target_pairs={{16,0},{32,16},{48,32},{64,48},{80,64},{96,80},{112,96},{128,112},... | collective-permute-start | bytes 13064 | tf_op jit(solution)/shard_map/ppermute | solution.py:23
  257.7 5.4 %collective-permute-start.28 = (f32[8,1,32]{2,1,0:T(1,128)S(1)}, f32[8,1,32]{2,1,0:T(1,128)S(1)}, u32[]{:S(2)}, u32[]{:S(2)}) collective-permute-start(f32[8,1,32]{2,1,0:T(1,128)S(1)} %get-tuple-element.68), channel_id=1, source_target_pairs={{0,4},{1,5},{2,6},{3,7},{4,8},{5,9},{6,10},{7,11},{8,12},{9,13},{1... | collective-permute-start | bytes 3080 | tf_op jit(solution)/shard_map/ppermute | solution.py:12
  266.1 9.5 %collective-permute-start.30 = (f32[1,34,32]{2,1,0:T(8,128)S(1)}, f32[1,34,32]{2,1,0:T(8,128)S(1)}, u32[]{:S(2)}, u32[]{:S(2)}) collective-permute-start(f32[1,34,32]{2,1,0:T(8,128)S(1)} %get-tuple-element.62), channel_id=1, source_target_pairs={{0,16},{16,32},{32,48},{48,64},{64,80},{80,96},{96,112},{112,128},... | collective-permute-start | bytes 13064 | tf_op jit(solution)/shard_map/ppermute | solution.py:20
  273.5 6.3 %collective-permute-start.31 = (f32[1,34,32]{2,1,0:T(8,128)S(1)}, f32[1,34,32]{2,1,0:T(8,128)S(1)}, u32[]{:S(2)}, u32[]{:S(2)}) collective-permute-start(f32[1,34,32]{2,1,0:T(8,128)S(1)} %get-tuple-element.63), channel_id=1, source_target_pairs={{16,0},{32,16},{48,32},{64,48},{80,64},{96,80},{112,96},{128,112},... | collective-permute-start | bytes 13064 | tf_op jit(solution)/shard_map/ppermute | solution.py:23
  287.7 5.8 %collective-permute-start.34 = (f32[4,1,16]{2,1,0:T(1,128)S(1)}, f32[4,1,16]{2,1,0:T(1,128)S(1)}, u32[]{:S(2)}, u32[]{:S(2)}) collective-permute-start(f32[4,1,16]{2,1,0:T(1,128)S(1)} %get-tuple-element.83), channel_id=1, source_target_pairs={{8,0},{9,1},{10,2},{11,3},{12,4},{13,5},{14,6},{15,7},{24,16},{25,... | collective-permute-start | bytes 776 | tf_op jit(solution)/shard_map/ppermute | solution.py:12
  289.0 11.4 %collective-permute-start.37 = (f32[4,16,16]{2,1,0:T(8,128)S(1)}, f32[4,16,16]{2,1,0:T(8,128)S(1)}, u32[]{:S(2)}, u32[]{:S(2)}) collective-permute-start(f32[4,16,16]{2,1,0:T(8,128)S(1)} %broadcast_multiply_fusion.7), channel_id=1, source_target_pairs={{0,4},{4,0},{1,5},{5,1},{2,6},{6,2},{3,7},{7,3},{8,12},{12,8},{9,1... | collective-permute-start | bytes 12296 | tf_op jit(solution)/shard_map/ppermute | solution.py:35
  293.7 6.8 %collective-permute-start.35 = (f32[1,34,16]{1,2,0:T(8,128)S(1)}, f32[1,34,16]{1,2,0:T(8,128)S(1)}, u32[]{:S(2)}, u32[]{:S(2)}) collective-permute-start(f32[1,34,16]{1,2,0:T(8,128)S(1)} %get-tuple-element.78), channel_id=1, source_target_pairs={{0,16},{16,32},{32,48},{48,64},{64,80},{80,96},{96,112},{112,128},... | collective-permute-start | bytes 6536 | tf_op jit(solution)/shard_map/ppermute | solution.py:20
  298.2 6.4 %collective-permute-start.36 = (f32[1,34,16]{1,2,0:T(8,128)S(1)}, f32[1,34,16]{1,2,0:T(8,128)S(1)}, u32[]{:S(2)}, u32[]{:S(2)}) collective-permute-start(f32[1,34,16]{1,2,0:T(8,128)S(1)} %get-tuple-element.79), channel_id=1, source_target_pairs={{16,0},{32,16},{48,32},{64,48},{80,64},{96,80},{112,96},{128,112},... | collective-permute-start | bytes 6536 | tf_op jit(solution)/shard_map/ppermute | solution.py:23
  307.3 5.8 %collective-permute-start.39 = (f32[4,1,16]{2,1,0:T(1,128)S(1)}, f32[4,1,16]{2,1,0:T(1,128)S(1)}, u32[]{:S(2)}, u32[]{:S(2)}) collective-permute-start(f32[4,1,16]{2,1,0:T(1,128)S(1)} %get-tuple-element.81), channel_id=1, source_target_pairs={{8,0},{9,1},{10,2},{11,3},{12,4},{13,5},{14,6},{15,7},{24,16},{25,... | collective-permute-start | bytes 776 | tf_op jit(solution)/shard_map/ppermute | solution.py:12
  313.3 5.4 %collective-permute-start.40 = (f32[1,34,16]{1,2,0:T(8,128)S(1)}, f32[1,34,16]{1,2,0:T(8,128)S(1)}, u32[]{:S(2)}, u32[]{:S(2)}) collective-permute-start(f32[1,34,16]{1,2,0:T(8,128)S(1)} %get-tuple-element.74), channel_id=1, source_target_pairs={{0,16},{16,32},{32,48},{48,64},{64,80},{80,96},{96,112},{112,128},... | collective-permute-start | bytes 6536 | tf_op jit(solution)/shard_map/ppermute | solution.py:20
  316.7 6.2 %collective-permute-start.41 = (f32[1,34,16]{1,2,0:T(8,128)S(1)}, f32[1,34,16]{1,2,0:T(8,128)S(1)}, u32[]{:S(2)}, u32[]{:S(2)}) collective-permute-start(f32[1,34,16]{1,2,0:T(8,128)S(1)} %get-tuple-element.75), channel_id=1, source_target_pairs={{16,0},{32,16},{48,32},{64,48},{80,64},{96,80},{112,96},{128,112},... | collective-permute-start | bytes 6536 | tf_op jit(solution)/shard_map/ppermute | solution.py:23
  318.7 19.8 %collective-permute-start.45 = (f32[2,16,8]{1,2,0:T(8,128)S(1)}, f32[2,16,8]{1,2,0:T(8,128)S(1)}, u32[]{:S(2)}, u32[]{:S(2)}) collective-permute-start(f32[2,16,8]{1,2,0:T(8,128)S(1)} %broadcast_multiply_fusion.10), channel_id=1, source_target_pairs={{0,8},{8,0},{1,9},{9,1},{2,10},{10,2},{3,11},{11,3},{4,12},{12,4},... | collective-permute-start | bytes 3080 | tf_op jit(solution)/shard_map/ppermute | solution.py:35
  329.1 5.7 %collective-permute-start.43 = (f32[1,34,8]{1,2,0:T(8,128)S(1)}, f32[1,34,8]{1,2,0:T(8,128)S(1)}, u32[]{:S(2)}, u32[]{:S(2)}) collective-permute-start(f32[1,34,8]{1,2,0:T(8,128)S(1)} %get-tuple-element.107), channel_id=1, source_target_pairs={{0,16},{16,32},{32,48},{48,64},{64,80},{80,96},{96,112},{112,128},... | collective-permute-start | bytes 3272 | tf_op jit(solution)/shard_map/ppermute | solution.py:20
  332.2 6.1 %collective-permute-start.44 = (f32[1,34,8]{1,2,0:T(8,128)S(1)}, f32[1,34,8]{1,2,0:T(8,128)S(1)}, u32[]{:S(2)}, u32[]{:S(2)}) collective-permute-start(f32[1,34,8]{1,2,0:T(8,128)S(1)} %get-tuple-element.108), channel_id=1, source_target_pairs={{16,0},{32,16},{48,32},{64,48},{80,64},{96,80},{112,96},{128,112},... | collective-permute-start | bytes 3272 | tf_op jit(solution)/shard_map/ppermute | solution.py:23
  340.6 6.1 %collective-permute-start.47 = (f32[1,34,8]{1,2,0:T(8,128)S(1)}, f32[1,34,8]{1,2,0:T(8,128)S(1)}, u32[]{:S(2)}, u32[]{:S(2)}) collective-permute-start(f32[1,34,8]{1,2,0:T(8,128)S(1)} %get-tuple-element.106), channel_id=1, source_target_pairs={{16,0},{32,16},{48,32},{64,48},{80,64},{96,80},{112,96},{128,112},... | collective-permute-start | bytes 3272 | tf_op jit(solution)/shard_map/ppermute | solution.py:23
  (20 other events, 116.2 us)
where the time goes:
time: 350 us; the launch traced here: 348 us
  starting transfers between devices  122 us (35%)
  local copies, waits for them, and re-layouts  100 us (29%)
  waiting for transfers between devices  76.5 us (22%)
  other arithmetic  47.8 us (14%)
    reshape x5, local copies, waits for them, and re-layouts, restrict(): values.reshape(size_a // 2, 2, size_b // 2, 2, size_c // 2, 2)  81.2 us
    ppermute x11, starting transfers between devices, extended(): lax.ppermute(lax.slice_in_dim(block, block.shape[dim] - width, None, axis...  46.5 us
    ppermute x18, starting transfers between devices, passed_along(): return lax.ppermute(block, axis, route)  45.1 us
    ppermute x11, waiting for transfers between devices, extended(): lax.ppermute(lax.slice_in_dim(block, 0, width, axis=dim), axis, backward)  41.4 us
    reduce_sum x8, other arithmetic, restrict(): values.reshape(size_a // 2, 2, size_b // 2, 2, size_c // 2, 2)  33.2 us
    ppermute x18, waiting for transfers between devices, passed_along(): return lax.ppermute(block, axis, route)  25.6 us
    ppermute x11, starting transfers between devices, extended(): lax.ppermute(lax.slice_in_dim(block, 0, width, axis=dim), axis, backward)  21.8 us
    select_n x4, local copies, waits for them, and re-layouts, merge_pairs(): jnp.where(upper_half, jnp.concatenate([theirs_reaction, coarse_reaction],...  11.6 us
  transfers between devices with their start and end apart: 48, of which 24 were waited for; matrix products, arithmetic and copies ran while one was open for 20% of the time, Pallas kernels for 0%

commit v1 on v0

v1 whole, which is shorter than its diff:
```python
import functools

import jax
import jax.numpy as jnp
from jax import lax
from jax.experimental import pallas as pl
from jax.experimental.pallas import tpu as pltpu
from jax.sharding import PartitionSpec as P

F32 = jnp.float32
LANES = 128
FAR = 14


def coefficients(level_index):
    upper_edge = 1.1 * (2.0 + 0.02 * 4.0**level_index)
    lower_edge = upper_edge / 8.0
    midpoint = (upper_edge + lower_edge) / 2.0
    half_span = (upper_edge - lower_edge) / 2.0
    sigma_value = midpoint / half_span
    rho_first = 1.0 / sigma_value
    rho_second = 1.0 / (2.0 * sigma_value - rho_first)
    return (midpoint, rho_second * rho_first, 2.0 * rho_second / half_span)


def iota(shape, dim):
    return lax.broadcasted_iota(jnp.int32, shape, dim)


def edges(axis):
    here = lax.axis_index(axis)
    before = jnp.where(here > 0, 1.0, 0.0).astype(F32)
    after = jnp.where(here < lax.axis_size(axis) - 1, 1.0, 0.0).astype(F32)
    return before, after


def blur_xy(below, here, above):
    rows = here.shape[0]
    total = (below + here) + (here + above)
    part = total + pltpu.roll(total, 1, 0)
    return part + pltpu.roll(part, rows - 1, 0)


def blur_z_full(values):
    lane = iota(values.shape, 1)
    part = values + jnp.where(lane == 0, 0.0, pltpu.roll(values, 1, 1))
    return part + jnp.where(lane == LANES - 1, values, pltpu.roll(part, LANES - 1, 1))


def blur_z_part(values):
    part = values + pltpu.roll(values, 1, 1)
    return part + pltpu.roll(part, LANES - 1, 1)


def pair_rows(values):
    return values + pltpu.roll(values, values.shape[0] - 1, 0)


def pair_matrix(first, count):
    source = iota((LANES, LANES), 0)
    target = iota((LANES, LANES), 1)
    hit = ((source - first) >> 1 == target) & (source >= first) & (target < count)
    return jnp.where(hit, 0.5, 0.0).astype(F32)


def exact_dot(a, b):
    return jnp.dot(a, b, precision=lax.Precision.HIGHEST, preferred_element_type=F32)


def flag_rows(flags_ref, rows):
    boxes = flags_ref.shape[2]
    lane = iota((rows, LANES), 1)
    out = jnp.zeros((rows, LANES), F32)
    for i in range(boxes):
        out = jnp.where(lane // (LANES // boxes) == i, flags_ref[0, 0, i].astype(F32), out)
    return out


def pack_rows(flags_ref, guess_lo, guess_hi, source_lo, source_hi, reaction_lo, reaction_hi, up, down):
    shape = up.shape
    row = iota(shape, 1)
    flag = flag_rows(flags_ref, 8)[None]
    up[...] = jnp.where(
        row >= 5,
        guess_hi[...],
        jnp.where(
            row >= 3,
            pltpu.roll(source_hi[...], 5, 1),
            jnp.where(row >= 1, pltpu.roll(reaction_hi[...], 3, 1), flag),
        ),
    )
    down[...] = jnp.where(
        row < 3,
        guess_lo[...],
        jnp.where(
            row < 5,
            pltpu.roll(source_lo[...], 3, 1),
            jnp.where(row < 7, pltpu.roll(reaction_lo[...], 5, 1), flag),
        ),
    )


def halo_tiles(from_before, from_after, before, after):
    row = iota(from_before.shape, 1)
    first = row < 4
    guess = jnp.where(first, from_after * after, from_before * before)
    source = jnp.where(first, pltpu.roll(from_after, 5, 1), pltpu.roll(from_before, 3, 1))
    reaction = jnp.where(first, pltpu.roll(from_after, 3, 1), pltpu.roll(from_before, 5, 1))
    return guess, source, reaction


def mask_plane(flags_ref, from_before, from_after, before, after):
    tile = from_before[0].shape
    row = iota(tile, 0)
    lo = jnp.broadcast_to(from_before[0][0:1] * before, tile)
    hi = jnp.broadcast_to(from_after[0][7:8] * after, tile)
    return flag_rows(flags_ref, 32), jnp.where(row < 4, hi, lo)


def pack_planes(
    flags_ref, from_before, from_after, guess_lo, guess_hi, source_lo, source_hi, reaction_lo, reaction_hi, up, down
):
    before, after = edges("agg")
    own_mask, halo_mask = mask_plane(flags_ref, from_before, from_after, before, after)
    planes = from_before.shape[0]
    for target, first, fields, local in (
        (up, planes - 4, (guess_hi, source_hi, reaction_hi), (1, 2, 2)),
        (down, 0, (guess_lo, source_lo, reaction_lo), (0, 0, 0)),
    ):
        tiles = halo_tiles(from_before[first : first + 4], from_after[first : first + 4], before, after)
        at = 0
        for field, tile, start, count in zip(fields, tiles, local, (3, 2, 2)):
            for i in range(count):
                target[at, 0:32, :] = field[start + i]
                target[at, 32:40, :] = tile[start + i]
                at += 1
        target[at, 0:32, :] = own_mask
        target[at, 32:40, :] = halo_mask


def fine_kernel(
    flags_ref, from_before, from_after, x_before, x_after, guess, source, reaction,
    iterate, coarse, g, s, k, d, u, w, m, pairs, kpairs,
):
    before, after = edges("agg")
    xbefore, xafter = edges("box")
    own_mask, halo_mask = mask_plane(flags_ref, from_before, from_after, before, after)
    m[0] = x_before[7] * xbefore
    m[1, 0:32, :] = own_mask
    m[1, 32:40, :] = halo_mask
    m[2] = x_after[7] * xafter
    g[0:3] = x_before[0:3] * xbefore
    g[35:38] = x_after[0:3] * xafter
    s[1:3] = x_before[3:5]
    s[35:37] = x_after[3:5]
    shift = 8.0 / 7.0
    k[1:3] = x_before[5:7] + shift
    k[35:37] = x_after[5:7] + shift

    def assemble(i, carry):
        tiles = halo_tiles(from_before[pl.ds(i * 4, 4)], from_after[pl.ds(i * 4, 4)], before, after)
        at = pl.ds(3 + i * 4, 4)
        mine = pl.ds(i * 4, 4)
        g[at, 0:32, :] = guess[mine]
        g[at, 32:40, :] = tiles[0]
        s[at, 0:32, :] = source[mine]
        s[at, 32:40, :] = tiles[1]
        k[at, 0:32, :] = reaction[mine] + shift
        k[at, 32:40, :] = tiles[2] + shift
        return carry

    lax.fori_loop(0, 8, assemble, 0)
    theta, c1, c2 = coefficients(0)

    def remainder(field, x):
        region = jnp.where(x < 3, 0, jnp.where(x < 35, 1, 2))
        middle = field[x]
        q = blur_z_full(blur_xy(field[x - 1], middle, field[x + 1]))
        return m[region] * (s[x] - k[x] * middle + q * (1.0 / 56.0)), middle

    def first(x, carry):
        r, middle = remainder(g, x)
        step = r * (1.0 / theta)
        d[x] = step
        u[x] = middle + step
        return carry

    lax.fori_loop(1, 37, first, 0)

    def second(x, carry):
        r, middle = remainder(u, x)
        w[x] = middle + (c1 * d[x] + c2 * r)
        return carry

    lax.fori_loop(2, 36, second, 0)

    def third(i, carry):
        x = 3 + 2 * i
        r0, middle0 = remainder(w, x)
        r1, middle1 = remainder(w, x + 1)
        iterate[2 * i] = middle0[0:32]
        iterate[2 * i + 1] = middle1[0:32]
        pairs[i] = pair_rows(r0 + r1)
        kpairs[i] = pair_rows(reaction[2 * i] + reaction[2 * i + 1])
        return carry

    lax.fori_loop(0, 16, third, 0)
    rf = jnp.concatenate([pairs[i, pl.ds(0, 16, stride=2), :] for i in range(16)], axis=0)
    rk = jnp.concatenate([kpairs[i, pl.ds(0, 16, stride=2), :] for i in range(16)], axis=0)
    to_low = pair_matrix(0, 64)
    to_high = pltpu.roll(to_low, 64, 1)
    coarse[...] = (exact_dot(rf, to_low) + exact_dot(rk, to_high)).reshape(16, 16, LANES)


def level_constants(level):
    theta, c1, c2 = coefficients(level)
    return (1.0 + c1) / theta + c2, c2 / theta


def coarse_kernel(
    y_before, own, y_after, x_before, x_after, e1, e2, e3, f4, k4,
    f, k, e, m, pairs, kpairs, fb, kb, eb, mb, fc, kc, ec, mc,
):
    before, after = edges("agg")
    xbefore, xafter = edges("box")
    shift = 8.0 / 7.0

    def masks(ref, rows, lo, hi, lanes):
        shape = (rows, LANES)
        row = iota(shape, 0)
        inside = jnp.where(row < lo, before, jnp.where(row >= hi, after, 1.0))
        inside = jnp.where(iota(shape, 1) < lanes, inside, 0.0)
        ref[0] = inside * xbefore
        ref[1] = inside
        ref[2] = inside * xafter

    masks(m, 48, 16, 32, 64)
    masks(mb, 32, 8, 16, 32)
    masks(mc, 16, 4, 8, 16)

    def take(x, block, region):
        f[x] = block * m[region]
        k[x] = pltpu.roll(block, 64, 1)

    def take_before(i, carry):
        take(i, x_before[i], 0)
        take(30 + i, x_after[i], 2)
        return carry

    lax.fori_loop(0, FAR, take_before, 0)

    def take_own(i, carry):
        take(FAR + i, jnp.concatenate([y_before[i], own[i], y_after[i]], axis=0), 1)
        return carry

    lax.fori_loop(0, 16, take_own, 0)

    def correct(level, f, k, e, m, x, lo, hi):
        alpha, beta = level_constants(level)
        region = jnp.where(x < lo, 0, jnp.where(x < hi, 1, 2))
        middle = f[x]
        q = blur_z_part(blur_xy(f[x - 1], middle, f[x + 1]))
        kk = k[x] + shift
        e[x] = m[region] * (middle * (alpha - beta * kk) + q * (beta / 56.0))

    def remainder(f, k, e, x):
        middle = e[x]
        q = blur_z_part(blur_xy(e[x - 1], middle, e[x + 1]))
        return f[x] - (k[x] + shift) * middle + q * (1.0 / 56.0)

    def one(x, carry):
        correct(1, f, k, e, m, x, 14, 30)
        return carry

    lax.fori_loop(1, 43, one, 0)

    def two(i, carry):
        x = 2 + 2 * i
        pairs[i, 0:48, :] = pair_rows(remainder(f, k, e, x) + remainder(f, k, e, x + 1))
        kpairs[i, 0:48, :] = pair_rows(k[x] + k[x + 1])
        return carry

    lax.fori_loop(0, 20, two, 0)
    e1[...] = e[14:30, 16:32, 0:64]
    to_low = pair_matrix(0, 32)
    rf = jnp.concatenate([pairs[i, pl.ds(0, 24, stride=2), :] for i in range(20)], axis=0)
    rk = jnp.concatenate([kpairs[i, pl.ds(0, 24, stride=2), :] for i in range(20)], axis=0)
    rf = exact_dot(rf, to_low).reshape(20, 24, LANES)
    rk = exact_dot(rk, to_low).reshape(20, 24, LANES)
    for region, start, stop in ((0, 0, 6), (1, 6, 14), (2, 14, 20)):
        fb[start:stop, 0:24, :] = rf[start:stop] * mb[region, 0:24, :]
    kb[:, 0:24, :] = rk
    fb[:, 24:32, :] = jnp.zeros((20, 8, LANES), F32)
    kb[:, 24:32, :] = jnp.zeros((20, 8, LANES), F32)

    def three(x, carry):
        correct(2, fb, kb, eb, mb, x, 6, 14)
        return carry

    lax.fori_loop(1, 19, three, 0)
    e2[...] = eb[6:14, 8:16, 0:32]

    def four(i, carry):
        x = 2 + 2 * i
        pairs[i, 0:32, :] = pair_rows(remainder(fb, kb, eb, x) + remainder(fb, kb, eb, x + 1))
        kpairs[i, 0:32, :] = pair_rows(kb[x] + kb[x + 1])
        return carry

    lax.fori_loop(0, 8, four, 0)
    to_low = pair_matrix(0, 16)
    rf = jnp.concatenate([pairs[i, pl.ds(0, 16, stride=2), :] for i in range(8)], axis=0)
    rk = jnp.concatenate([kpairs[i, pl.ds(0, 16, stride=2), :] for i in range(8)], axis=0)
    rf = exact_dot(rf, to_low).reshape(8, 16, LANES)
    rk = exact_dot(rk, to_low).reshape(8, 16, LANES)
    for region, start, stop in ((0, 0, 2), (1, 2, 6), (2, 6, 8)):
        fc[start:stop] = rf[start:stop] * mc[region]
    kc[...] = rk
    for x in range(1, 7):
        correct(3, fc, kc, ec, mc, x, 2, 6)
    e3[...] = ec[2:6, 4:8, 0:16]
    for i in range(2):
        x = 2 + 2 * i
        pairs[i, 0:16, :] = pair_rows(remainder(fc, kc, ec, x) + remainder(fc, kc, ec, x + 1))
    for i in range(4):
        kpairs[i, 0:16, :] = pair_rows(kc[2 * i] + kc[2 * i + 1])
    to_low = pair_matrix(0, 8)
    rf = jnp.concatenate([pairs[i, pl.ds(0, 8, stride=2), :] for i in range(2)], axis=0)
    rk = jnp.concatenate([kpairs[i, pl.ds(0, 8, stride=2), :] for i in range(4)], axis=0)
    f4[...] = exact_dot(rf, to_low).reshape(2, 8, LANES)
    k4[...] = exact_dot(rk, to_low).reshape(4, 8, LANES)


def pack_last(y_before, own, y_after, out):
    before, after = edges("agg")
    row = iota(own.shape, 1)
    lo = pltpu.roll(y_before[...], 6, 1) * before
    hi = pltpu.roll(y_after[...], 2, 1) * after
    out[...] = jnp.where(row < 2, lo, jnp.where(row < 4, own[...], jnp.where(row < 6, hi, 0.0)))


def last_kernel(own, x_before, x_after, k4, e4, rest, f, e):
    before, after = edges("agg")
    xbefore, xafter = edges("box")
    shift = 8.0 / 7.0
    alpha, beta = level_constants(4)
    f[0:2] = x_before[...] * xbefore
    f[2:4] = own[...]
    f[4:6] = x_after[...] * xafter
    shape = (8, LANES)
    row = iota(shape, 0)
    inside = jnp.where(row < 2, before, jnp.where(row >= 4, after, 1.0))
    inside = jnp.where((iota(shape, 1) < 8) & (row < 6), inside, 0.0)
    for x in range(1, 5):
        middle = f[x]
        q = blur_z_part(blur_xy(f[x - 1], middle, f[x + 1]))
        value = inside * (middle * (alpha - beta * (k4[x - 1] + shift)) + q * (beta / 56.0))
        e[x] = value * xbefore if x == 1 else value * xafter if x == 4 else value
    for x in (2, 3):
        middle = e[x]
        q = blur_z_part(blur_xy(e[x - 1], middle, e[x + 1]))
        left = f[x] - (k4[x - 1] + shift) * middle + q * (1.0 / 56.0)
        e4[x - 2] = middle[2:4, 0:8]
        rest[x - 2] = left[2:4, 0:8]


def neighbours_of(up, down, axis):
    count = lax.axis_size(axis)
    ahead = [(i, (i + 1) % count) for i in range(count)]
    back = [(i, (i - 1) % count) for i in range(count)]
    return lax.ppermute(up, axis, ahead), lax.ppermute(down, axis, back)


def shaped(*dims):
    return jax.ShapeDtypeStruct(dims, F32)


def call(body, out_shape, scratch=(), in_specs=None, grid=None, out_specs=None, name=None):
    extra = {}
    if in_specs is not None:
        extra["in_specs"] = in_specs
    if grid is not None:
        extra["grid"] = grid
        extra["out_specs"] = out_specs
    return pl.pallas_call(
        body,
        out_shape=out_shape,
        scratch_shapes=[pltpu.VMEM(dims, F32) for dims in scratch],
        compiler_params=pltpu.CompilerParams(vmem_limit_bytes=40 * 1024 * 1024),
        name=name,
        **extra,
    )


def per_device(source, guess, reaction, flags):
    smem = pl.BlockSpec(memory_space=pltpu.SMEM)
    vmem = pl.BlockSpec(memory_space=pltpu.VMEM)
    rows_lo = pl.BlockSpec((32, 8, LANES), lambda i: (0, 0, 0))
    rows_hi = pl.BlockSpec((32, 8, LANES), lambda i: (0, 3, 0))
    whole = pl.BlockSpec((32, 8, LANES), lambda i: (0, 0, 0))
    up, down = call(
        pack_rows,
        (shaped(32, 8, LANES), shaped(32, 8, LANES)),
        in_specs=[smem, rows_lo, rows_hi, rows_lo, rows_hi, rows_lo, rows_hi],
        grid=(1,),
        out_specs=(whole, whole),
        name="pack_rows",
    )(flags, guess, guess, source, source, reaction, reaction)
    y_before, y_after = neighbours_of(up, down, "agg")
    planes_lo = pl.BlockSpec((4, 32, LANES), lambda i: (0, 0, 0))
    planes_hi = pl.BlockSpec((4, 32, LANES), lambda i: (7, 0, 0))
    strip = pl.BlockSpec((8, 40, LANES), lambda i: (0, 0, 0))
    up, down = call(
        pack_planes,
        (shaped(8, 40, LANES), shaped(8, 40, LANES)),
        in_specs=[smem, whole, whole, planes_lo, planes_hi, planes_lo, planes_hi, planes_lo, planes_hi],
        grid=(1,),
        out_specs=(strip, strip),
        name="pack_planes",
    )(flags, y_before, y_after, guess, guess, source, source, reaction, reaction)
    x_before, x_after = neighbours_of(up, down, "box")
    big = (38, 40, LANES)
    iterate, coarse = call(
        fine_kernel,
        (shaped(32, 32, LANES), shaped(16, 16, LANES)),
        scratch=[big] * 6 + [(3, 40, LANES), (16, 40, LANES), (16, 32, LANES)],
        in_specs=[smem] + [vmem] * 7,
        name="fine",
    )(flags, y_before, y_after, x_before, x_after, guess, source, reaction)
    y_before, y_after = neighbours_of(coarse, coarse, "agg")
    extended = jnp.concatenate([y_before, coarse, y_after], axis=1)
    x_before, x_after = neighbours_of(extended[16 - FAR :], extended[:FAR], "box")
    e1, e2, e3, f4, k4 = call(
        coarse_kernel,
        (shaped(16, 16, 64), shaped(8, 8, 32), shaped(4, 4, 16), shaped(2, 8, LANES), shaped(4, 8, LANES)),
        scratch=[(44, 48, LANES)] * 3 + [(3, 48, LANES), (20, 48, LANES), (20, 48, LANES)]
        + [(20, 32, LANES)] * 3 + [(3, 32, LANES)] + [(8, 16, LANES)] * 3 + [(3, 16, LANES)],
        name="coarse",
    )(y_before, coarse, y_after, x_before, x_after)
    y_before, y_after = neighbours_of(f4, f4, "agg")
    last = call(pack_last, shaped(2, 8, LANES), name="pack_last")(y_before, f4, y_after)
    x_before, x_after = neighbours_of(last, last, "box")
    e4, rest = call(
        last_kernel,
        (shaped(2, 2, 8), shaped(2, 2, 8)),
        scratch=[(6, 8, LANES), (6, 8, LANES)],
        name="last",
    )(last, x_before, x_after, k4)
    return iterate, e1, e2, e3, e4, rest


def solution(mesh):
    spec = P("box", "agg", None)
    return jax.shard_map(
        per_device, mesh=mesh, in_specs=(spec,) * 4, out_specs=(spec,) * 6, check_vma=False
    )
```

time: 350 us -> 90.1 us (0.26)
  local copies, waits for them, and re-layouts: 100 us -> 3.85 us
  starting transfers between devices: 122 us -> 26.2 us
  waiting for transfers between devices: 76.5 us -> 23.4 us
  other arithmetic: 47.8 us -> 0 us
  Pallas kernels: 0 us -> 35.4 us
    ppermute x48 -> x12, starting transfers between devices: 122 us -> 26.2 us  [neighbours_of(): return (lax.ppermute(up, axis, ahead), lax.ppermute(down, axis, back))]
    reshape x5 -> x0, local copies, waits for them, and re-layouts: 81.2 us -> none  [restrict(): values.reshape(size_a // 2, 2, size_b // 2, 2, size_c // 2, 2)]
    ppermute x48 -> x12, waiting for transfers between devices: 76.5 us -> 23.4 us  [neighbours_of(): return (lax.ppermute(up, axis, ahead), lax.ppermute(down, axis, back))]
    pallas_call x0 -> x6, Pallas kernels: none -> 35.4 us  [the longest x1 18.1 us: per_device(): call(coarse_kernel, (shaped(16, 16, 64), shaped(8, 8, 32), shaped(4, 4, 1...]
    reduce_sum x8 -> x0, other arithmetic: 33.2 us -> none  [restrict(): values.reshape(size_a // 2, 2, size_b // 2, 2, size_c // 2, 2)]
    select_n x4 -> x0, local copies, waits for them, and re-layouts: 11.6 us -> none  [merge_pairs(): jnp.where(upper_half, jnp.concatenate([theirs_reaction, coarse_reaction],...]
    concatenate x24 -> x0, other arithmetic: 5.01 us -> none  [the longest x22 4.86 us: extended(): block = jnp.concatenate([low, block, high], axis=dim)]
    add x7 -> x0, other arithmetic: 4.63 us -> none  [the longest x4 1.72 us: per_device(): correction = first_step + second_step]
  transfers between devices with their start and end apart: 48 -> 12, of which waited for: 24 -> 8; matrix products, arithmetic and copies ran while one was open for 20% -> 0% of each run, Pallas kernels for 0% -> 0%
where the time goes in v1:
time: 90.1 us; the launch traced here: 89.5 us
  Pallas kernels  35.4 us (39%)
  starting transfers between devices  26.2 us (29%)
  waiting for transfers between devices  23.4 us (26%)
  local copies, waits for them, and re-layouts  3.85 us (4%)
    ppermute x12, starting transfers between devices, neighbours_of(): return (lax.ppermute(up, axis, ahead), lax.ppermute(down, axis, back))  26.2 us
    ppermute x12, waiting for transfers between devices, neighbours_of(): return (lax.ppermute(up, axis, ahead), lax.ppermute(down, axis, back))  23.4 us
    pallas_call x1, Pallas kernels, per_device(): call(coarse_kernel, (shaped(16, 16, 64), shaped(8, 8, 32), shaped(4, 4, 1...  18.1 us
    pallas_call x1, Pallas kernels, per_device(): call(fine_kernel, (shaped(32, 32, LANES), shaped(16, 16, LANES)), scratch...  15.3 us
    unnamed x10, local copies, waits for them, and re-layouts  3.79 us
  transfers between devices with their start and end apart: 12, of which 8 were waited for; matrix products, arithmetic and copies ran while one was open for 0% of the time, Pallas kernels for 0%

profile of v1, /device:TPU:97, one launch (start us, length us, event | category | flops | bytes accessed | tf_op | source)
XLA Modules:
  0.0 89.5 jit_solution(7684511325878081645)
XLA Ops:
  0.6 1.0 %copy-done = f32[32,32,128]{2,1,0:T(8,128)S(1)} copy-done((f32[32,32,128]{2,1,0:T(8,128)S(1)}, f32[32,32,128]{2,1,0:T(8,128)}, u32[]{:S(2)}) %copy-start) | copy-done | bytes 524312
  1.7 1.0 %copy-done.1 = f32[32,32,128]{2,1,0:T(8,128)S(1)} copy-done((f32[32,32,128]{2,1,0:T(8,128)S(1)}, f32[32,32,128]{2,1,0:T(8,128)}, u32[]{:S(2)}) %copy-start.1) | copy-done | bytes 524312
  2.7 1.0 %copy-done.2 = f32[32,32,128]{2,1,0:T(8,128)S(1)} copy-done((f32[32,32,128]{2,1,0:T(8,128)S(1)}, f32[32,32,128]{2,1,0:T(8,128)}, u32[]{:S(2)}) %copy-start.2) | copy-done | bytes 524312
  3.8 0.7 copy-done.3
  4.4 0.6 pack_rows.1
  5.0 1.3 %collective-permute-start = (f32[32,8,128]{2,1,0:T(8,128)S(1)}, f32[32,8,128]{2,1,0:T(8,128)S(1)}, u32[]{:S(2)}, u32[]{:S(2)}) collective-permute-start(f32[32,8,128]{2,1,0:T(8,128)S(1)} %get-tuple-element.19), channel_id=1, source_target_pairs={{0,1},{1,2},{2,3},{3,4},{4,5},{5,6},{6,7},{7,8},{8,9},{9,10},{10,1... | collective-permute-start | bytes 393224 | tf_op jit(solution)/shard_map/ppermute | solution.py:370
  6.3 3.8 %collective-permute-start.1 = (f32[32,8,128]{2,1,0:T(8,128)S(1)}, f32[32,8,128]{2,1,0:T(8,128)S(1)}, u32[]{:S(2)}, u32[]{:S(2)}) collective-permute-start(f32[32,8,128]{2,1,0:T(8,128)S(1)} %get-tuple-element.20), channel_id=1, source_target_pairs={{0,15},{1,0},{2,1},{3,2},{4,3},{5,4},{6,5},{7,6},{8,7},{9,8},{10,9... | collective-permute-start | bytes 393224 | tf_op jit(solution)/shard_map/ppermute | solution.py:370
  10.1 3.0 %collective-permute-done.from_before = f32[32,8,128]{2,1,0:T(8,128)S(1)} collective-permute-done((f32[32,8,128]{2,1,0:T(8,128)S(1)}, f32[32,8,128]{2,1,0:T(8,128)S(1)}, u32[]{:S(2)}, u32[]{:S(2)}) %collective-permute-start) | collective-permute-done | bytes 131104 | tf_op jit(solution)/shard_map/ppermute | solution.py:370
  13.1 0.0 collective-permute-done.1.from_after
  13.1 0.6 pack_planes.1
  13.7 4.1 %collective-permute-start.2 = (f32[8,40,128]{2,1,0:T(8,128)S(1)}, f32[8,40,128]{2,1,0:T(8,128)S(1)}, u32[]{:S(2)}, u32[]{:S(2)}) collective-permute-start(f32[8,40,128]{2,1,0:T(8,128)S(1)} %get-tuple-element.21), channel_id=1, source_target_pairs={{0,16},{16,32},{32,48},{48,64},{64,80},{80,96},{96,112},{112,128},... | collective-permute-start | bytes 491528 | tf_op jit(solution)/shard_map/ppermute | solution.py:370
  17.8 0.0 collective-permute-start.3
  17.8 2.3 %collective-permute-done.2.x_before = f32[8,40,128]{2,1,0:T(8,128)S(1)} collective-permute-done((f32[8,40,128]{2,1,0:T(8,128)S(1)}, f32[8,40,128]{2,1,0:T(8,128)S(1)}, u32[]{:S(2)}, u32[]{:S(2)}) %collective-permute-start.2) | collective-permute-done | bytes 163872 | tf_op jit(solution)/shard_map/ppermute | solution.py:370
  20.1 3.7 %collective-permute-done.3.x_after = f32[8,40,128]{2,1,0:T(8,128)S(1)} collective-permute-done((f32[8,40,128]{2,1,0:T(8,128)S(1)}, f32[8,40,128]{2,1,0:T(8,128)S(1)}, u32[]{:S(2)}, u32[]{:S(2)}) %collective-permute-start.3) | collective-permute-done | bytes 163872 | tf_op jit(solution)/shard_map/ppermute | solution.py:370
  23.7 15.3 %fine.1 = (f32[32,32,128]{2,1,0:T(8,128)}, f32[16,16,128]{2,1,0:T(8,128)S(1)}) custom-call(s32[1,1,4]{2,1,0:T(1,128)S(1)} %copy-done.3, f32[32,8,128]{2,1,0:T(8,128)S(1)} %collective-permute-done.from_before, f32[32,8,128]{2,1,0:T(8,128)S(1)} %collective-permute-done.1.from_after, f32[8,40,128]{2,1,0:T(8,128)S(1)} %collective-permute-done.2.x_before, ...), custom_call_target="tpu_custom_call" | custom-call | tf_op jit(solution)/shard_map/fine/pallas_call | solution.py:422
  39.1 0.0 collective-permute-start.4
  39.1 4.9 %collective-permute-start.5 = (f32[16,16,128]{2,1,0:T(8,128)S(1)}, f32[16,16,128]{2,1,0:T(8,128)S(1)}, u32[]{:S(2)}, u32[]{:S(2)}) collective-permute-start(f32[16,16,128]{2,1,0:T(8,128)S(1)} %get-tuple-element.24.own), channel_id=1, source_target_pairs={{0,15},{1,0},{2,1},{3,2},{4,3},{5,4},{6,5},{7,6},{8,7},{9,8},{10,9... | collective-permute-start | bytes 393224 | tf_op jit(solution)/shard_map/ppermute | solution.py:370
  43.9 2.4 %collective-permute-done.4.y_before = f32[16,16,128]{2,1,0:T(8,128)S(1)} collective-permute-done((f32[16,16,128]{2,1,0:T(8,128)S(1)}, f32[16,16,128]{2,1,0:T(8,128)S(1)}, u32[]{:S(2)}, u32[]{:S(2)}) %collective-permute-start.4) | collective-permute-done | bytes 131104 | tf_op jit(solution)/shard_map/ppermute | solution.py:370
  46.3 0.0 collective-permute-done.5.y_after
  46.4 0.0 collective-permute-start.7
  46.4 2.9 %collective-permute-start.6 = (f32[14,48,128]{2,1,0:T(8,128)S(1)}, f32[14,48,128]{2,1,0:T(8,128)S(1)}, u32[]{:S(2)}, u32[]{:S(2)}) collective-permute-start(f32[14,48,128]{2,1,0:T(8,128)S(1)} %get-tuple-element.33), channel_id=1, source_target_pairs={{0,16},{16,32},{32,48},{48,64},{64,80},{80,96},{96,112},{112,128},... | collective-permute-start | bytes 1032200 | tf_op jit(solution)/shard_map/ppermute | solution.py:370
  49.4 4.9 %collective-permute-done.7.x_after = f32[14,48,128]{2,1,0:T(8,128)S(1)} collective-permute-done((f32[14,48,128]{2,1,0:T(8,128)S(1)}, f32[14,48,128]{2,1,0:T(8,128)S(1)}, u32[]{:S(2)}, u32[]{:S(2)}) %collective-permute-start.7) | collective-permute-done | bytes 344096 | tf_op jit(solution)/shard_map/ppermute | solution.py:370
  54.3 0.0 collective-permute-done.6.x_before
  54.3 18.1 %coarse.1 = (f32[16,16,64]{2,1,0:T(8,128)}, f32[8,8,32]{2,1,0:T(8,128)}, f32[4,4,16]{2,1,0:T(4,128)}, f32[2,8,128]{2,1,0:T(8,128)S(1)}, f32[4,8,128]{2,1,0:T(8,128)S(1)}) custom-call(f32[16,16,128]{2,1,0:T(8,128)S(1)} %collective-permute-done.4.y_before, f32[16,16,128]{2,1,0:T(8,128)S(1)} %get-tuple-element.24.own, ...), custom_call_target="tpu_custom_call" | custom-call | tf_op jit(solution)/shard_map/coarse/pallas_call | solution.py:432
  72.4 4.7 %collective-permute-start.9 = (f32[2,8,128]{2,1,0:T(8,128)S(1)}, f32[2,8,128]{2,1,0:T(8,128)S(1)}, u32[]{:S(2)}, u32[]{:S(2)}) collective-permute-start(f32[2,8,128]{2,1,0:T(8,128)S(1)} %get-tuple-element.28.own), channel_id=1, source_target_pairs={{0,15},{1,0},{2,1},{3,2},{4,3},{5,4},{6,5},{7,6},{8,7},{9,8},{10,9... | collective-permute-start | bytes 24584 | tf_op jit(solution)/shard_map/ppermute | solution.py:370
  77.1 0.0 collective-permute-start.8
  77.1 0.8 collective-permute-done.9.y_after
  77.9 5.0 %collective-permute-done.8.y_before = f32[2,8,128]{2,1,0:T(8,128)S(1)} collective-permute-done((f32[2,8,128]{2,1,0:T(8,128)S(1)}, f32[2,8,128]{2,1,0:T(8,128)S(1)}, u32[]{:S(2)}, u32[]{:S(2)}) %collective-permute-start.8) | collective-permute-done | bytes 8224 | tf_op jit(solution)/shard_map/ppermute | solution.py:370
  82.9 0.0 collective-permute-start.11
  82.9 4.4 %collective-permute-start.10 = (f32[2,8,128]{2,1,0:T(8,128)S(1)}, f32[2,8,128]{2,1,0:T(8,128)S(1)}, u32[]{:S(2)}, u32[]{:S(2)}) collective-permute-start(f32[2,8,128]{2,1,0:T(8,128)S(1)} %pack_last.1.own), channel_id=1, source_target_pairs={{0,16},{16,32},{32,48},{48,64},{64,80},{80,96},{96,112},{112,128},... | collective-permute-start | bytes 24584 | tf_op jit(solution)/shard_map/ppermute | solution.py:370
  87.3 1.3 %collective-permute-done.11.x_after = f32[2,8,128]{2,1,0:T(8,128)S(1)} collective-permute-done((f32[2,8,128]{2,1,0:T(8,128)S(1)}, f32[2,8,128]{2,1,0:T(8,128)S(1)}, u32[]{:S(2)}, u32[]{:S(2)}) %collective-permute-start.11) | collective-permute-done | bytes 8224 | tf_op jit(solution)/shard_map/ppermute | solution.py:370
  88.7 0.9 last.1
  (10 shorter events, 0.1 us)
Async XLA Ops:
  0.6 1.0 %copy-start = (f32[32,32,128]{2,1,0:T(8,128)S(1)}, f32[32,32,128]{2,1,0:T(8,128)}, u32[]{:S(2)}) copy-start(f32[32,32,128]{2,1,0:T(8,128)} %guess.1) | copy-start | bytes 1572868
  1.7 1.0 %copy-start.1 = (f32[32,32,128]{2,1,0:T(8,128)S(1)}, f32[32,32,128]{2,1,0:T(8,128)}, u32[]{:S(2)}) copy-start(f32[32,32,128]{2,1,0:T(8,128)} %source.1) | copy-start | bytes 1572868
  2.7 1.0 %copy-start.2 = (f32[32,32,128]{2,1,0:T(8,128)S(1)}, f32[32,32,128]{2,1,0:T(8,128)}, u32[]{:S(2)}) copy-start(f32[32,32,128]{2,1,0:T(8,128)} %reaction.1) | copy-start | bytes 1572868
  3.8 0.7 copy-start.3
  5.0 8.1 %collective-permute-start = (f32[32,8,128]{2,1,0:T(8,128)S(1)}, f32[32,8,128]{2,1,0:T(8,128)S(1)}, u32[]{:S(2)}, u32[]{:S(2)}) collective-permute-start(f32[32,8,128]{2,1,0:T(8,128)S(1)} %get-tuple-element.19), channel_id=1, source_target_pairs={{0,1},{1,2},{2,3},{3,4},{4,5},{5,6},{6,7},{7,8},{8,9},{9,10},{10,1... | collective-permute-start | bytes 393224 | tf_op jit(solution)/shard_map/ppermute | solution.py:370
  6.3 6.8 %collective-permute-start.1 = (f32[32,8,128]{2,1,0:T(8,128)S(1)}, f32[32,8,128]{2,1,0:T(8,128)S(1)}, u32[]{:S(2)}, u32[]{:S(2)}) collective-permute-start(f32[32,8,128]{2,1,0:T(8,128)S(1)} %get-tuple-element.20), channel_id=1, source_target_pairs={{0,15},{1,0},{2,1},{3,2},{4,3},{5,4},{6,5},{7,6},{8,7},{9,8},{10,9... | collective-permute-start | bytes 393224 | tf_op jit(solution)/shard_map/ppermute | solution.py:370
  13.7 6.4 %collective-permute-start.2 = (f32[8,40,128]{2,1,0:T(8,128)S(1)}, f32[8,40,128]{2,1,0:T(8,128)S(1)}, u32[]{:S(2)}, u32[]{:S(2)}) collective-permute-start(f32[8,40,128]{2,1,0:T(8,128)S(1)} %get-tuple-element.21), channel_id=1, source_target_pairs={{0,16},{16,32},{32,48},{48,64},{64,80},{80,96},{96,112},{112,128},... | collective-permute-start | bytes 491528 | tf_op jit(solution)/shard_map/ppermute | solution.py:370
  17.8 6.0 %collective-permute-start.3 = (f32[8,40,128]{2,1,0:T(8,128)S(1)}, f32[8,40,128]{2,1,0:T(8,128)S(1)}, u32[]{:S(2)}, u32[]{:S(2)}) collective-permute-start(f32[8,40,128]{2,1,0:T(8,128)S(1)} %get-tuple-element.22), channel_id=1, source_target_pairs={{0,240},{16,0},{32,16},{48,32},{64,48},{80,64},{96,80},{112,96},{1... | collective-permute-start | bytes 491528 | tf_op jit(solution)/shard_map/ppermute | solution.py:370
  39.1 7.2 %collective-permute-start.4 = (f32[16,16,128]{2,1,0:T(8,128)S(1)}, f32[16,16,128]{2,1,0:T(8,128)S(1)}, u32[]{:S(2)}, u32[]{:S(2)}) collective-permute-start(f32[16,16,128]{2,1,0:T(8,128)S(1)} %get-tuple-element.24.own), channel_id=1, source_target_pairs={{0,1},{1,2},{2,3},{3,4},{4,5},{5,6},{6,7},{7,8},{8,9},{9,10},{10,1... | collective-permute-start | bytes 393224 | tf_op jit(solution)/shard_map/ppermute | solution.py:370
  39.1 7.3 %collective-permute-start.5 = (f32[16,16,128]{2,1,0:T(8,128)S(1)}, f32[16,16,128]{2,1,0:T(8,128)S(1)}, u32[]{:S(2)}, u32[]{:S(2)}) collective-permute-start(f32[16,16,128]{2,1,0:T(8,128)S(1)} %get-tuple-element.24.own), channel_id=1, source_target_pairs={{0,15},{1,0},{2,1},{3,2},{4,3},{5,4},{6,5},{7,6},{8,7},{9,8},{10,9... | collective-permute-start | bytes 393224 | tf_op jit(solution)/shard_map/ppermute | solution.py:370
  46.4 7.9 %collective-permute-start.7 = (f32[14,48,128]{2,1,0:T(8,128)S(1)}, f32[14,48,128]{2,1,0:T(8,128)S(1)}, u32[]{:S(2)}, u32[]{:S(2)}) collective-permute-start(f32[14,48,128]{2,1,0:T(8,128)S(1)} %get-tuple-element.32), channel_id=1, source_target_pairs={{0,240},{16,0},{32,16},{48,32},{64,48},{80,64},{96,80},{112,96},{1... | collective-permute-start | bytes 1032200 | tf_op jit(solution)/shard_map/ppermute | solution.py:370
  46.4 7.9 %collective-permute-start.6 = (f32[14,48,128]{2,1,0:T(8,128)S(1)}, f32[14,48,128]{2,1,0:T(8,128)S(1)}, u32[]{:S(2)}, u32[]{:S(2)}) collective-permute-start(f32[14,48,128]{2,1,0:T(8,128)S(1)} %get-tuple-element.33), channel_id=1, source_target_pairs={{0,16},{16,32},{32,48},{48,64},{64,80},{80,96},{96,112},{112,128},... | collective-permute-start | bytes 1032200 | tf_op jit(solution)/shard_map/ppermute | solution.py:370
  72.4 5.5 %collective-permute-start.9 = (f32[2,8,128]{2,1,0:T(8,128)S(1)}, f32[2,8,128]{2,1,0:T(8,128)S(1)}, u32[]{:S(2)}, u32[]{:S(2)}) collective-permute-start(f32[2,8,128]{2,1,0:T(8,128)S(1)} %get-tuple-element.28.own), channel_id=1, source_target_pairs={{0,15},{1,0},{2,1},{3,2},{4,3},{5,4},{6,5},{7,6},{8,7},{9,8},{10,9... | collective-permute-start | bytes 24584 | tf_op jit(solution)/shard_map/ppermute | solution.py:370
  77.1 5.8 %collective-permute-start.8 = (f32[2,8,128]{2,1,0:T(8,128)S(1)}, f32[2,8,128]{2,1,0:T(8,128)S(1)}, u32[]{:S(2)}, u32[]{:S(2)}) collective-permute-start(f32[2,8,128]{2,1,0:T(8,128)S(1)} %get-tuple-element.28.own), channel_id=1, source_target_pairs={{0,1},{1,2},{2,3},{3,4},{4,5},{5,6},{6,7},{7,8},{8,9},{9,10},{10,1... | collective-permute-start | bytes 24584 | tf_op jit(solution)/shard_map/ppermute | solution.py:370
  82.9 5.7 %collective-permute-start.11 = (f32[2,8,128]{2,1,0:T(8,128)S(1)}, f32[2,8,128]{2,1,0:T(8,128)S(1)}, u32[]{:S(2)}, u32[]{:S(2)}) collective-permute-start(f32[2,8,128]{2,1,0:T(8,128)S(1)} %pack_last.1.own), channel_id=1, source_target_pairs={{0,240},{16,0},{32,16},{48,32},{64,48},{80,64},{96,80},{112,96},{1... | collective-permute-start | bytes 24584 | tf_op jit(solution)/shard_map/ppermute | solution.py:370
  82.9 5.7 %collective-permute-start.10 = (f32[2,8,128]{2,1,0:T(8,128)S(1)}, f32[2,8,128]{2,1,0:T(8,128)S(1)}, u32[]{:S(2)}, u32[]{:S(2)}) collective-permute-start(f32[2,8,128]{2,1,0:T(8,128)S(1)} %pack_last.1.own), channel_id=1, source_target_pairs={{0,16},{16,32},{32,48},{48,64},{64,80},{80,96},{96,112},{112,128},... | collective-permute-start | bytes 24584 | tf_op jit(solution)/shard_map/ppermute | solution.py:370

commit v2 on v0

v2 whole, which is shorter than its diff:
```python
import functools

import jax
import jax.numpy as jnp
from jax import lax
from jax.experimental import pallas as pl
from jax.experimental.pallas import tpu as pltpu
from jax.sharding import PartitionSpec as P

F32 = jnp.float32
LANES = 128
FAR = 14


def coefficients(level_index):
    upper_edge = 1.1 * (2.0 + 0.02 * 4.0**level_index)
    lower_edge = upper_edge / 8.0
    midpoint = (upper_edge + lower_edge) / 2.0
    half_span = (upper_edge - lower_edge) / 2.0
    sigma_value = midpoint / half_span
    rho_first = 1.0 / sigma_value
    rho_second = 1.0 / (2.0 * sigma_value - rho_first)
    return (midpoint, rho_second * rho_first, 2.0 * rho_second / half_span)


def iota(shape, dim):
    return lax.broadcasted_iota(jnp.int32, shape, dim)


def edges(axis):
    here = lax.axis_index(axis)
    before = jnp.where(here > 0, 1.0, 0.0).astype(F32)
    after = jnp.where(here < lax.axis_size(axis) - 1, 1.0, 0.0).astype(F32)
    return before, after


def blurred(planes, blur_z):
    sums = [a + b for a, b in zip(planes[:-1], planes[1:])]
    out = []
    for low, high in zip(sums[:-1], sums[1:]):
        total = low + high
        part = total + pltpu.roll(total, 1, 0)
        out.append(blur_z(part + pltpu.roll(part, part.shape[0] - 1, 0)))
    return out


def blur_z_full(values):
    lane = iota(values.shape, 1)
    part = values + jnp.where(lane == 0, 0.0, pltpu.roll(values, 1, 1))
    return part + jnp.where(lane == LANES - 1, values, pltpu.roll(part, LANES - 1, 1))


def blur_z_halves(values):
    lane = iota(values.shape, 1) & 63
    part = values + jnp.where(lane == 0, 0.0, pltpu.roll(values, 1, 1))
    return part + jnp.where(lane == 63, values, pltpu.roll(part, LANES - 1, 1))


def blur_z_part(values):
    part = values + pltpu.roll(values, 1, 1)
    return part + pltpu.roll(part, LANES - 1, 1)


def pair_rows(values):
    return values + pltpu.roll(values, values.shape[0] - 1, 0)


def pair_matrix():
    source = iota((LANES, LANES), 0)
    target = iota((LANES, LANES), 1)
    return jnp.where(source >> 1 == target, 0.5, 0.0).astype(F32)


def pair_matrix_halves():
    source = iota((LANES, LANES), 0)
    target = iota((LANES, LANES), 1)
    hit = ((source & 64) == (target & 64)) & ((source & 63) >> 1 == (target & 63))
    return jnp.where(hit, 0.5, 0.0).astype(F32)


def exact_dot(a, b):
    return jnp.dot(a, b, precision=lax.Precision.HIGHEST, preferred_element_type=F32)


def loop(first, stop, size, body):
    count = (stop - first) // size

    def step(i, carry):
        body(first + i * size)
        return carry

    lax.fori_loop(0, count, step, 0)


def copy_all(sems, *pairs):
    copies = [pltpu.make_async_copy(a, b, sems.at[i]) for i, (a, b) in enumerate(pairs)]
    for copy in copies:
        copy.start()
    return copies


def pack_rows(
    flags, guess, source, reaction, up, down, strip_up, strip_down,
    flag_smem, guess_lo, guess_hi, source_lo, source_hi, reaction_lo, reaction_hi, sems,
):
    lo, hi = pl.ds(0, 8), pl.ds(24, 8)
    copies = copy_all(
        sems,
        (flags, flag_smem),
        (guess.at[:, lo, :], guess_lo),
        (guess.at[:, hi, :], guess_hi),
        (source.at[:, lo, :], source_lo),
        (source.at[:, hi, :], source_hi),
        (reaction.at[:, lo, :], reaction_lo),
        (reaction.at[:, hi, :], reaction_hi),
        (guess.at[29:32], strip_up.at[0:3]),
        (source.at[30:32], strip_up.at[3:5]),
        (reaction.at[30:32], strip_up.at[5:7]),
        (guess.at[0:3], strip_down.at[0:3]),
        (source.at[0:2], strip_down.at[3:5]),
        (reaction.at[0:2], strip_down.at[5:7]),
    )
    for copy in copies[:7]:
        copy.wait()
    boxes = flags.shape[2]
    lane = iota((8, LANES), 1)
    flag = jnp.zeros((8, LANES), F32)
    for i in range(boxes):
        flag = jnp.where(lane // (LANES // boxes) == i, flag_smem[0, 0, i].astype(F32), flag)
    flag = flag[None]
    row = iota(up.shape, 1)
    up[...] = jnp.where(
        row >= 5,
        guess_hi[...],
        jnp.where(
            row >= 3,
            pltpu.roll(source_hi[...], 5, 1),
            jnp.where(row >= 1, pltpu.roll(reaction_hi[...], 3, 1), flag),
        ),
    )
    down[...] = jnp.where(
        row < 3,
        guess_lo[...],
        jnp.where(
            row < 5,
            pltpu.roll(source_lo[...], 3, 1),
            jnp.where(row < 7, pltpu.roll(reaction_lo[...], 5, 1), flag),
        ),
    )
    for copy in copies[7:]:
        copy.wait()


def halo_tiles(from_before, from_after, before, after):
    row = iota(from_before.shape, 1)
    first = row < 4
    guess = jnp.where(first, from_after * after, from_before * before)
    source = jnp.where(first, pltpu.roll(from_after, 5, 1), pltpu.roll(from_before, 3, 1))
    reaction = jnp.where(first, pltpu.roll(from_after, 3, 1), pltpu.roll(from_before, 5, 1))
    return guess, source, reaction


def pack_planes(own, from_before, from_after, strip_up, strip_down, up, down):
    before, after = edges("agg")
    tile = (8, LANES)
    own_mask = jnp.broadcast_to(own[0, 0:1, :], (32, LANES))
    lo_mask = jnp.broadcast_to(from_before[0, 0:1, :] * before, tile)
    hi_mask = jnp.broadcast_to(from_after[0, 7:8, :] * after, tile)
    halo_mask = jnp.where(iota(tile, 0) < 4, hi_mask, lo_mask)
    planes = from_before.shape[0]
    for target, strip, first, local in (
        (up, strip_up, planes - 4, (1, 2, 2)),
        (down, strip_down, 0, (0, 0, 0)),
    ):
        tiles = halo_tiles(from_before[first : first + 4], from_after[first : first + 4], before, after)
        target[0:7, 0:32, :] = strip[...]
        at = 0
        for tile, start, count in zip(tiles, local, (3, 2, 2)):
            target[at : at + count, 32:40, :] = tile[start : start + count]
            at += count
        target[7, 0:32, :] = own_mask
        target[7, 32:40, :] = halo_mask


SHIFT = 8.0 / 7.0


def compact(values, ref, rows):
    return jnp.concatenate([ref[i, pl.ds(0, rows, stride=2), :] for i in values], axis=0)


def fine_inner(
    packed, from_before, from_after, guess, source, reaction,
    g, s, k, d, u, w, coarse, pairs, kpairs, sems,
):
    rows = pl.ds(0, 32)
    copies = copy_all(
        sems, (guess, g.at[:, rows, :]), (source, s.at[:, rows, :]), (reaction, k.at[:, rows, :])
    )
    before, after = edges("agg")
    theta, c1, c2 = coefficients(0)

    def assemble(x):
        at = pl.ds(x, 8)
        tiles = halo_tiles(from_before[at], from_after[at], before, after)
        g[at, 32:40, :] = tiles[0]
        s[at, 32:40, :] = tiles[1]
        k[at, 32:40, :] = tiles[2]

    loop(0, 32, 8, assemble)
    for copy in copies:
        copy.wait()

    def remainders(field, x, size):
        planes = [field[x + i] for i in range(-1, size + 1)]
        mask = packed[7]
        out = []
        for i, q in enumerate(blurred(planes, blur_z_full)):
            r = mask * (s[x + i] - (k[x + i] + SHIFT) * planes[i + 1] + q * (1.0 / 56.0))
            out.append((r, planes[i + 1]))
        return out

    def first(x):
        out = remainders(g, x, 3)
        for i, (r, middle) in enumerate(out):
            step = r * (1.0 / theta)
            d[x + i] = step
            u[x + i] = middle + step

    loop(1, 31, 3, first)

    def second(x):
        out = [m + (c1 * d[x + i] + c2 * r) for i, (r, m) in enumerate(remainders(u, x, 4))]
        for i, value in enumerate(out):
            w[x + i] = value

    loop(2, 30, 4, second)

    def third(x):
        out = [r for r, _ in remainders(w, x, 4)]
        at = (x - 4) // 2
        pairs[at] = pair_rows(out[0] + out[1])
        pairs[at + 1] = pair_rows(out[2] + out[3])

    loop(4, 28, 4, third)

    def fourth(i):
        out = [pair_rows(k[2 * i + 2 * j, 0:32, :] + k[2 * i + 2 * j + 1, 0:32, :]) for j in range(4)]
        for j, value in enumerate(out):
            kpairs[i + j] = value

    loop(0, 16, 4, fourth)
    to_low = pair_matrix()
    rk = exact_dot(compact(range(16), kpairs, 16), pltpu.roll(to_low, 64, 1)).reshape(16, 16, LANES)
    rf = exact_dot(compact(range(12), pairs, 16), to_low).reshape(12, 16, LANES)
    coarse[0:2] = rk[0:2]
    coarse[2:14] = rk[2:14] + rf
    coarse[14:16] = rk[14:16]


def fine_outer(packed, x_before, x_after, g, s, k, d, u, w, inner, coarse, edge, pairs):
    xbefore, xafter = edges("box")
    theta, c1, c2 = coefficients(0)
    new_d, new_u, new_w = {}, {}, {}

    def side(x, before, after, own):
        return before(x + 3) if x < 0 else after(x - 32) if x > 31 else own(x)

    def guess_at(x):
        return side(x, lambda i: x_before[i] * xbefore, lambda i: x_after[i] * xafter, lambda i: g[i])

    def source_at(x):
        return side(x, lambda i: x_before[i + 2], lambda i: x_after[i + 3], lambda i: s[i])

    def reaction_at(x):
        return side(x, lambda i: x_before[i + 4], lambda i: x_after[i + 5], lambda i: k[i])

    def mask_at(x):
        return side(x, lambda i: x_before[7] * xbefore, lambda i: x_after[7] * xafter, lambda i: packed[7])

    def remainders(field, first, size):
        planes = [field(x) for x in range(first - 1, first + size + 1)]
        out = []
        for i, q in enumerate(blurred(planes, blur_z_full)):
            x = first + i
            r = mask_at(x) * (source_at(x) - (reaction_at(x) + SHIFT) * planes[i + 1] + q * (1.0 / 56.0))
            out.append((x, r, planes[i + 1]))
        return out

    for first in (-2, 31):
        for x, r, middle in remainders(guess_at, first, 3):
            new_d[x] = r * (1.0 / theta)
            new_u[x] = middle + new_d[x]
    for first in (-1, 30):
        for x, r, middle in remainders(lambda i: new_u[i] if i in new_u else u[i], first, 3):
            step = new_d[x] if x in new_d else d[x]
            new_w[x] = middle + (c1 * step + c2 * r)
    for at, x in enumerate((0, 1, 30, 31)):
        edge[at] = new_w[x][0:32]
    for at, first in enumerate((0, 28)):
        out = [r for _, r, _ in remainders(lambda i: new_w[i] if i in new_w else w[i], first, 4)]
        pairs[2 * at] = pair_rows(out[0] + out[1])
        pairs[2 * at + 1] = pair_rows(out[2] + out[3])
    rf = exact_dot(compact(range(4), pairs, 16), pair_matrix()).reshape(4, 16, LANES)
    coarse[0:2] = inner[0:2] + rf[0:2]
    coarse[2:14] = inner[2:14]
    coarse[14:16] = inner[14:16] + rf[2:4]


def level_constants(level):
    theta, c1, c2 = coefficients(level)
    return (1.0 + c1) / theta + c2, c2 / theta


def low_half(shape):
    return iota(shape, len(shape) - 1) < 64


def masks_of(rows, lo, hi, lanes):
    before, after = edges("agg")
    xbefore, xafter = edges("box")
    shape = (rows, LANES)
    row = iota(shape, 0)
    inside = jnp.where(row < lo, before, jnp.where(row >= hi, after, 1.0))
    inside = jnp.where((iota(shape, 1) & 63) < lanes, inside, 0.0)
    return inside * jnp.where(low_half(shape), xbefore, xafter), inside


def corrections(level, planes, reactions, masks, blur_z):
    alpha, beta = level_constants(level)
    return [
        m * (f * (alpha - beta * (k + SHIFT)) + q * (beta / 56.0))
        for f, k, m, q in zip(planes[1:-1], reactions, masks, blurred(planes, blur_z))
    ]


def coarse_remainders(planes, fields, reactions, blur_z):
    return [
        f - (k + SHIFT) * e + q * (1.0 / 56.0)
        for f, k, e, q in zip(fields, reactions, planes[1:-1], blurred(planes, blur_z))
    ]


def swap(values):
    return pltpu.roll(values, 64, 1)


def coarse_inner(y_before, own, y_after, f, k, e, f2, k2, pairs, kpairs):
    _, inside = masks_of(48, 16, 32, 64)
    low = low_half((48, LANES))
    for j in range(8):
        lo = jnp.concatenate([y_before[j], own[j], y_after[j]], axis=0)
        hi = jnp.concatenate([y_before[15 - j], own[15 - j], y_after[15 - j]], axis=0)
        f[j] = jnp.where(low, lo, swap(hi)) * inside
        k[j] = jnp.where(low, swap(lo), hi)
    fields = [f[j] for j in range(8)]
    reactions = [k[j] for j in range(8)]
    value = corrections(1, fields + [swap(fields[7])], reactions[1:], [inside] * 7, blur_z_halves)
    for j in range(7):
        e[j + 1] = value[j]
    rest = coarse_remainders(value + [swap(value[6])], fields[2:], reactions[2:], blur_z_halves)
    for j in range(3):
        pairs[j] = pair_rows(rest[2 * j] + rest[2 * j + 1])
        kpairs[j] = pair_rows(reactions[2 * j + 2] + reactions[2 * j + 3])
    halve = pair_matrix_halves()
    _, inside = masks_of(24, 8, 16, 32)
    rf = exact_dot(compact(range(3), pairs, 24), halve).reshape(3, 24, LANES)
    for j in range(3):
        f2[j] = rf[j] * inside
    k2[...] = exact_dot(compact(range(3), kpairs, 24), halve).reshape(3, 24, LANES)


def coarse_outer(
    x_before, x_after, f_in, k_in, e_in, f2_in, k2_in, e1, e2, e3, f4, k4,
    f, k, e, pairs, kpairs,
):
    outside, inside = masks_of(48, 16, 32, 64)
    low = low_half((48, LANES))

    def take(j):
        out = []
        for i in range(2):
            lo, hi = x_before[j + i], x_after[13 - j - i]
            out.append((jnp.where(low, lo, swap(hi)) * outside, jnp.where(low, swap(lo), hi)))
        for i in range(2):
            f[j + i], k[j + i] = out[i]

    loop(0, 14, 2, take)
    for j in (0, 1):
        f[14 + j] = f_in[j]
        k[14 + j] = k_in[j]

    def one(j):
        out = corrections(
            1,
            [f[j + i] for i in range(-1, 4)],
            [k[j + i] for i in range(3)],
            [outside] * 3,
            blur_z_halves,
        )
        for i in range(3):
            e[j + i] = out[i]

    loop(1, 13, 3, one)
    value = corrections(1, [f[j] for j in range(12, 16)], [k[13], k[14]], [outside, inside], blur_z_halves)
    e[13], e[14] = value
    e[15] = e_in[1]
    e[16] = e_in[2]

    def two(j):
        out = coarse_remainders(
            [e[j + i] for i in range(-1, 3)],
            [f[j + i] for i in range(2)],
            [k[j + i] for i in range(2)],
            blur_z_halves,
        )
        p = (j - 2) // 2
        pairs[p] = pair_rows(out[0] + out[1])
        kpairs[p] = pair_rows(k[j] + k[j + 1])

    loop(2, 16, 2, two)
    half = slice(16, 32)
    e1[0] = e[14, half, 0:64]
    e1[15] = swap(e[14, half, :])[:, 0:64]
    for j in range(1, 8):
        value = e_in[j, half, :]
        e1[j] = value[:, 0:64]
        e1[15 - j] = swap(value)[:, 0:64]
    halve = pair_matrix_halves()
    rf = exact_dot(compact(range(7), pairs, 24), halve).reshape(7, 24, LANES)
    rk = exact_dot(compact(range(7), kpairs, 24), halve).reshape(7, 24, LANES)
    outside, inside = masks_of(24, 8, 16, 32)
    fields = [rf[j] * (outside if j < 6 else inside) for j in range(7)] + [f2_in[j] for j in range(3)]
    reactions = [rk[j] for j in range(7)] + [k2_in[j] for j in range(3)]
    value = corrections(
        2, fields + [swap(fields[9])], reactions[1:], [outside] * 5 + [inside] * 4, blur_z_part
    )
    for j in range(4):
        own = value[5 + j][8:16]
        e2[j] = own[:, 0:32]
        e2[7 - j] = swap(own)[:, 0:32]
    rest = coarse_remainders(value + [swap(value[8])], fields[2:], reactions[2:], blur_z_part)
    for p in range(4):
        pairs[p, 0:24, :] = pair_rows(rest[2 * p] + rest[2 * p + 1])
        kpairs[p, 0:24, :] = pair_rows(reactions[2 * p + 2] + reactions[2 * p + 3])
    rf = exact_dot(compact(range(4), pairs, 16), halve).reshape(4, 16, LANES)
    rk = exact_dot(compact(range(4), kpairs, 16), halve).reshape(4, 16, LANES)
    outside, inside = masks_of(16, 4, 8, 16)
    fields = [rf[0] * outside, rf[1] * outside, rf[2] * inside, rf[3] * inside]
    reactions = [rk[j] for j in range(4)]
    value = corrections(3, fields + [swap(fields[3])], reactions[1:], [outside, inside, inside], blur_z_part)
    for j in range(2):
        own = value[1 + j][0:8]
        e3[j] = own[4:8, 0:16]
        e3[3 - j] = swap(own)[4:8, 0:16]
    rest = coarse_remainders(value + [swap(value[2])], fields[2:], reactions[2:], blur_z_part)
    pairs[0, 0:16, :] = pair_rows(rest[0] + rest[1])
    for p in range(2):
        kpairs[p, 0:16, :] = pair_rows(reactions[2 * p] + reactions[2 * p + 1])
    f4[...] = exact_dot(compact(range(1), pairs, 8), halve)
    k4[...] = exact_dot(compact(range(2), kpairs, 8), halve).reshape(2, 8, LANES)


def pack_last(y_before, own, y_after, out):
    before, after = edges("agg")
    row = iota(own.shape, 0)
    lo = pltpu.roll(y_before[...], 6, 0) * before
    hi = pltpu.roll(y_after[...], 2, 0) * after
    out[...] = jnp.where(row < 2, lo, jnp.where(row < 4, own[...], jnp.where(row < 6, hi, 0.0)))


def last_kernel(own, x_before, x_after, k4, e4, rest):
    outside, inside = masks_of(8, 2, 4, 8)
    low = low_half(own.shape)
    inside = jnp.where(iota(own.shape, 0) < 6, inside, 0.0)
    outside = jnp.where(iota(own.shape, 0) < 6, outside, 0.0)
    middle = own[...] * inside
    fields = [
        jnp.where(low, x_before[...], x_after[...]) * outside,
        swap(jnp.where(low, x_after[...], x_before[...])) * outside,
        middle,
        swap(middle),
    ]
    value = corrections(4, fields, [k4[0], k4[1]], [outside, inside], blur_z_part)
    left = coarse_remainders(value + [swap(value[1])], [middle], [k4[1]], blur_z_part)[0]
    for out, here in ((e4, value[1]), (rest, left)):
        out[0] = here[2:4, 0:8]
        out[1] = swap(here)[2:4, 0:8]


def neighbours_of(up, down, axis):
    count = lax.axis_size(axis)
    ahead = [(i, (i + 1) % count) for i in range(count)]
    back = [(i, (i - 1) % count) for i in range(count)]
    return lax.ppermute(up, axis, ahead), lax.ppermute(down, axis, back)


VMEM = pl.BlockSpec(memory_space=pltpu.VMEM)
HBM = pl.BlockSpec(memory_space=pltpu.HBM)


def call(body, outs, ins, scratch=(), copies=0, flops=0, name=None):
    sems = [pltpu.SemaphoreType.DMA((copies,))] if copies else []
    return pl.pallas_call(
        body,
        out_shape=[jax.ShapeDtypeStruct(dims, F32) for dims in outs],
        in_specs=ins,
        out_specs=[VMEM] * len(outs),
        scratch_shapes=[s if not isinstance(s, tuple) else pltpu.VMEM(s, F32) for s in scratch] + sems,
        compiler_params=pltpu.CompilerParams(vmem_limit_bytes=40 * 1024 * 1024),
        cost_estimate=pl.CostEstimate(flops=flops, transcendentals=0, bytes_accessed=flops),
        name=name,
    )


def per_device(source, guess, reaction, flags):
    tile = (32, 8, LANES)
    own, down, strip_up, strip_down = call(
        pack_rows,
        [tile, tile, (7, 32, LANES), (7, 32, LANES)],
        [HBM] * 4,
        scratch=[pltpu.SMEM((1, 1, flags.shape[2]), jnp.int32)] + [tile] * 6,
        copies=13,
        name="pack_rows",
    )(flags, guess, source, reaction)
    y_before, y_after = neighbours_of(own, down, "agg")
    packed, down = call(
        pack_planes, [(8, 40, LANES)] * 2, [VMEM] * 5, name="pack_planes"
    )(own, y_before, y_after, strip_up, strip_down)
    x_before, x_after = neighbours_of(packed, down, "box")
    big = (32, 40, LANES)
    *fields, inner = call(
        fine_inner,
        [big] * 6 + [(16, 16, LANES)],
        [VMEM] * 3 + [HBM] * 3,
        scratch=[(12, 40, LANES), (16, 32, LANES)],
        copies=3,
        flops=8000000,
        name="fine_inner",
    )(packed, y_before, y_after, guess, source, reaction)
    coarse, edge = call(
        fine_outer,
        [(16, 16, LANES), (4, 32, LANES)],
        [VMEM] * 10,
        scratch=[(4, 40, LANES)],
        name="fine_outer",
    )(packed, x_before, x_after, *fields, inner)
    iterate = jnp.concatenate([edge[0:2], fields[5][2:30, 0:32], edge[2:4]], axis=0)
    y_before, y_after = neighbours_of(coarse, coarse, "agg")
    extended = jnp.concatenate([y_before, coarse, y_after], axis=1)
    x_before, x_after = neighbours_of(extended[16 - FAR :], extended[:FAR], "box")
    plane = (48, LANES)
    inner = call(
        coarse_inner,
        [(8,) + plane] * 3 + [(3, 24, LANES)] * 2,
        [VMEM] * 3,
        scratch=[(3,) + plane] * 2,
        flops=4000000,
        name="coarse_inner",
    )(y_before, coarse, y_after)
    e1, e2, e3, f4, k4 = call(
        coarse_outer,
        [(16, 16, 64), (8, 8, 32), (4, 4, 16), (8, LANES), (2, 8, LANES)],
        [VMEM] * 7,
        scratch=[(16,) + plane] * 2 + [(17,) + plane] + [(7,) + plane] * 2,
        name="coarse_outer",
    )(x_before, x_after, *inner)
    y_before, y_after = neighbours_of(f4, f4, "agg")
    (last,) = call(pack_last, [(8, LANES)], [VMEM] * 3, name="pack_last")(y_before, f4, y_after)
    x_before, x_after = neighbours_of(last, last, "box")
    e4, rest = call(
        last_kernel, [(2, 2, 8), (2, 2, 8)], [VMEM] * 4, name="last"
    )(last, x_before, x_after, k4)
    return iterate, e1, e2, e3, e4, rest


def solution(mesh):
    spec = P("box", "agg", None)
    return jax.shard_map(
        per_device, mesh=mesh, in_specs=(spec,) * 4, out_specs=(spec,) * 6, check_vma=False
    )
```

time: 350 us -> 59.6 us (0.17)
  starting transfers between devices: 122 us -> 23 us
  local copies, waits for them, and re-layouts: 100 us -> 3.92 us
  waiting for transfers between devices: 76.5 us -> 17.9 us
  other arithmetic: 47.8 us -> 0.83 us
  Pallas kernels: 0 us -> 12.8 us
    ppermute x48 -> x12, starting transfers between devices: 122 us -> 23 us  [neighbours_of(): return (lax.ppermute(up, axis, ahead), lax.ppermute(down, axis, back))]
    reshape x5 -> x0, local copies, waits for them, and re-layouts: 81.2 us -> none  [restrict(): values.reshape(size_a // 2, 2, size_b // 2, 2, size_c // 2, 2)]
    ppermute x48 -> x12, waiting for transfers between devices: 76.5 us -> 17.9 us  [neighbours_of(): return (lax.ppermute(up, axis, ahead), lax.ppermute(down, axis, back))]
    reduce_sum x8 -> x0, other arithmetic: 33.2 us -> none  [restrict(): values.reshape(size_a // 2, 2, size_b // 2, 2, size_c // 2, 2)]
    pallas_call x0 -> x8, Pallas kernels: none -> 12.8 us  [the longest x1 4.83 us: per_device(): call(coarse_outer, [(16, 16, 64), (8, 8, 32), (4, 4, 16), (8, LANES), (2,...]
    select_n x4 -> x0, local copies, waits for them, and re-layouts: 11.6 us -> none  [merge_pairs(): jnp.where(upper_half, jnp.concatenate([theirs_reaction, coarse_reaction],...]
    add x7 -> x0, other arithmetic: 4.63 us -> none  [the longest x4 1.72 us: per_device(): correction = first_step + second_step]
    concatenate x24 -> x1, other arithmetic: 5.01 us -> 0.83 us  [per_device(): jnp.concatenate([edge[0:2], fields[5][2:30, 0:32], edge[2:4]], axis=0)]
  transfers between devices with their start and end apart: 48 -> 12, of which waited for: 24 -> 7; matrix products, arithmetic and copies ran while one was open for 20% -> 2% of each run, Pallas kernels for 0% -> 9%
where the time goes in v2:
time: 59.6 us; the launch traced here: 59.3 us
  starting transfers between devices  23 us (39%)
  waiting for transfers between devices  17.9 us (30%)
  Pallas kernels  12.8 us (21%)
  local copies, waits for them, and re-layouts  3.92 us (7%)
  other arithmetic  0.83 us (1%)
  between operations  0.78 us (1%)
    ppermute x12, starting transfers between devices, neighbours_of(): return (lax.ppermute(up, axis, ahead), lax.ppermute(down, axis, back))  23 us
    ppermute x12, waiting for transfers between devices, neighbours_of(): return (lax.ppermute(up, axis, ahead), lax.ppermute(down, axis, back))  17.9 us
    pallas_call x1, Pallas kernels, per_device(): call(coarse_outer, [(16, 16, 64), (8, 8, 32), (4, 4, 16), (8, LANES), (2,...  4.83 us
    pallas_call x1, Pallas kernels, per_device(): call(fine_inner, [big] * 6 + [(16, 16, LANES)], [VMEM] * 3 + [HBM] * 3, s...  4.66 us
    unnamed x16, local copies, waits for them, and re-layouts  3.81 us
  transfers between devices with their start and end apart: 12, of which 7 were waited for; matrix products, arithmetic and copies ran while one was open for 2% of the time, Pallas kernels for 9%

profile of v2, /device:TPU:97, one launch (start us, length us, event | category | flops | bytes accessed | tf_op | source)
XLA Modules:
  0.0 59.3 jit_solution(12702504612299715063)
XLA Ops:
  0.6 0.0 copy-start
  0.6 1.0 %copy-done = f32[32,32,128]{2,1,0:T(8,128)S(1)} copy-done((f32[32,32,128]{2,1,0:T(8,128)S(1)}, f32[32,32,128]{2,1,0:T(8,128)}, u32[]{:S(2)}) %copy-start) | copy-done | bytes 524312
  1.7 1.0 %copy-done.2 = f32[32,32,128]{2,1,0:T(8,128)S(1)} copy-done((f32[32,32,128]{2,1,0:T(8,128)S(1)}, f32[32,32,128]{2,1,0:T(8,128)}, u32[]{:S(2)}) %copy-start.2) | copy-done | bytes 524312
  2.7 1.0 %copy-done.4 = f32[32,32,128]{2,1,0:T(8,128)S(1)} copy-done((f32[32,32,128]{2,1,0:T(8,128)S(1)}, f32[32,32,128]{2,1,0:T(8,128)}, u32[]{:S(2)}) %copy-start.4) | copy-done | bytes 524312
  3.8 0.7 %copy-done.6 = s32[1,1,4]{2,1,0:T(1,128)S(1)} copy-done((s32[1,1,4]{2,1,0:T(1,128)S(1)}, s32[1,1,4]{2,1,0:T(1,128)}, u32[]{:S(2)}) %copy-start.6) | copy-done | bytes 40
  4.4 0.7 %pack_rows.1 = (f32[32,8,128]{2,1,0:T(8,128)S(1)}, f32[32,8,128]{2,1,0:T(8,128)S(1)}, f32[7,32,128]{2,1,0:T(8,128)S(1)}, f32[7,32,128]{2,1,0:T(8,128)S(1)}) custom-call(s32[1,1,4]{2,1,0:T(1,128)S(1)} %copy-done.6, f32[32,32,128]{2,1,0:T(8,128)S(1)} %copy-done, f32[32,32,128]{2,1,0:T(8,128)S(1)} %copy-done.2, f32[32,32,128]{2,1,0:T(8,128)S(1)} %copy-done.4), custom_call_target="tpu_custom_call" | custom-call | tf_op jit(solution)/shard_map/pack_rows/pallas_call | solution.py:518
  5.2 0.0 copy-start.1
  5.2 1.3 %collective-permute-start = (f32[32,8,128]{2,1,0:T(8,128)S(1)}, f32[32,8,128]{2,1,0:T(8,128)S(1)}, u32[]{:S(2)}, u32[]{:S(2)}) collective-permute-start(f32[32,8,128]{2,1,0:T(8,128)S(1)} %get-tuple-element.33.own), channel_id=1, source_target_pairs={{0,1},{1,2},{2,3},{3,4},{4,5},{5,6},{6,7},{7,8},{8,9},{9,10},{10,1... | collective-permute-start | bytes 393224 | tf_op jit(solution)/shard_map/ppermute | solution.py:495
  6.5 3.8 %collective-permute-start.1 = (f32[32,8,128]{2,1,0:T(8,128)S(1)}, f32[32,8,128]{2,1,0:T(8,128)S(1)}, u32[]{:S(2)}, u32[]{:S(2)}) collective-permute-start(f32[32,8,128]{2,1,0:T(8,128)S(1)} %get-tuple-element.34), channel_id=1, source_target_pairs={{0,15},{1,0},{2,1},{3,2},{4,3},{5,4},{6,5},{7,6},{8,7},{9,8},{10,9... | collective-permute-start | bytes 393224 | tf_op jit(solution)/shard_map/ppermute | solution.py:495
  10.3 3.0 %collective-permute-done.from_before = f32[32,8,128]{2,1,0:T(8,128)S(1)} collective-permute-done((f32[32,8,128]{2,1,0:T(8,128)S(1)}, f32[32,8,128]{2,1,0:T(8,128)S(1)}, u32[]{:S(2)}, u32[]{:S(2)}) %collective-permute-start) | collective-permute-done | bytes 131104 | tf_op jit(solution)/shard_map/ppermute | solution.py:495
  13.3 4.1 %collective-permute-start.2 = (f32[8,40,128]{2,1,0:T(8,128)S(1)}, f32[8,40,128]{2,1,0:T(8,128)S(1)}, u32[]{:S(2)}, u32[]{:S(2)}) collective-permute-start(f32[8,40,128]{2,1,0:T(8,128)S(1)} %get-tuple-element.37.packed), channel_id=1, source_target_pairs={{0,16},{16,32},{32,48},{48,64},{64,80},{80,96},{96,112},{112,128},... | collective-permute-start | bytes 491528 | tf_op jit(solution)/shard_map/ppermute | solution.py:495
  17.4 0.0 collective-permute-start.3
  17.4 4.7 %fine_inner.1 = (f32[32,40,128]{2,1,0:T(8,128)S(1)}, f32[32,40,128]{2,1,0:T(8,128)S(1)}, f32[32,40,128]{2,1,0:T(8,128)S(1)}, f32[32,40,128]{2,1,0:T(8,128)S(1)},...) custom-call(f32[8,40,128]{2,1,0:T(8,128)S(1)} %get-tuple-element.37.packed, ...), custom_call_target="tpu_custom_call" | custom-call | flops 8000000 | bytes 8000000 | tf_op jit(solution)/shard_map/fine_inner/pallas_call | solution.py:532
  22.1 0.0 collective-permute-done.2.x_before
  22.1 1.3 %collective-permute-done.3.x_after = f32[8,40,128]{2,1,0:T(8,128)S(1)} collective-permute-done((f32[8,40,128]{2,1,0:T(8,128)S(1)}, f32[8,40,128]{2,1,0:T(8,128)S(1)}, u32[]{:S(2)}, u32[]{:S(2)}) %collective-permute-start.3) | collective-permute-done | bytes 163872 | tf_op jit(solution)/shard_map/ppermute | solution.py:495
  23.4 0.7 %fine_outer.1 = (f32[16,16,128]{2,1,0:T(8,128)S(1)}, f32[4,32,128]{2,1,0:T(8,128)S(1)}) custom-call(f32[8,40,128]{2,1,0:T(8,128)S(1)} %get-tuple-element.37.packed, f32[8,40,128]{2,1,0:T(8,128)S(1)} %collective-permute-done.2.x_before, f32[8,40,128]{2,1,0:T(8,128)S(1)} %collective-permute-done.3.x_after, f32[32,40,128]{2,1,0:T(8,128)S(1)} %get-tuple-element.39.g, ...), custom_call_target="tpu_custom_call" | custom-call | tf_op jit(solution)/shard_map/fine_outer/pallas_call | solution.py:541
  24.1 0.1 collective-permute-start.4
  24.2 4.9 %collective-permute-start.5 = (f32[16,16,128]{2,1,0:T(8,128)S(1)}, f32[16,16,128]{2,1,0:T(8,128)S(1)}, u32[]{:S(2)}, u32[]{:S(2)}) collective-permute-start(f32[16,16,128]{2,1,0:T(8,128)S(1)} %get-tuple-element.47.own), channel_id=1, source_target_pairs={{0,15},{1,0},{2,1},{3,2},{4,3},{5,4},{6,5},{7,6},{8,7},{9,8},{10,9... | collective-permute-start | bytes 393224 | tf_op jit(solution)/shard_map/ppermute | solution.py:495
  29.1 2.3 %collective-permute-done.4.y_before = f32[16,16,128]{2,1,0:T(8,128)S(1)} collective-permute-done((f32[16,16,128]{2,1,0:T(8,128)S(1)}, f32[16,16,128]{2,1,0:T(8,128)S(1)}, u32[]{:S(2)}, u32[]{:S(2)}) %collective-permute-start.4) | collective-permute-done | bytes 131104 | tf_op jit(solution)/shard_map/ppermute | solution.py:495
  31.4 0.0 collective-permute-done.5.y_after
  31.5 2.8 %collective-permute-start.6 = (f32[14,48,128]{2,1,0:T(8,128)S(1)}, f32[14,48,128]{2,1,0:T(8,128)S(1)}, u32[]{:S(2)}, u32[]{:S(2)}) collective-permute-start(f32[14,48,128]{2,1,0:T(8,128)S(1)} %get-tuple-element.61), channel_id=1, source_target_pairs={{0,16},{16,32},{32,48},{48,64},{64,80},{80,96},{96,112},{112,128},... | collective-permute-start | bytes 1032200 | tf_op jit(solution)/shard_map/ppermute | solution.py:495
  34.3 0.8 %coarse_inner.1 = (f32[8,48,128]{2,1,0:T(8,128)S(1)}, f32[8,48,128]{2,1,0:T(8,128)S(1)}, f32[8,48,128]{2,1,0:T(8,128)S(1)}, f32[3,24,128]{2,1,0:T(8,128)S(1)}, f32[3,24,128]{2,1,0:T(8,128)S(1)}) custom-call(f32[16,16,128]{2,1,0:T(8,128)S(1)} %collective-permute-done.4.y_before, f32[16,16,128]{2,1,0:T(8,128)S(1)} %get-tuple-element.47.own, ...), custom_call_target="tpu_custom_call" | custom-call | flops 4000000 | bytes 4000000 | tf_op jit(solution)/shard_map/coarse_inner/pallas_call | solution.py:553
  35.1 3.3 %collective-permute-done.6.x_before = f32[14,48,128]{2,1,0:T(8,128)S(1)} collective-permute-done((f32[14,48,128]{2,1,0:T(8,128)S(1)}, f32[14,48,128]{2,1,0:T(8,128)S(1)}, u32[]{:S(2)}, u32[]{:S(2)}) %collective-permute-start.6) | collective-permute-done | bytes 344096 | tf_op jit(solution)/shard_map/ppermute | solution.py:495
  38.5 3.7 %collective-permute-done.7.x_after = f32[14,48,128]{2,1,0:T(8,128)S(1)} collective-permute-done((f32[14,48,128]{2,1,0:T(8,128)S(1)}, f32[14,48,128]{2,1,0:T(8,128)S(1)}, u32[]{:S(2)}, u32[]{:S(2)}) %collective-permute-start.7) | collective-permute-done | bytes 344096 | tf_op jit(solution)/shard_map/ppermute | solution.py:495
  42.2 4.8 %coarse_outer.1 = (f32[16,16,64]{2,1,0:T(8,128)}, f32[8,8,32]{2,1,0:T(8,128)}, f32[4,4,16]{2,1,0:T(4,128)}, f32[8,128]{1,0:T(8,128)S(1)}, f32[2,8,128]{2,1,0:T(8,128)S(1)}) custom-call(f32[14,48,128]{2,1,0:T(8,128)S(1)} %collective-permute-done.6.x_before, f32[14,48,128]{2,1,0:T(8,128)S(1)} %collective-permute-done.7.x_after, ...), custom_call_target="tpu_custom_call" | custom-call | tf_op jit(solution)/shard_map/coarse_outer/pallas_call | solution.py:561
  47.0 0.0 collective-permute-start.8
  47.0 5.0 %collective-permute-start.9 = (f32[8,128]{1,0:T(8,128)S(1)}, f32[8,128]{1,0:T(8,128)S(1)}, u32[]{:S(2)}, u32[]{:S(2)}) collective-permute-start(f32[8,128]{1,0:T(8,128)S(1)} %get-tuple-element.56.own), channel_id=1, source_target_pairs={{0,15},{1,0},{2,1},{3,2},{4,3},{5,4},{6,5},{7,6},{8,7},{9,8},{10,9... | collective-permute-start | bytes 12296 | tf_op jit(solution)/shard_map/ppermute | solution.py:495
  52.0 1.0 %collective-permute-done.8.y_before = f32[8,128]{1,0:T(8,128)S(1)} collective-permute-done((f32[8,128]{1,0:T(8,128)S(1)}, f32[8,128]{1,0:T(8,128)S(1)}, u32[]{:S(2)}, u32[]{:S(2)}) %collective-permute-start.8) | collective-permute-done | bytes 4128 | tf_op jit(solution)/shard_map/ppermute | solution.py:495
  53.0 0.9 %collective-permute-start.10 = (f32[8,128]{1,0:T(8,128)S(1)}, f32[8,128]{1,0:T(8,128)S(1)}, u32[]{:S(2)}, u32[]{:S(2)}) collective-permute-start(f32[8,128]{1,0:T(8,128)S(1)} %pack_last.1.own), channel_id=1, source_target_pairs={{0,16},{16,32},{32,48},{48,64},{64,80},{80,96},{96,112},{112,128},... | collective-permute-start | bytes 12296 | tf_op jit(solution)/shard_map/ppermute | solution.py:495
  54.0 0.8 %pad_maximum_fusion = f32[32,32,128]{2,1,0:T(8,128)} fusion(f32[2,32,128]{2,1,0:T(8,128)S(1)} %get-tuple-element.63, f32[28,32,128]{2,1,0:T(8,128)S(1)} %slice.16, f32[2,32,128]{2,1,0:T(8,128)S(1)} %get-tuple-element.62), kind=kLoop, calls=%fused_computation | loop fusion | flops 262144 | bytes 1048576 | tf_op jit(solution)/shard_map/concatenate | solution.py:548
  54.8 3.4 %collective-permute-done.11.x_after = f32[8,128]{1,0:T(8,128)S(1)} collective-permute-done((f32[8,128]{1,0:T(8,128)S(1)}, f32[8,128]{1,0:T(8,128)S(1)}, u32[]{:S(2)}, u32[]{:S(2)}) %collective-permute-start.11) | collective-permute-done | bytes 4128 | tf_op jit(solution)/shard_map/ppermute | solution.py:495
  58.2 1.1 %last.1 = (f32[2,2,8]{2,1,0:T(2,128)}, f32[2,2,8]{2,1,0:T(2,128)}) custom-call(f32[8,128]{1,0:T(8,128)S(1)} %pack_last.1.own, f32[8,128]{1,0:T(8,128)S(1)} %collective-permute-done.10.x_before, f32[8,128]{1,0:T(8,128)S(1)} %collective-permute-done.11.x_after, f32[2,8,128]{2,1,0:T(8,128)S(1)} %get-tuple-element.57.k4), custom_call_target="tpu_custom_call" | custom-call | tf_op jit(solution)/shard_map/last/pallas_call | solution.py:571
  (21 shorter events, 0.2 us)
Async XLA Ops:
  0.6 1.0 %copy-start = (f32[32,32,128]{2,1,0:T(8,128)S(1)}, f32[32,32,128]{2,1,0:T(8,128)}, u32[]{:S(2)}) copy-start(f32[32,32,128]{2,1,0:T(8,128)} %guess.3) | copy-start | bytes 1572868
  1.7 1.0 %copy-start.2 = (f32[32,32,128]{2,1,0:T(8,128)S(1)}, f32[32,32,128]{2,1,0:T(8,128)}, u32[]{:S(2)}) copy-start(f32[32,32,128]{2,1,0:T(8,128)} %source.3) | copy-start | bytes 1572868
  2.7 1.0 %copy-start.4 = (f32[32,32,128]{2,1,0:T(8,128)S(1)}, f32[32,32,128]{2,1,0:T(8,128)}, u32[]{:S(2)}) copy-start(f32[32,32,128]{2,1,0:T(8,128)} %reaction.3) | copy-start | bytes 1572868
  3.8 0.7 %copy-start.6 = (s32[1,1,4]{2,1,0:T(1,128)S(1)}, s32[1,1,4]{2,1,0:T(1,128)}, u32[]{:S(2)}) copy-start(s32[1,1,4]{2,1,0:T(1,128)} %flags.1) | copy-start | bytes 52
  4.4 13.0 %copy-start.3 = (f32[32,32,128]{2,1,0:T(8,128)S(1)}, f32[32,32,128]{2,1,0:T(8,128)}, u32[]{:S(2)}) copy-start(f32[32,32,128]{2,1,0:T(8,128)} %source.3) | copy-start | bytes 1572868
  4.4 13.0 %copy-start.5 = (f32[32,32,128]{2,1,0:T(8,128)S(1)}, f32[32,32,128]{2,1,0:T(8,128)}, u32[]{:S(2)}) copy-start(f32[32,32,128]{2,1,0:T(8,128)} %reaction.3) | copy-start | bytes 1572868
  5.2 12.3 %copy-start.1 = (f32[32,32,128]{2,1,0:T(8,128)S(1)}, f32[32,32,128]{2,1,0:T(8,128)}, u32[]{:S(2)}) copy-start(f32[32,32,128]{2,1,0:T(8,128)} %guess.3) | copy-start | bytes 1572868
  5.2 8.1 %collective-permute-start = (f32[32,8,128]{2,1,0:T(8,128)S(1)}, f32[32,8,128]{2,1,0:T(8,128)S(1)}, u32[]{:S(2)}, u32[]{:S(2)}) collective-permute-start(f32[32,8,128]{2,1,0:T(8,128)S(1)} %get-tuple-element.33.own), channel_id=1, source_target_pairs={{0,1},{1,2},{2,3},{3,4},{4,5},{5,6},{6,7},{7,8},{8,9},{9,10},{10,1... | collective-permute-start | bytes 393224 | tf_op jit(solution)/shard_map/ppermute | solution.py:495
  6.5 6.8 %collective-permute-start.1 = (f32[32,8,128]{2,1,0:T(8,128)S(1)}, f32[32,8,128]{2,1,0:T(8,128)S(1)}, u32[]{:S(2)}, u32[]{:S(2)}) collective-permute-start(f32[32,8,128]{2,1,0:T(8,128)S(1)} %get-tuple-element.34), channel_id=1, source_target_pairs={{0,15},{1,0},{2,1},{3,2},{4,3},{5,4},{6,5},{7,6},{8,7},{9,8},{10,9... | collective-permute-start | bytes 393224 | tf_op jit(solution)/shard_map/ppermute | solution.py:495
  13.3 8.8 %collective-permute-start.2 = (f32[8,40,128]{2,1,0:T(8,128)S(1)}, f32[8,40,128]{2,1,0:T(8,128)S(1)}, u32[]{:S(2)}, u32[]{:S(2)}) collective-permute-start(f32[8,40,128]{2,1,0:T(8,128)S(1)} %get-tuple-element.37.packed), channel_id=1, source_target_pairs={{0,16},{16,32},{32,48},{48,64},{64,80},{80,96},{96,112},{112,128},... | collective-permute-start | bytes 491528 | tf_op jit(solution)/shard_map/ppermute | solution.py:495
  17.4 6.0 %collective-permute-start.3 = (f32[8,40,128]{2,1,0:T(8,128)S(1)}, f32[8,40,128]{2,1,0:T(8,128)S(1)}, u32[]{:S(2)}, u32[]{:S(2)}) collective-permute-start(f32[8,40,128]{2,1,0:T(8,128)S(1)} %get-tuple-element.38), channel_id=1, source_target_pairs={{0,240},{16,0},{32,16},{48,32},{64,48},{80,64},{96,80},{112,96},{1... | collective-permute-start | bytes 491528 | tf_op jit(solution)/shard_map/ppermute | solution.py:495
  24.1 7.3 %collective-permute-start.4 = (f32[16,16,128]{2,1,0:T(8,128)S(1)}, f32[16,16,128]{2,1,0:T(8,128)S(1)}, u32[]{:S(2)}, u32[]{:S(2)}) collective-permute-start(f32[16,16,128]{2,1,0:T(8,128)S(1)} %get-tuple-element.47.own), channel_id=1, source_target_pairs={{0,1},{1,2},{2,3},{3,4},{4,5},{5,6},{6,7},{7,8},{8,9},{9,10},{10,1... | collective-permute-start | bytes 393224 | tf_op jit(solution)/shard_map/ppermute | solution.py:495
  24.2 7.2 %collective-permute-start.5 = (f32[16,16,128]{2,1,0:T(8,128)S(1)}, f32[16,16,128]{2,1,0:T(8,128)S(1)}, u32[]{:S(2)}, u32[]{:S(2)}) collective-permute-start(f32[16,16,128]{2,1,0:T(8,128)S(1)} %get-tuple-element.47.own), channel_id=1, source_target_pairs={{0,15},{1,0},{2,1},{3,2},{4,3},{5,4},{6,5},{7,6},{8,7},{9,8},{10,9... | collective-permute-start | bytes 393224 | tf_op jit(solution)/shard_map/ppermute | solution.py:495
  31.5 7.0 %collective-permute-start.6 = (f32[14,48,128]{2,1,0:T(8,128)S(1)}, f32[14,48,128]{2,1,0:T(8,128)S(1)}, u32[]{:S(2)}, u32[]{:S(2)}) collective-permute-start(f32[14,48,128]{2,1,0:T(8,128)S(1)} %get-tuple-element.61), channel_id=1, source_target_pairs={{0,16},{16,32},{32,48},{48,64},{64,80},{80,96},{96,112},{112,128},... | collective-permute-start | bytes 1032200 | tf_op jit(solution)/shard_map/ppermute | solution.py:495
  34.3 7.9 %collective-permute-start.7 = (f32[14,48,128]{2,1,0:T(8,128)S(1)}, f32[14,48,128]{2,1,0:T(8,128)S(1)}, u32[]{:S(2)}, u32[]{:S(2)}) collective-permute-start(f32[14,48,128]{2,1,0:T(8,128)S(1)} %get-tuple-element.60), channel_id=1, source_target_pairs={{0,240},{16,0},{32,16},{48,32},{64,48},{80,64},{96,80},{112,96},{1... | collective-permute-start | bytes 1032200 | tf_op jit(solution)/shard_map/ppermute | solution.py:495
  47.0 6.0 %collective-permute-start.8 = (f32[8,128]{1,0:T(8,128)S(1)}, f32[8,128]{1,0:T(8,128)S(1)}, u32[]{:S(2)}, u32[]{:S(2)}) collective-permute-start(f32[8,128]{1,0:T(8,128)S(1)} %get-tuple-element.56.own), channel_id=1, source_target_pairs={{0,1},{1,2},{2,3},{3,4},{4,5},{5,6},{6,7},{7,8},{8,9},{9,10},{10,1... | collective-permute-start | bytes 12296 | tf_op jit(solution)/shard_map/ppermute | solution.py:495
  47.0 6.0 %collective-permute-start.9 = (f32[8,128]{1,0:T(8,128)S(1)}, f32[8,128]{1,0:T(8,128)S(1)}, u32[]{:S(2)}, u32[]{:S(2)}) collective-permute-start(f32[8,128]{1,0:T(8,128)S(1)} %get-tuple-element.56.own), channel_id=1, source_target_pairs={{0,15},{1,0},{2,1},{3,2},{4,3},{5,4},{6,5},{7,6},{8,7},{9,8},{10,9... | collective-permute-start | bytes 12296 | tf_op jit(solution)/shard_map/ppermute | solution.py:495
  53.0 1.8 %collective-permute-start.10 = (f32[8,128]{1,0:T(8,128)S(1)}, f32[8,128]{1,0:T(8,128)S(1)}, u32[]{:S(2)}, u32[]{:S(2)}) collective-permute-start(f32[8,128]{1,0:T(8,128)S(1)} %pack_last.1.own), channel_id=1, source_target_pairs={{0,16},{16,32},{32,48},{48,64},{64,80},{80,96},{96,112},{112,128},... | collective-permute-start | bytes 12296 | tf_op jit(solution)/shard_map/ppermute | solution.py:495
  54.0 4.2 %collective-permute-start.11 = (f32[8,128]{1,0:T(8,128)S(1)}, f32[8,128]{1,0:T(8,128)S(1)}, u32[]{:S(2)}, u32[]{:S(2)}) collective-permute-start(f32[8,128]{1,0:T(8,128)S(1)} %pack_last.1.own), channel_id=1, source_target_pairs={{0,240},{16,0},{32,16},{48,32},{64,48},{80,64},{96,80},{112,96},{1... | collective-permute-start | bytes 12296 | tf_op jit(solution)/shard_map/ppermute | solution.py:495

commit v3 on v2

--- a/solution.py
+++ b/solution.py
@@ -65,21 +65,23 @@
     return values + pltpu.roll(values, values.shape[0] - 1, 0)
 
 
-def pair_matrix():
-    source = iota((LANES, LANES), 0)
-    target = iota((LANES, LANES), 1)
-    return jnp.where(source >> 1 == target, 0.5, 0.0).astype(F32)
+def pair_matrix(first):
+    source = iota((2 * LANES, LANES), 0) & (LANES - 1)
+    target = iota((2 * LANES, LANES), 1)
+    return jnp.where((source >> 1) + first == target, 0.5, 0.0).astype(jnp.bfloat16)
 
 
 def pair_matrix_halves():
-    source = iota((LANES, LANES), 0)
-    target = iota((LANES, LANES), 1)
+    source = iota((2 * LANES, LANES), 0) & (LANES - 1)
+    target = iota((2 * LANES, LANES), 1)
     hit = ((source & 64) == (target & 64)) & ((source & 63) >> 1 == (target & 63))
-    return jnp.where(hit, 0.5, 0.0).astype(F32)
-
-
-def exact_dot(a, b):
-    return jnp.dot(a, b, precision=lax.Precision.HIGHEST, preferred_element_type=F32)
+    return jnp.where(hit, 0.5, 0.0).astype(jnp.bfloat16)
+
+
+def paired(values, matrix):
+    coarse = values.astype(jnp.bfloat16)
+    fine = (values - coarse.astype(F32)).astype(jnp.bfloat16)
+    return jnp.dot(jnp.concatenate([coarse, fine], axis=1), matrix, preferred_element_type=F32)
 
 
 def loop(first, stop, size, body):
@@ -99,56 +101,14 @@
     return copies
 
 
-def pack_rows(
-    flags, guess, source, reaction, up, down, strip_up, strip_down,
-    flag_smem, guess_lo, guess_hi, source_lo, source_hi, reaction_lo, reaction_hi, sems,
-):
-    lo, hi = pl.ds(0, 8), pl.ds(24, 8)
-    copies = copy_all(
-        sems,
-        (flags, flag_smem),
-        (guess.at[:, lo, :], guess_lo),
-        (guess.at[:, hi, :], guess_hi),
-        (source.at[:, lo, :], source_lo),
-        (source.at[:, hi, :], source_hi),
-        (reaction.at[:, lo, :], reaction_lo),
-        (reaction.at[:, hi, :], reaction_hi),
-        (guess.at[29:32], strip_up.at[0:3]),
-        (source.at[30:32], strip_up.at[3:5]),
-        (reaction.at[30:32], strip_up.at[5:7]),
-        (guess.at[0:3], strip_down.at[0:3]),
-        (source.at[0:2], strip_down.at[3:5]),
-        (reaction.at[0:2], strip_down.at[5:7]),
-    )
-    for copy in copies[:7]:
-        copy.wait()
+def row_messages(source, guess, reaction, flags):
+    depth = source.shape[2]
     boxes = flags.shape[2]
-    lane = iota((8, LANES), 1)
-    flag = jnp.zeros((8, LANES), F32)
-    for i in range(boxes):
-        flag = jnp.where(lane // (LANES // boxes) == i, flag_smem[0, 0, i].astype(F32), flag)
-    flag = flag[None]
-    row = iota(up.shape, 1)
-    up[...] = jnp.where(
-        row >= 5,
-        guess_hi[...],
-        jnp.where(
-            row >= 3,
-            pltpu.roll(source_hi[...], 5, 1),
-            jnp.where(row >= 1, pltpu.roll(reaction_hi[...], 3, 1), flag),
-        ),
-    )
-    down[...] = jnp.where(
-        row < 3,
-        guess_lo[...],
-        jnp.where(
-            row < 5,
-            pltpu.roll(source_lo[...], 3, 1),
-            jnp.where(row < 7, pltpu.roll(reaction_lo[...], 5, 1), flag),
-        ),
-    )
-    for copy in copies[7:]:
-        copy.wait()
+    flag = jnp.repeat(flags[0, 0].astype(F32), depth // boxes)
+    flag = jnp.broadcast_to(flag, (source.shape[0], 1, depth))
+    up = jnp.concatenate([flag, reaction[:, -2:], source[:, -2:], guess[:, -3:]], axis=1)
+    down = jnp.concatenate([guess[:, :3], source[:, :2], reaction[:, :2], flag], axis=1)
+    return up, down
 
 
 def halo_tiles(from_before, from_after, before, after):
@@ -250,9 +210,8 @@
             kpairs[i + j] = value
 
     loop(0, 16, 4, fourth)
-    to_low = pair_matrix()
-    rk = exact_dot(compact(range(16), kpairs, 16), pltpu.roll(to_low, 64, 1)).reshape(16, 16, LANES)
-    rf = exact_dot(compact(range(12), pairs, 16), to_low).reshape(12, 16, LANES)
+    rk = paired(compact(range(16), kpairs, 16), pair_matrix(64)).reshape(16, 16, LANES)
+    rf = paired(compact(range(12), pairs, 16), pair_matrix(0)).reshape(12, 16, LANES)
     coarse[0:2] = rk[0:2]
     coarse[2:14] = rk[2:14] + rf
     coarse[14:16] = rk[14:16]
@@ -301,7 +260,7 @@
         out = [r for _, r, _ in remainders(lambda i: new_w[i] if i in new_w else w[i], first, 4)]
         pairs[2 * at] = pair_rows(out[0] + out[1])
         pairs[2 * at + 1] = pair_rows(out[2] + out[3])
-    rf = exact_dot(compact(range(4), pairs, 16), pair_matrix()).reshape(4, 16, LANES)
+    rf = paired(compact(range(4), pairs, 16), pair_matrix(0)).reshape(4, 16, LANES)
     coarse[0:2] = inner[0:2] + rf[0:2]
     coarse[2:14] = inner[2:14]
     coarse[14:16] = inner[14:16] + rf[2:4]
@@ -364,10 +323,11 @@
         kpairs[j] = pair_rows(reactions[2 * j + 2] + reactions[2 * j + 3])
     halve = pair_matrix_halves()
     _, inside = masks_of(24, 8, 16, 32)
-    rf = exact_dot(compact(range(3), pairs, 24), halve).reshape(3, 24, LANES)
+    both = jnp.concatenate([compact(range(3), pairs, 24), compact(range(3), kpairs, 24)], axis=0)
+    both = paired(both, halve).reshape(6, 24, LANES)
     for j in range(3):
-        f2[j] = rf[j] * inside
-    k2[...] = exact_dot(compact(range(3), kpairs, 24), halve).reshape(3, 24, LANES)
+        f2[j] = both[j] * inside
+    k2[...] = both[3:6]
 
 
 def coarse_outer(
@@ -420,15 +380,20 @@
 
     loop(2, 16, 2, two)
     half = slice(16, 32)
+    halve = pair_matrix_halves()
+
+    def both(fields, reactions, rows):
+        values = [compact(range(fields), pairs, rows), compact(range(reactions), kpairs, rows)]
+        out = paired(jnp.concatenate(values, axis=0), halve).reshape(fields + reactions, rows, LANES)
+        return out[:fields], out[fields:]
+
     e1[0] = e[14, half, 0:64]
     e1[15] = swap(e[14, half, :])[:, 0:64]
     for j in range(1, 8):
         value = e_in[j, half, :]
         e1[j] = value[:, 0:64]
         e1[15 - j] = swap(value)[:, 0:64]
-    halve = pair_matrix_halves()
-    rf = exact_dot(compact(range(7), pairs, 24), halve).reshape(7, 24, LANES)
-    rk = exact_dot(compact(range(7), kpairs, 24), halve).reshape(7, 24, LANES)
+    rf, rk = both(7, 7, 24)
     outside, inside = masks_of(24, 8, 16, 32)
     fields = [rf[j] * (outside if j < 6 else inside) for j in range(7)] + [f2_in[j] for j in range(3)]
     reactions = [rk[j] for j in range(7)] + [k2_in[j] for j in range(3)]
@@ -443,8 +408,7 @@
     for p in range(4):
         pairs[p, 0:24, :] = pair_rows(rest[2 * p] + rest[2 * p + 1])
         kpairs[p, 0:24, :] = pair_rows(reactions[2 * p + 2] + reactions[2 * p + 3])
-    rf = exact_dot(compact(range(4), pairs, 16), halve).reshape(4, 16, LANES)
-    rk = exact_dot(compact(range(4), kpairs, 16), halve).reshape(4, 16, LANES)
+    rf, rk = both(4, 4, 16)
     outside, inside = masks_of(16, 4, 8, 16)
     fields = [rf[0] * outside, rf[1] * outside, rf[2] * inside, rf[3] * inside]
     reactions = [rk[j] for j in range(4)]
@@ -457,8 +421,9 @@
     pairs[0, 0:16, :] = pair_rows(rest[0] + rest[1])
     for p in range(2):
         kpairs[p, 0:16, :] = pair_rows(reactions[2 * p] + reactions[2 * p + 1])
-    f4[...] = exact_dot(compact(range(1), pairs, 8), halve)
-    k4[...] = exact_dot(compact(range(2), kpairs, 8), halve).reshape(2, 8, LANES)
+    rf, rk = both(1, 2, 8)
+    f4[...] = rf[0]
+    k4[...] = rk
 
 
 def pack_last(y_before, own, y_after, out):
@@ -514,16 +479,10 @@
 
 
 def per_device(source, guess, reaction, flags):
-    tile = (32, 8, LANES)
-    own, down, strip_up, strip_down = call(
-        pack_rows,
-        [tile, tile, (7, 32, LANES), (7, 32, LANES)],
-        [HBM] * 4,
-        scratch=[pltpu.SMEM((1, 1, flags.shape[2]), jnp.int32)] + [tile] * 6,
-        copies=13,
-        name="pack_rows",
-    )(flags, guess, source, reaction)
+    own, down = row_messages(source, guess, reaction, flags)
     y_before, y_after = neighbours_of(own, down, "agg")
+    strip_up = jnp.concatenate([guess[-3:], source[-2:], reaction[-2:]], axis=0)
+    strip_down = jnp.concatenate([guess[:3], source[:2], reaction[:2]], axis=0)
     packed, down = call(
         pack_planes, [(8, 40, LANES)] * 2, [VMEM] * 5, name="pack_planes"
     )(own, y_before, y_after, strip_up, strip_down)

time: 59.6 us -> 57.7 us (0.968)
  Pallas kernels: 12.8 us -> 11.4 us
  other arithmetic: 0.83 us -> 1.68 us
  local copies, waits for them, and re-layouts: 3.92 us -> 3.31 us
    unnamed x16 -> x8, local copies, waits for them, and re-layouts: 3.81 us -> 0.04 us
    slice x0 -> x5, local copies, waits for them, and re-layouts: none -> 3 us  [the longest x1 1.15 us: row_messages(): source[:, :2]]
    pallas_call x1 -> x0, Pallas kernels: 0.72 us -> none  [per_device(): call(pack_rows, [tile, tile, (7, 32, LANES), (7, 32, LANES)], [HBM] * 4,...]
    convert_element_type x0 -> x1, other arithmetic: none -> 0.72 us  [row_messages(): flag = jnp.repeat(flags[0, 0].astype(F32), depth // boxes)]
  transfers between devices with their start and end apart: 12 -> 12, of which waited for: 7 -> 7; matrix products, arithmetic and copies ran while one was open for 2% -> 3% of each run, Pallas kernels for 9% -> 9%
where the time goes in v3:
time: 57.7 us; the launch traced here: 57.4 us
  starting transfers between devices  22.8 us (40%)
  waiting for transfers between devices  17.4 us (30%)
  Pallas kernels  11.4 us (20%)
  local copies, waits for them, and re-layouts  3.31 us (6%)
  other arithmetic  1.68 us (3%)
  between operations  0.79 us (1%)
    ppermute x12, starting transfers between devices, neighbours_of(): return (lax.ppermute(up, axis, ahead), lax.ppermute(down, axis, back))  22.8 us
    ppermute x12, waiting for transfers between devices, neighbours_of(): return (lax.ppermute(up, axis, ahead), lax.ppermute(down, axis, back))  17.4 us
    pallas_call x1, Pallas kernels, per_device(): call(fine_inner, [big] * 6 + [(16, 16, LANES)], [VMEM] * 3 + [HBM] * 3, s...  4.47 us
    pallas_call x1, Pallas kernels, per_device(): call(coarse_outer, [(16, 16, 64), (8, 8, 32), (4, 4, 16), (8, LANES), (2,...  4.45 us
  transfers between devices with their start and end apart: 12, of which 7 were waited for; matrix products, arithmetic and copies ran while one was open for 3% of the time, Pallas kernels for 9%

profile of v3, /device:TPU:97, one launch (start us, length us, event | category | flops | bytes accessed | tf_op | source)
XLA Modules:
  0.0 57.4 jit_solution(3870372287608932543)
XLA Ops:
  0.6 1.1 %fusion.3 = (f32[32,3,128]{2,1,0:T(4,128)S(1)}, f32[32,3,128]{2,1,0:T(4,128)S(1)}) fusion(f32[32,32,128]{2,1,0:T(8,128)} %guess.1), kind=kLoop, calls=%fused_computation.12 | loop fusion | bytes 196608 | tf_op jit(solution)/shard_map/slice | solution.py:110
  1.7 0.0 copy-start.1
  1.7 0.7 %convert_bitcast_fusion = f32[4]{0:T(128)S(1)} fusion(s32[1,1,4]{2,1,0:T(1,128)} %param.7), kind=kLoop, calls=%fused_computation.8 | loop fusion | flops 4 | bytes 32 | tf_op jit(solution)/shard_map/convert_element_type | solution.py:107
  2.4 0.1 broadcast_in_dim.6
  2.5 0.1 reshape.16
  2.6 1.1 %fusion.4 = (f32[32,2,128]{2,1,0:T(2,128)S(1)}, f32[32,2,128]{2,1,0:T(2,128)S(1)}, f32[32,2,128]{2,1,0:T(2,128)S(1)}, f32[32,2,128]{2,1,0:T(2,128)S(1)}) fusion(f32[32,32,128]{2,1,0:T(8,128)} %source.1, f32[32,32,128]{2,1,0:T(8,128)} %reaction.1), kind=kLoop, calls=%fused_computation.13 | loop fusion | bytes 262144 | tf_op jit(solution)/shard_map/slice | solution.py:110
  3.8 0.1 pad_maximum_fusion.2
  3.9 1.3 %collective-permute-start = (f32[32,8,128]{2,1,0:T(8,128)S(1)}, f32[32,8,128]{2,1,0:T(8,128)S(1)}, u32[]{:S(2)}, u32[]{:S(2)}) collective-permute-start(f32[32,8,128]{2,1,0:T(8,128)S(1)} %get-tuple-element.69.own), channel_id=1, source_target_pairs={{0,1},{1,2},{2,3},{3,4},{4,5},{5,6},{6,7},{7,8},{8,9},{9,10},{10,1... | collective-permute-start | bytes 393224 | tf_op jit(solution)/shard_map/ppermute | solution.py:460
  5.2 3.8 %collective-permute-start.1 = (f32[32,8,128]{2,1,0:T(8,128)S(1)}, f32[32,8,128]{2,1,0:T(8,128)S(1)}, u32[]{:S(2)}, u32[]{:S(2)}) collective-permute-start(f32[32,8,128]{2,1,0:T(8,128)S(1)} %get-tuple-element.68), channel_id=1, source_target_pairs={{0,15},{1,0},{2,1},{3,2},{4,3},{5,4},{6,5},{7,6},{8,7},{9,8},{10,9... | collective-permute-start | bytes 393224 | tf_op jit(solution)/shard_map/ppermute | solution.py:460
  9.0 0.8 %fusion.2 = (f32[2,32,128]{2,1,0:T(8,128)S(1)}, f32[2,32,128]{2,1,0:T(8,128)S(1)}) fusion(f32[32,32,128]{2,1,0:T(8,128)} %reaction.1), kind=kLoop, calls=%fused_computation.11 | loop fusion | bytes 131072 | tf_op jit(solution)/shard_map/slice | solution.py:485
  9.8 2.1 %collective-permute-done.from_before = f32[32,8,128]{2,1,0:T(8,128)S(1)} collective-permute-done((f32[32,8,128]{2,1,0:T(8,128)S(1)}, f32[32,8,128]{2,1,0:T(8,128)S(1)}, u32[]{:S(2)}, u32[]{:S(2)}) %collective-permute-start) | collective-permute-done | bytes 131104 | tf_op jit(solution)/shard_map/ppermute | solution.py:460
  12.0 0.0 collective-permute-done.1.from_after
  12.0 4.1 %collective-permute-start.2 = (f32[8,40,128]{2,1,0:T(8,128)S(1)}, f32[8,40,128]{2,1,0:T(8,128)S(1)}, u32[]{:S(2)}, u32[]{:S(2)}) collective-permute-start(f32[8,40,128]{2,1,0:T(8,128)S(1)} %get-tuple-element.29.packed), channel_id=1, source_target_pairs={{0,16},{16,32},{32,48},{48,64},{64,80},{80,96},{96,112},{112,128},... | collective-permute-start | bytes 491528 | tf_op jit(solution)/shard_map/ppermute | solution.py:460
  16.1 0.0 collective-permute-start.3
  16.1 4.5 %fine_inner.1 = (f32[32,40,128]{2,1,0:T(8,128)S(1)}, f32[32,40,128]{2,1,0:T(8,128)S(1)}, f32[32,40,128]{2,1,0:T(8,128)S(1)}, f32[32,40,128]{2,1,0:T(8,128)S(1)},...) custom-call(f32[8,40,128]{2,1,0:T(8,128)S(1)} %get-tuple-element.29.packed, ...), custom_call_target="tpu_custom_call" | custom-call | flops 8000000 | bytes 8000000 | tf_op jit(solution)/shard_map/fine_inner/pallas_call | solution.py:491
  20.6 0.0 collective-permute-done.2.x_before
  20.6 1.5 %collective-permute-done.3.x_after = f32[8,40,128]{2,1,0:T(8,128)S(1)} collective-permute-done((f32[8,40,128]{2,1,0:T(8,128)S(1)}, f32[8,40,128]{2,1,0:T(8,128)S(1)}, u32[]{:S(2)}, u32[]{:S(2)}) %collective-permute-start.3) | collective-permute-done | bytes 163872 | tf_op jit(solution)/shard_map/ppermute | solution.py:460
  22.1 0.7 %fine_outer.1 = (f32[16,16,128]{2,1,0:T(8,128)S(1)}, f32[4,32,128]{2,1,0:T(8,128)S(1)}) custom-call(f32[8,40,128]{2,1,0:T(8,128)S(1)} %get-tuple-element.29.packed, f32[8,40,128]{2,1,0:T(8,128)S(1)} %collective-permute-done.2.x_before, f32[8,40,128]{2,1,0:T(8,128)S(1)} %collective-permute-done.3.x_after, f32[32,40,128]{2,1,0:T(8,128)S(1)} %get-tuple-element.31.g, ...), custom_call_target="tpu_custom_call" | custom-call | tf_op jit(solution)/shard_map/fine_outer/pallas_call | solution.py:500
  22.8 0.1 collective-permute-start.4
  22.9 4.9 %collective-permute-start.5 = (f32[16,16,128]{2,1,0:T(8,128)S(1)}, f32[16,16,128]{2,1,0:T(8,128)S(1)}, u32[]{:S(2)}, u32[]{:S(2)}) collective-permute-start(f32[16,16,128]{2,1,0:T(8,128)S(1)} %get-tuple-element.39.own), channel_id=1, source_target_pairs={{0,15},{1,0},{2,1},{3,2},{4,3},{5,4},{6,5},{7,6},{8,7},{9,8},{10,9... | collective-permute-start | bytes 393224 | tf_op jit(solution)/shard_map/ppermute | solution.py:460
  27.8 2.3 %collective-permute-done.4.y_before = f32[16,16,128]{2,1,0:T(8,128)S(1)} collective-permute-done((f32[16,16,128]{2,1,0:T(8,128)S(1)}, f32[16,16,128]{2,1,0:T(8,128)S(1)}, u32[]{:S(2)}, u32[]{:S(2)}) %collective-permute-start.4) | collective-permute-done | bytes 131104 | tf_op jit(solution)/shard_map/ppermute | solution.py:460
  30.2 2.6 %collective-permute-start.6 = (f32[14,48,128]{2,1,0:T(8,128)S(1)}, f32[14,48,128]{2,1,0:T(8,128)S(1)}, u32[]{:S(2)}, u32[]{:S(2)}) collective-permute-start(f32[14,48,128]{2,1,0:T(8,128)S(1)} %get-tuple-element.65), channel_id=1, source_target_pairs={{0,16},{16,32},{32,48},{48,64},{64,80},{80,96},{96,112},{112,128},... | collective-permute-start | bytes 1032200 | tf_op jit(solution)/shard_map/ppermute | solution.py:460
  32.8 0.7 %coarse_inner.1 = (f32[8,48,128]{2,1,0:T(8,128)S(1)}, f32[8,48,128]{2,1,0:T(8,128)S(1)}, f32[8,48,128]{2,1,0:T(8,128)S(1)}, f32[3,24,128]{2,1,0:T(8,128)S(1)}, f32[3,24,128]{2,1,0:T(8,128)S(1)}) custom-call(f32[16,16,128]{2,1,0:T(8,128)S(1)} %collective-permute-done.4.y_before, f32[16,16,128]{2,1,0:T(8,128)S(1)} %get-tuple-element.39.own, ...), custom_call_target="tpu_custom_call" | custom-call | flops 4000000 | bytes 4000000 | tf_op jit(solution)/shard_map/coarse_inner/pallas_call | solution.py:512
  33.5 3.4 %collective-permute-done.6.x_before = f32[14,48,128]{2,1,0:T(8,128)S(1)} collective-permute-done((f32[14,48,128]{2,1,0:T(8,128)S(1)}, f32[14,48,128]{2,1,0:T(8,128)S(1)}, u32[]{:S(2)}, u32[]{:S(2)}) %collective-permute-start.6) | collective-permute-done | bytes 344096 | tf_op jit(solution)/shard_map/ppermute | solution.py:460
  37.0 3.7 %collective-permute-done.7.x_after = f32[14,48,128]{2,1,0:T(8,128)S(1)} collective-permute-done((f32[14,48,128]{2,1,0:T(8,128)S(1)}, f32[14,48,128]{2,1,0:T(8,128)S(1)}, u32[]{:S(2)}, u32[]{:S(2)}) %collective-permute-start.7) | collective-permute-done | bytes 344096 | tf_op jit(solution)/shard_map/ppermute | solution.py:460
  40.7 4.4 %coarse_outer.1 = (f32[16,16,64]{2,1,0:T(8,128)}, f32[8,8,32]{2,1,0:T(8,128)}, f32[4,4,16]{2,1,0:T(4,128)}, f32[8,128]{1,0:T(8,128)S(1)}, f32[2,8,128]{2,1,0:T(8,128)S(1)}) custom-call(f32[14,48,128]{2,1,0:T(8,128)S(1)} %collective-permute-done.6.x_before, f32[14,48,128]{2,1,0:T(8,128)S(1)} %collective-permute-done.7.x_after, ...), custom_call_target="tpu_custom_call" | custom-call | tf_op jit(solution)/shard_map/coarse_outer/pallas_call | solution.py:520
  45.1 5.0 %collective-permute-start.9 = (f32[8,128]{1,0:T(8,128)S(1)}, f32[8,128]{1,0:T(8,128)S(1)}, u32[]{:S(2)}, u32[]{:S(2)}) collective-permute-start(f32[8,128]{1,0:T(8,128)S(1)} %get-tuple-element.48.own), channel_id=1, source_target_pairs={{0,15},{1,0},{2,1},{3,2},{4,3},{5,4},{6,5},{7,6},{8,7},{9,8},{10,9... | collective-permute-start | bytes 12296 | tf_op jit(solution)/shard_map/ppermute | solution.py:460
  50.1 1.0 %collective-permute-done.8.y_before = f32[8,128]{1,0:T(8,128)S(1)} collective-permute-done((f32[8,128]{1,0:T(8,128)S(1)}, f32[8,128]{1,0:T(8,128)S(1)}, u32[]{:S(2)}, u32[]{:S(2)}) %collective-permute-start.8) | collective-permute-done | bytes 4128 | tf_op jit(solution)/shard_map/ppermute | solution.py:460
  51.1 0.9 %collective-permute-start.10 = (f32[8,128]{1,0:T(8,128)S(1)}, f32[8,128]{1,0:T(8,128)S(1)}, u32[]{:S(2)}, u32[]{:S(2)}) collective-permute-start(f32[8,128]{1,0:T(8,128)S(1)} %pack_last.1.own), channel_id=1, source_target_pairs={{0,16},{16,32},{32,48},{48,64},{64,80},{80,96},{96,112},{112,128},... | collective-permute-start | bytes 12296 | tf_op jit(solution)/shard_map/ppermute | solution.py:460
  52.1 0.8 %pad_maximum_fusion = f32[32,32,128]{2,1,0:T(8,128)} fusion(f32[2,32,128]{2,1,0:T(8,128)S(1)} %get-tuple-element.67, f32[28,32,128]{2,1,0:T(8,128)S(1)} %slice.64, f32[2,32,128]{2,1,0:T(8,128)S(1)} %get-tuple-element.66), kind=kLoop, calls=%fused_computation | loop fusion | flops 262144 | bytes 1048576 | tf_op jit(solution)/shard_map/concatenate | solution.py:507
  52.9 3.4 %collective-permute-done.11.x_after = f32[8,128]{1,0:T(8,128)S(1)} collective-permute-done((f32[8,128]{1,0:T(8,128)S(1)}, f32[8,128]{1,0:T(8,128)S(1)}, u32[]{:S(2)}, u32[]{:S(2)}) %collective-permute-start.11) | collective-permute-done | bytes 4128 | tf_op jit(solution)/shard_map/ppermute | solution.py:460
  56.3 1.1 %last.1 = (f32[2,2,8]{2,1,0:T(2,128)}, f32[2,2,8]{2,1,0:T(2,128)}) custom-call(f32[8,128]{1,0:T(8,128)S(1)} %pack_last.1.own, f32[8,128]{1,0:T(8,128)S(1)} %collective-permute-done.10.x_before, f32[8,128]{1,0:T(8,128)S(1)} %collective-permute-done.11.x_after, f32[2,8,128]{2,1,0:T(8,128)S(1)} %get-tuple-element.49.k4), custom_call_target="tpu_custom_call" | custom-call | tf_op jit(solution)/shard_map/last/pallas_call | solution.py:530
  (23 shorter events, 0.2 us)
Async XLA Ops:
  0.6 8.3 %copy-start = (f32[32,32,128]{2,1,0:T(8,128)S(1)}, f32[32,32,128]{2,1,0:T(8,128)}, u32[]{:S(2)}) copy-start(f32[32,32,128]{2,1,0:T(8,128)} %guess.1) | copy-start | bytes 1572868
  1.7 7.3 %copy-start.1 = (f32[32,32,128]{2,1,0:T(8,128)S(1)}, f32[32,32,128]{2,1,0:T(8,128)}, u32[]{:S(2)}) copy-start(f32[32,32,128]{2,1,0:T(8,128)} %source.1) | copy-start | bytes 1572868
  3.9 8.1 %collective-permute-start = (f32[32,8,128]{2,1,0:T(8,128)S(1)}, f32[32,8,128]{2,1,0:T(8,128)S(1)}, u32[]{:S(2)}, u32[]{:S(2)}) collective-permute-start(f32[32,8,128]{2,1,0:T(8,128)S(1)} %get-tuple-element.69.own), channel_id=1, source_target_pairs={{0,1},{1,2},{2,3},{3,4},{4,5},{5,6},{6,7},{7,8},{8,9},{9,10},{10,1... | collective-permute-start | bytes 393224 | tf_op jit(solution)/shard_map/ppermute | solution.py:460
  5.2 6.8 %collective-permute-start.1 = (f32[32,8,128]{2,1,0:T(8,128)S(1)}, f32[32,8,128]{2,1,0:T(8,128)S(1)}, u32[]{:S(2)}, u32[]{:S(2)}) collective-permute-start(f32[32,8,128]{2,1,0:T(8,128)S(1)} %get-tuple-element.68), channel_id=1, source_target_pairs={{0,15},{1,0},{2,1},{3,2},{4,3},{5,4},{6,5},{7,6},{8,7},{9,8},{10,9... | collective-permute-start | bytes 393224 | tf_op jit(solution)/shard_map/ppermute | solution.py:460
  9.8 6.3 %copy-start.2 = (f32[32,32,128]{2,1,0:T(8,128)S(1)}, f32[32,32,128]{2,1,0:T(8,128)}, u32[]{:S(2)}) copy-start(f32[32,32,128]{2,1,0:T(8,128)} %reaction.1) | copy-start | bytes 1572868
  12.0 8.6 %collective-permute-start.2 = (f32[8,40,128]{2,1,0:T(8,128)S(1)}, f32[8,40,128]{2,1,0:T(8,128)S(1)}, u32[]{:S(2)}, u32[]{:S(2)}) collective-permute-start(f32[8,40,128]{2,1,0:T(8,128)S(1)} %get-tuple-element.29.packed), channel_id=1, source_target_pairs={{0,16},{16,32},{32,48},{48,64},{64,80},{80,96},{96,112},{112,128},... | collective-permute-start | bytes 491528 | tf_op jit(solution)/shard_map/ppermute | solution.py:460
  16.1 6.0 %collective-permute-start.3 = (f32[8,40,128]{2,1,0:T(8,128)S(1)}, f32[8,40,128]{2,1,0:T(8,128)S(1)}, u32[]{:S(2)}, u32[]{:S(2)}) collective-permute-start(f32[8,40,128]{2,1,0:T(8,128)S(1)} %get-tuple-element.30), channel_id=1, source_target_pairs={{0,240},{16,0},{32,16},{48,32},{64,48},{80,64},{96,80},{112,96},{1... | collective-permute-start | bytes 491528 | tf_op jit(solution)/shard_map/ppermute | solution.py:460
  22.8 7.3 %collective-permute-start.4 = (f32[16,16,128]{2,1,0:T(8,128)S(1)}, f32[16,16,128]{2,1,0:T(8,128)S(1)}, u32[]{:S(2)}, u32[]{:S(2)}) collective-permute-start(f32[16,16,128]{2,1,0:T(8,128)S(1)} %get-tuple-element.39.own), channel_id=1, source_target_pairs={{0,1},{1,2},{2,3},{3,4},{4,5},{5,6},{6,7},{7,8},{8,9},{9,10},{10,1... | collective-permute-start | bytes 393224 | tf_op jit(solution)/shard_map/ppermute | solution.py:460
  22.9 7.2 %collective-permute-start.5 = (f32[16,16,128]{2,1,0:T(8,128)S(1)}, f32[16,16,128]{2,1,0:T(8,128)S(1)}, u32[]{:S(2)}, u32[]{:S(2)}) collective-permute-start(f32[16,16,128]{2,1,0:T(8,128)S(1)} %get-tuple-element.39.own), channel_id=1, source_target_pairs={{0,15},{1,0},{2,1},{3,2},{4,3},{5,4},{6,5},{7,6},{8,7},{9,8},{10,9... | collective-permute-start | bytes 393224 | tf_op jit(solution)/shard_map/ppermute | solution.py:460
  30.2 6.8 %collective-permute-start.6 = (f32[14,48,128]{2,1,0:T(8,128)S(1)}, f32[14,48,128]{2,1,0:T(8,128)S(1)}, u32[]{:S(2)}, u32[]{:S(2)}) collective-permute-start(f32[14,48,128]{2,1,0:T(8,128)S(1)} %get-tuple-element.65), channel_id=1, source_target_pairs={{0,16},{16,32},{32,48},{48,64},{64,80},{80,96},{96,112},{112,128},... | collective-permute-start | bytes 1032200 | tf_op jit(solution)/shard_map/ppermute | solution.py:460
  32.8 7.9 %collective-permute-start.7 = (f32[14,48,128]{2,1,0:T(8,128)S(1)}, f32[14,48,128]{2,1,0:T(8,128)S(1)}, u32[]{:S(2)}, u32[]{:S(2)}) collective-permute-start(f32[14,48,128]{2,1,0:T(8,128)S(1)} %get-tuple-element.64), channel_id=1, source_target_pairs={{0,240},{16,0},{32,16},{48,32},{64,48},{80,64},{96,80},{112,96},{1... | collective-permute-start | bytes 1032200 | tf_op jit(solution)/shard_map/ppermute | solution.py:460
  45.1 6.0 %collective-permute-start.8 = (f32[8,128]{1,0:T(8,128)S(1)}, f32[8,128]{1,0:T(8,128)S(1)}, u32[]{:S(2)}, u32[]{:S(2)}) collective-permute-start(f32[8,128]{1,0:T(8,128)S(1)} %get-tuple-element.48.own), channel_id=1, source_target_pairs={{0,1},{1,2},{2,3},{3,4},{4,5},{5,6},{6,7},{7,8},{8,9},{9,10},{10,1... | collective-permute-start | bytes 12296 | tf_op jit(solution)/shard_map/ppermute | solution.py:460
  45.1 6.0 %collective-permute-start.9 = (f32[8,128]{1,0:T(8,128)S(1)}, f32[8,128]{1,0:T(8,128)S(1)}, u32[]{:S(2)}, u32[]{:S(2)}) collective-permute-start(f32[8,128]{1,0:T(8,128)S(1)} %get-tuple-element.48.own), channel_id=1, source_target_pairs={{0,15},{1,0},{2,1},{3,2},{4,3},{5,4},{6,5},{7,6},{8,7},{9,8},{10,9... | collective-permute-start | bytes 12296 | tf_op jit(solution)/shard_map/ppermute | solution.py:460
  51.1 1.8 %collective-permute-start.10 = (f32[8,128]{1,0:T(8,128)S(1)}, f32[8,128]{1,0:T(8,128)S(1)}, u32[]{:S(2)}, u32[]{:S(2)}) collective-permute-start(f32[8,128]{1,0:T(8,128)S(1)} %pack_last.1.own), channel_id=1, source_target_pairs={{0,16},{16,32},{32,48},{48,64},{64,80},{80,96},{96,112},{112,128},... | collective-permute-start | bytes 12296 | tf_op jit(solution)/shard_map/ppermute | solution.py:460
  52.1 4.2 %collective-permute-start.11 = (f32[8,128]{1,0:T(8,128)S(1)}, f32[8,128]{1,0:T(8,128)S(1)}, u32[]{:S(2)}, u32[]{:S(2)}) collective-permute-start(f32[8,128]{1,0:T(8,128)S(1)} %pack_last.1.own), channel_id=1, source_target_pairs={{0,240},{16,0},{32,16},{48,32},{64,48},{80,64},{96,80},{112,96},{1... | collective-permute-start | bytes 12296 | tf_op jit(solution)/shard_map/ppermute | solution.py:460

commit v4 on v2

--- a/solution.py
+++ b/solution.py
@@ -65,25 +65,30 @@
     return values + pltpu.roll(values, values.shape[0] - 1, 0)
 
 
-def pair_matrix():
-    source = iota((LANES, LANES), 0)
-    target = iota((LANES, LANES), 1)
-    return jnp.where(source >> 1 == target, 0.5, 0.0).astype(F32)
+def pair_matrix(first):
+    source = iota((2 * LANES, LANES), 0) & (LANES - 1)
+    target = iota((2 * LANES, LANES), 1)
+    return jnp.where((source >> 1) + first == target, 0.5, 0.0).astype(jnp.bfloat16)
 
 
 def pair_matrix_halves():
-    source = iota((LANES, LANES), 0)
-    target = iota((LANES, LANES), 1)
+    source = iota((2 * LANES, LANES), 0) & (LANES - 1)
+    target = iota((2 * LANES, LANES), 1)
     hit = ((source & 64) == (target & 64)) & ((source & 63) >> 1 == (target & 63))
-    return jnp.where(hit, 0.5, 0.0).astype(F32)
-
-
-def exact_dot(a, b):
-    return jnp.dot(a, b, precision=lax.Precision.HIGHEST, preferred_element_type=F32)
+    return jnp.where(hit, 0.5, 0.0).astype(jnp.bfloat16)
+
+
+def paired(values, matrix):
+    coarse = values.astype(jnp.bfloat16)
+    fine = (values - coarse.astype(F32)).astype(jnp.bfloat16)
+    return jnp.dot(jnp.concatenate([coarse, fine], axis=1), matrix, preferred_element_type=F32)
 
 
 def loop(first, stop, size, body):
     count = (stop - first) // size
+    if count == 1:
+        body(first)
+        return
 
     def step(i, carry):
         body(first + i * size)
@@ -201,13 +206,13 @@
     theta, c1, c2 = coefficients(0)
 
     def assemble(x):
-        at = pl.ds(x, 8)
+        at = pl.ds(x, 32)
         tiles = halo_tiles(from_before[at], from_after[at], before, after)
         g[at, 32:40, :] = tiles[0]
         s[at, 32:40, :] = tiles[1]
         k[at, 32:40, :] = tiles[2]
 
-    loop(0, 32, 8, assemble)
+    loop(0, 32, 32, assemble)
     for copy in copies:
         copy.wait()
 
@@ -221,38 +226,37 @@
         return out
 
     def first(x):
-        out = remainders(g, x, 3)
+        out = remainders(g, x, 10)
         for i, (r, middle) in enumerate(out):
             step = r * (1.0 / theta)
             d[x + i] = step
             u[x + i] = middle + step
 
-    loop(1, 31, 3, first)
+    loop(1, 31, 10, first)
 
     def second(x):
-        out = [m + (c1 * d[x + i] + c2 * r) for i, (r, m) in enumerate(remainders(u, x, 4))]
+        out = [m + (c1 * d[x + i] + c2 * r) for i, (r, m) in enumerate(remainders(u, x, 14))]
         for i, value in enumerate(out):
             w[x + i] = value
 
-    loop(2, 30, 4, second)
+    loop(2, 30, 14, second)
 
     def third(x):
-        out = [r for r, _ in remainders(w, x, 4)]
+        out = [r for r, _ in remainders(w, x, 24)]
         at = (x - 4) // 2
-        pairs[at] = pair_rows(out[0] + out[1])
-        pairs[at + 1] = pair_rows(out[2] + out[3])
-
-    loop(4, 28, 4, third)
+        for i in range(len(out) // 2):
+            pairs[at + i] = pair_rows(out[2 * i] + out[2 * i + 1])
+
+    loop(4, 28, 24, third)
 
     def fourth(i):
-        out = [pair_rows(k[2 * i + 2 * j, 0:32, :] + k[2 * i + 2 * j + 1, 0:32, :]) for j in range(4)]
+        out = [pair_rows(k[2 * i + 2 * j, 0:32, :] + k[2 * i + 2 * j + 1, 0:32, :]) for j in range(16)]
         for j, value in enumerate(out):
             kpairs[i + j] = value
 
-    loop(0, 16, 4, fourth)
-    to_low = pair_matrix()
-    rk = exact_dot(compact(range(16), kpairs, 16), pltpu.roll(to_low, 64, 1)).reshape(16, 16, LANES)
-    rf = exact_dot(compact(range(12), pairs, 16), to_low).reshape(12, 16, LANES)
+    loop(0, 16, 16, fourth)
+    rk = paired(compact(range(16), kpairs, 16), pair_matrix(64)).reshape(16, 16, LANES)
+    rf = paired(compact(range(12), pairs, 16), pair_matrix(0)).reshape(12, 16, LANES)
     coarse[0:2] = rk[0:2]
     coarse[2:14] = rk[2:14] + rf
     coarse[14:16] = rk[14:16]
@@ -301,7 +305,7 @@
         out = [r for _, r, _ in remainders(lambda i: new_w[i] if i in new_w else w[i], first, 4)]
         pairs[2 * at] = pair_rows(out[0] + out[1])
         pairs[2 * at + 1] = pair_rows(out[2] + out[3])
-    rf = exact_dot(compact(range(4), pairs, 16), pair_matrix()).reshape(4, 16, LANES)
+    rf = paired(compact(range(4), pairs, 16), pair_matrix(0)).reshape(4, 16, LANES)
     coarse[0:2] = inner[0:2] + rf[0:2]
     coarse[2:14] = inner[2:14]
     coarse[14:16] = inner[14:16] + rf[2:4]
@@ -364,101 +368,80 @@
         kpairs[j] = pair_rows(reactions[2 * j + 2] + reactions[2 * j + 3])
     halve = pair_matrix_halves()
     _, inside = masks_of(24, 8, 16, 32)
-    rf = exact_dot(compact(range(3), pairs, 24), halve).reshape(3, 24, LANES)
+    both = jnp.concatenate([compact(range(3), pairs, 24), compact(range(3), kpairs, 24)], axis=0)
+    both = paired(both, halve).reshape(6, 24, LANES)
     for j in range(3):
-        f2[j] = rf[j] * inside
-    k2[...] = exact_dot(compact(range(3), kpairs, 24), halve).reshape(3, 24, LANES)
+        f2[j] = both[j] * inside
+    k2[...] = both[3:6]
 
 
 def coarse_outer(
-    x_before, x_after, f_in, k_in, e_in, f2_in, k2_in, e1, e2, e3, f4, k4,
-    f, k, e, pairs, kpairs,
+    x_before, x_after, f_in, k_in, e_in, f2_in, k2_in, own1, own2, own3, f4, k4,
+    pairs, kpairs,
 ):
     outside, inside = masks_of(48, 16, 32, 64)
     low = low_half((48, LANES))
-
-    def take(j):
-        out = []
-        for i in range(2):
-            lo, hi = x_before[j + i], x_after[13 - j - i]
-            out.append((jnp.where(low, lo, swap(hi)) * outside, jnp.where(low, swap(lo), hi)))
-        for i in range(2):
-            f[j + i], k[j + i] = out[i]
-
-    loop(0, 14, 2, take)
-    for j in (0, 1):
-        f[14 + j] = f_in[j]
-        k[14 + j] = k_in[j]
-
-    def one(j):
-        out = corrections(
-            1,
-            [f[j + i] for i in range(-1, 4)],
-            [k[j + i] for i in range(3)],
-            [outside] * 3,
-            blur_z_halves,
-        )
-        for i in range(3):
-            e[j + i] = out[i]
-
-    loop(1, 13, 3, one)
-    value = corrections(1, [f[j] for j in range(12, 16)], [k[13], k[14]], [outside, inside], blur_z_halves)
-    e[13], e[14] = value
-    e[15] = e_in[1]
-    e[16] = e_in[2]
-
-    def two(j):
-        out = coarse_remainders(
-            [e[j + i] for i in range(-1, 3)],
-            [f[j + i] for i in range(2)],
-            [k[j + i] for i in range(2)],
-            blur_z_halves,
-        )
-        p = (j - 2) // 2
-        pairs[p] = pair_rows(out[0] + out[1])
-        kpairs[p] = pair_rows(k[j] + k[j + 1])
-
-    loop(2, 16, 2, two)
-    half = slice(16, 32)
-    e1[0] = e[14, half, 0:64]
-    e1[15] = swap(e[14, half, :])[:, 0:64]
+    halve = pair_matrix_halves()
+
+    def both(fields, reactions, rows):
+        values = [compact(range(fields), pairs, rows), compact(range(reactions), kpairs, rows)]
+        out = paired(jnp.concatenate(values, axis=0), halve).reshape(fields + reactions, rows, LANES)
+        return [out[i] for i in range(fields)], [out[fields + i] for i in range(reactions)]
+
+    fields, reactions = [], []
+    for j in range(FAR):
+        lo, hi = x_before[j], x_after[FAR - 1 - j]
+        fields.append(jnp.where(low, lo, swap(hi)) * outside)
+        reactions.append(jnp.where(low, swap(lo), hi))
+    for j in range(2):
+        fields.append(f_in[j])
+        reactions.append(k_in[j])
+    for j in range(7):
+        kpairs[j] = pair_rows(reactions[2 * j + 2] + reactions[2 * j + 3])
+    value = corrections(1, fields, reactions[1:15], [outside] * 13 + [inside], blur_z_halves)
+    own1[0] = value[13][16:32]
     for j in range(1, 8):
-        value = e_in[j, half, :]
-        e1[j] = value[:, 0:64]
-        e1[15 - j] = swap(value)[:, 0:64]
-    halve = pair_matrix_halves()
-    rf = exact_dot(compact(range(7), pairs, 24), halve).reshape(7, 24, LANES)
-    rk = exact_dot(compact(range(7), kpairs, 24), halve).reshape(7, 24, LANES)
+        own1[j] = e_in[j, 16:32, :]
+    rest = coarse_remainders(value + [e_in[1], e_in[2]], fields[2:], reactions[2:], blur_z_halves)
+    for j in range(7):
+        pairs[j] = pair_rows(rest[2 * j] + rest[2 * j + 1])
+    rf, rk = both(7, 7, 24)
     outside, inside = masks_of(24, 8, 16, 32)
     fields = [rf[j] * (outside if j < 6 else inside) for j in range(7)] + [f2_in[j] for j in range(3)]
-    reactions = [rk[j] for j in range(7)] + [k2_in[j] for j in range(3)]
+    reactions = rk + [k2_in[j] for j in range(3)]
+    for p in range(4):
+        kpairs[p, 0:24, :] = pair_rows(reactions[2 * p + 2] + reactions[2 * p + 3])
     value = corrections(
         2, fields + [swap(fields[9])], reactions[1:], [outside] * 5 + [inside] * 4, blur_z_part
     )
     for j in range(4):
-        own = value[5 + j][8:16]
-        e2[j] = own[:, 0:32]
-        e2[7 - j] = swap(own)[:, 0:32]
+        own2[j] = value[5 + j][8:16]
     rest = coarse_remainders(value + [swap(value[8])], fields[2:], reactions[2:], blur_z_part)
     for p in range(4):
         pairs[p, 0:24, :] = pair_rows(rest[2 * p] + rest[2 * p + 1])
-        kpairs[p, 0:24, :] = pair_rows(reactions[2 * p + 2] + reactions[2 * p + 3])
-    rf = exact_dot(compact(range(4), pairs, 16), halve).reshape(4, 16, LANES)
-    rk = exact_dot(compact(range(4), kpairs, 16), halve).reshape(4, 16, LANES)
+    rf, rk = both(4, 4, 16)
     outside, inside = masks_of(16, 4, 8, 16)
     fields = [rf[0] * outside, rf[1] * outside, rf[2] * inside, rf[3] * inside]
-    reactions = [rk[j] for j in range(4)]
-    value = corrections(3, fields + [swap(fields[3])], reactions[1:], [outside, inside, inside], blur_z_part)
+    for p in range(2):
+        kpairs[p, 0:16, :] = pair_rows(rk[2 * p] + rk[2 * p + 1])
+    value = corrections(3, fields + [swap(fields[3])], rk[1:], [outside, inside, inside], blur_z_part)
     for j in range(2):
-        own = value[1 + j][0:8]
-        e3[j] = own[4:8, 0:16]
-        e3[3 - j] = swap(own)[4:8, 0:16]
-    rest = coarse_remainders(value + [swap(value[2])], fields[2:], reactions[2:], blur_z_part)
+        own3[j] = value[1 + j][0:8]
+    rest = coarse_remainders(value + [swap(value[2])], fields[2:], rk[2:], blur_z_part)
     pairs[0, 0:16, :] = pair_rows(rest[0] + rest[1])
-    for p in range(2):
-        kpairs[p, 0:16, :] = pair_rows(reactions[2 * p] + reactions[2 * p + 1])
-    f4[...] = exact_dot(compact(range(1), pairs, 8), halve)
-    k4[...] = exact_dot(compact(range(2), kpairs, 8), halve).reshape(2, 8, LANES)
+    rf, rk = both(1, 2, 8)
+    f4[...] = rf[0]
+    k4[0] = rk[0]
+    k4[1] = rk[1]
+
+
+def unfold(own1, own2, own3, e1, e2, e3):
+    for own, out, rows in ((own1, e1, slice(0, 16)), (own2, e2, slice(0, 8)), (own3, e3, slice(4, 8))):
+        planes, _, lanes = out.shape
+        for j in range(planes // 2):
+            value = own[j]
+            out[j] = value[rows, 0:lanes]
+            out[planes - 1 - j] = swap(value)[rows, 0:lanes]
 
 
 def pack_last(y_before, own, y_after, out):
@@ -515,6 +498,9 @@
 
 def per_device(source, guess, reaction, flags):
     tile = (32, 8, LANES)
+    flags, guess, source, reaction = (
+        pltpu.with_memory_space_constraint(v, pltpu.HBM) for v in (flags, guess, source, reaction)
+    )
     own, down, strip_up, strip_down = call(
         pack_rows,
         [tile, tile, (7, 32, LANES), (7, 32, LANES)],
@@ -558,13 +544,16 @@
         flops=4000000,
         name="coarse_inner",
     )(y_before, coarse, y_after)
-    e1, e2, e3, f4, k4 = call(
+    *owns, f4, k4 = call(
         coarse_outer,
-        [(16, 16, 64), (8, 8, 32), (4, 4, 16), (8, LANES), (2, 8, LANES)],
+        [(8, 16, LANES), (4, 8, LANES), (2, 8, LANES), (8, LANES), (2, 8, LANES)],
         [VMEM] * 7,
-        scratch=[(16,) + plane] * 2 + [(17,) + plane] + [(7,) + plane] * 2,
+        scratch=[(7,) + plane] * 2,
         name="coarse_outer",
     )(x_before, x_after, *inner)
+    e1, e2, e3 = call(
+        unfold, [(16, 16, 64), (8, 8, 32), (4, 4, 16)], [VMEM] * 3, flops=2000000, name="unfold"
+    )(*owns)
     y_before, y_after = neighbours_of(f4, f4, "agg")
     (last,) = call(pack_last, [(8, LANES)], [VMEM] * 3, name="pack_last")(y_before, f4, y_after)
     x_before, x_after = neighbours_of(last, last, "box")

time: 59.6 us -> 52.5 us (0.88)
  local copies, waits for them, and re-layouts: 3.92 us -> 0.13 us
  Pallas kernels: 12.8 us -> 9.84 us
  starting transfers between devices: 23 us -> 22 us
  waiting for transfers between devices: 17.9 us -> 18.7 us
    unnamed x16 -> x2, local copies, waits for them, and re-layouts: 3.81 us -> 0.02 us
    pallas_call x1 -> x2, Pallas kernels: 4.83 us -> 2.72 us  [the longest x1 1.98 us: per_device(): call(coarse_outer, [(8, 16, LANES), (4, 8, LANES), (2, 8, LANES), (8, LAN...]
    pallas_call x1, Pallas kernels: 4.66 us -> 3.21 us  [per_device(): call(fine_inner, [big] * 6 + [(16, 16, LANES)], [VMEM] * 3 + [HBM] * 3, s...]
    ppermute x12, starting transfers between devices: 23 us -> 22 us  [neighbours_of(): return (lax.ppermute(up, axis, ahead), lax.ppermute(down, axis, back))]
    ppermute x12, waiting for transfers between devices: 17.9 us -> 18.7 us  [neighbours_of(): return (lax.ppermute(up, axis, ahead), lax.ppermute(down, axis, back))]
    pallas_call x1, Pallas kernels: 0.72 us -> 1.39 us  [per_device(): call(pack_rows, [tile, tile, (7, 32, LANES), (7, 32, LANES)], [HBM] * 4,...]
where the time goes in v4:
time: 52.5 us; the launch traced here: 52.2 us
  starting transfers between devices  22 us (42%)
  waiting for transfers between devices  18.7 us (36%)
  Pallas kernels  9.84 us (19%)
  other arithmetic  0.83 us (2%)
  between operations  0.73 us (1%)
    ppermute x12, starting transfers between devices, neighbours_of(): return (lax.ppermute(up, axis, ahead), lax.ppermute(down, axis, back))  22 us
    ppermute x12, waiting for transfers between devices, neighbours_of(): return (lax.ppermute(up, axis, ahead), lax.ppermute(down, axis, back))  18.7 us
    pallas_call x1, Pallas kernels, per_device(): call(fine_inner, [big] * 6 + [(16, 16, LANES)], [VMEM] * 3 + [HBM] * 3, s...  3.21 us
    pallas_call x1, Pallas kernels, per_device(): call(coarse_outer, [(8, 16, LANES), (4, 8, LANES), (2, 8, LANES), (8, LAN...  1.98 us
    pallas_call x1, Pallas kernels, per_device(): call(pack_rows, [tile, tile, (7, 32, LANES), (7, 32, LANES)], [HBM] * 4,...  1.39 us
    pallas_call x1, Pallas kernels, per_device(): call(last_kernel, [(2, 2, 8), (2, 2, 8)], [VMEM] * 4, name='last')  1.08 us
  transfers between devices with their start and end apart: 12, of which 7 were waited for; matrix products, arithmetic and copies ran while one was open for 2% of the time, Pallas kernels for 9%

profile of v4, /device:TPU:97, one launch (start us, length us, event | category | flops | bytes accessed | tf_op | source)
XLA Modules:
  0.0 52.2 jit_solution(7117689679519312003)
XLA Ops:
  0.6 1.4 %pack_rows.1 = (f32[32,8,128]{2,1,0:T(8,128)S(1)}, f32[32,8,128]{2,1,0:T(8,128)S(1)}, f32[7,32,128]{2,1,0:T(8,128)S(1)}, f32[7,32,128]{2,1,0:T(8,128)S(1)}) custom-call(s32[1,1,4]{2,1,0:T(1,128)} %flags.1, f32[32,32,128]{2,1,0:T(8,128)} %guess.3, f32[32,32,128]{2,1,0:T(8,128)} %source.3, f32[32,32,128]{2,1,0:T(8,128)} %reaction.3), custom_call_target="tpu_custom_call" | custom-call | tf_op jit(solution)/shard_map/pack_rows/pallas_call | solution.py:504
  2.0 1.3 %collective-permute-start = (f32[32,8,128]{2,1,0:T(8,128)S(1)}, f32[32,8,128]{2,1,0:T(8,128)S(1)}, u32[]{:S(2)}, u32[]{:S(2)}) collective-permute-start(f32[32,8,128]{2,1,0:T(8,128)S(1)} %get-tuple-element.36.own), channel_id=1, source_target_pairs={{0,1},{1,2},{2,3},{3,4},{4,5},{5,6},{6,7},{7,8},{8,9},{9,10},{10,1... | collective-permute-start | bytes 393224 | tf_op jit(solution)/shard_map/ppermute | solution.py:478
  3.3 3.8 %collective-permute-start.1 = (f32[32,8,128]{2,1,0:T(8,128)S(1)}, f32[32,8,128]{2,1,0:T(8,128)S(1)}, u32[]{:S(2)}, u32[]{:S(2)}) collective-permute-start(f32[32,8,128]{2,1,0:T(8,128)S(1)} %get-tuple-element.37), channel_id=1, source_target_pairs={{0,15},{1,0},{2,1},{3,2},{4,3},{5,4},{6,5},{7,6},{8,7},{9,8},{10,9... | collective-permute-start | bytes 393224 | tf_op jit(solution)/shard_map/ppermute | solution.py:478
  7.1 3.0 %collective-permute-done.from_before = f32[32,8,128]{2,1,0:T(8,128)S(1)} collective-permute-done((f32[32,8,128]{2,1,0:T(8,128)S(1)}, f32[32,8,128]{2,1,0:T(8,128)S(1)}, u32[]{:S(2)}, u32[]{:S(2)}) %collective-permute-start) | collective-permute-done | bytes 131104 | tf_op jit(solution)/shard_map/ppermute | solution.py:478
  10.1 0.0 collective-permute-done.1.from_after
  10.1 4.1 %collective-permute-start.2 = (f32[8,40,128]{2,1,0:T(8,128)S(1)}, f32[8,40,128]{2,1,0:T(8,128)S(1)}, u32[]{:S(2)}, u32[]{:S(2)}) collective-permute-start(f32[8,40,128]{2,1,0:T(8,128)S(1)} %get-tuple-element.40.packed), channel_id=1, source_target_pairs={{0,16},{16,32},{32,48},{48,64},{64,80},{80,96},{96,112},{112,128},... | collective-permute-start | bytes 491528 | tf_op jit(solution)/shard_map/ppermute | solution.py:478
  14.3 0.0 collective-permute-start.3
  14.3 3.2 %fine_inner.1 = (f32[32,40,128]{2,1,0:T(8,128)S(1)}, f32[32,40,128]{2,1,0:T(8,128)S(1)}, f32[32,40,128]{2,1,0:T(8,128)S(1)}, f32[32,40,128]{2,1,0:T(8,128)S(1)},...) custom-call(f32[8,40,128]{2,1,0:T(8,128)S(1)} %get-tuple-element.40.packed, ...), custom_call_target="tpu_custom_call" | custom-call | flops 8000000 | bytes 8000000 | tf_op jit(solution)/shard_map/fine_inner/pallas_call | solution.py:518
  17.5 0.0 collective-permute-done.2.x_before
  17.5 2.7 %collective-permute-done.3.x_after = f32[8,40,128]{2,1,0:T(8,128)S(1)} collective-permute-done((f32[8,40,128]{2,1,0:T(8,128)S(1)}, f32[8,40,128]{2,1,0:T(8,128)S(1)}, u32[]{:S(2)}, u32[]{:S(2)}) %collective-permute-start.3) | collective-permute-done | bytes 163872 | tf_op jit(solution)/shard_map/ppermute | solution.py:478
  20.2 0.7 %fine_outer.1 = (f32[16,16,128]{2,1,0:T(8,128)S(1)}, f32[4,32,128]{2,1,0:T(8,128)S(1)}) custom-call(f32[8,40,128]{2,1,0:T(8,128)S(1)} %get-tuple-element.40.packed, f32[8,40,128]{2,1,0:T(8,128)S(1)} %collective-permute-done.2.x_before, f32[8,40,128]{2,1,0:T(8,128)S(1)} %collective-permute-done.3.x_after, f32[32,40,128]{2,1,0:T(8,128)S(1)} %get-tuple-element.42.g, ...), custom_call_target="tpu_custom_call" | custom-call | tf_op jit(solution)/shard_map/fine_outer/pallas_call | solution.py:527
  20.9 0.1 collective-permute-start.4
  21.0 4.9 %collective-permute-start.5 = (f32[16,16,128]{2,1,0:T(8,128)S(1)}, f32[16,16,128]{2,1,0:T(8,128)S(1)}, u32[]{:S(2)}, u32[]{:S(2)}) collective-permute-start(f32[16,16,128]{2,1,0:T(8,128)S(1)} %get-tuple-element.50.own), channel_id=1, source_target_pairs={{0,15},{1,0},{2,1},{3,2},{4,3},{5,4},{6,5},{7,6},{8,7},{9,8},{10,9... | collective-permute-start | bytes 393224 | tf_op jit(solution)/shard_map/ppermute | solution.py:478
  25.9 2.3 %collective-permute-done.4.y_before = f32[16,16,128]{2,1,0:T(8,128)S(1)} collective-permute-done((f32[16,16,128]{2,1,0:T(8,128)S(1)}, f32[16,16,128]{2,1,0:T(8,128)S(1)}, u32[]{:S(2)}, u32[]{:S(2)}) %collective-permute-start.4) | collective-permute-done | bytes 131104 | tf_op jit(solution)/shard_map/ppermute | solution.py:478
  28.2 0.0 collective-permute-done.5.y_after
  28.3 1.7 %collective-permute-start.6 = (f32[14,48,128]{2,1,0:T(8,128)S(1)}, f32[14,48,128]{2,1,0:T(8,128)S(1)}, u32[]{:S(2)}, u32[]{:S(2)}) collective-permute-start(f32[14,48,128]{2,1,0:T(8,128)S(1)} %get-tuple-element.67), channel_id=1, source_target_pairs={{0,16},{16,32},{32,48},{48,64},{64,80},{80,96},{96,112},{112,128},... | collective-permute-start | bytes 1032200 | tf_op jit(solution)/shard_map/ppermute | solution.py:478
  30.0 0.0 collective-permute-start.7
  30.1 0.7 %coarse_inner.1 = (f32[8,48,128]{2,1,0:T(8,128)S(1)}, f32[8,48,128]{2,1,0:T(8,128)S(1)}, f32[8,48,128]{2,1,0:T(8,128)S(1)}, f32[3,24,128]{2,1,0:T(8,128)S(1)}, f32[3,24,128]{2,1,0:T(8,128)S(1)}) custom-call(f32[16,16,128]{2,1,0:T(8,128)S(1)} %collective-permute-done.4.y_before, f32[16,16,128]{2,1,0:T(8,128)S(1)} %get-tuple-element.50.own, ...), custom_call_target="tpu_custom_call" | custom-call | flops 4000000 | bytes 4000000 | tf_op jit(solution)/shard_map/coarse_inner/pallas_call | solution.py:539
  30.8 3.4 %collective-permute-done.6.x_before = f32[14,48,128]{2,1,0:T(8,128)S(1)} collective-permute-done((f32[14,48,128]{2,1,0:T(8,128)S(1)}, f32[14,48,128]{2,1,0:T(8,128)S(1)}, u32[]{:S(2)}, u32[]{:S(2)}) %collective-permute-start.6) | collective-permute-done | bytes 344096 | tf_op jit(solution)/shard_map/ppermute | solution.py:478
  34.2 3.7 %collective-permute-done.7.x_after = f32[14,48,128]{2,1,0:T(8,128)S(1)} collective-permute-done((f32[14,48,128]{2,1,0:T(8,128)S(1)}, f32[14,48,128]{2,1,0:T(8,128)S(1)}, u32[]{:S(2)}, u32[]{:S(2)}) %collective-permute-start.7) | collective-permute-done | bytes 344096 | tf_op jit(solution)/shard_map/ppermute | solution.py:478
  37.9 2.0 %coarse_outer.1 = (f32[8,16,128]{2,1,0:T(8,128)S(1)}, f32[4,8,128]{2,1,0:T(8,128)S(1)}, f32[2,8,128]{2,1,0:T(8,128)S(1)}, f32[8,128]{1,0:T(8,128)S(1)}, f32[2,8,128]{2,1,0:T(8,128)S(1)}) custom-call(f32[14,48,128]{2,1,0:T(8,128)S(1)} %collective-permute-done.6.x_before, f32[14,48,128]{2,1,0:T(8,128)S(1)} %collective-permute-done.7.x_after, ...), custom_call_target="tpu_custom_call" | custom-call | tf_op jit(solution)/shard_map/coarse_outer/pallas_call | solution.py:547
  39.9 0.0 collective-permute-start.8
  39.9 4.9 %collective-permute-start.9 = (f32[8,128]{1,0:T(8,128)S(1)}, f32[8,128]{1,0:T(8,128)S(1)}, u32[]{:S(2)}, u32[]{:S(2)}) collective-permute-start(f32[8,128]{1,0:T(8,128)S(1)} %get-tuple-element.62.own), channel_id=1, source_target_pairs={{0,15},{1,0},{2,1},{3,2},{4,3},{5,4},{6,5},{7,6},{8,7},{9,8},{10,9... | collective-permute-start | bytes 12296 | tf_op jit(solution)/shard_map/ppermute | solution.py:478
  44.8 0.9 %collective-permute-done.8.y_before = f32[8,128]{1,0:T(8,128)S(1)} collective-permute-done((f32[8,128]{1,0:T(8,128)S(1)}, f32[8,128]{1,0:T(8,128)S(1)}, u32[]{:S(2)}, u32[]{:S(2)}) %collective-permute-start.8) | collective-permute-done | bytes 4128 | tf_op jit(solution)/shard_map/ppermute | solution.py:478
  45.7 0.0 collective-permute-done.9.y_after
  45.8 1.1 %collective-permute-start.10 = (f32[8,128]{1,0:T(8,128)S(1)}, f32[8,128]{1,0:T(8,128)S(1)}, u32[]{:S(2)}, u32[]{:S(2)}) collective-permute-start(f32[8,128]{1,0:T(8,128)S(1)} %pack_last.1.own), channel_id=1, source_target_pairs={{0,16},{16,32},{32,48},{48,64},{64,80},{80,96},{96,112},{112,128},... | collective-permute-start | bytes 12296 | tf_op jit(solution)/shard_map/ppermute | solution.py:478
  46.9 0.0 collective-permute-start.11
  46.9 0.8 %pad_maximum_fusion = f32[32,32,128]{2,1,0:T(8,128)} fusion(f32[2,32,128]{2,1,0:T(8,128)S(1)} %get-tuple-element.69, f32[28,32,128]{2,1,0:T(8,128)S(1)} %slice.16, f32[2,32,128]{2,1,0:T(8,128)S(1)} %get-tuple-element.68), kind=kLoop, calls=%fused_computation | loop fusion | flops 262144 | bytes 1048576 | tf_op jit(solution)/shard_map/concatenate | solution.py:534
  47.7 0.7 %unfold.1 = (f32[16,16,64]{2,1,0:T(8,128)}, f32[8,8,32]{2,1,0:T(8,128)}, f32[4,4,16]{2,1,0:T(4,128)}) custom-call(f32[8,16,128]{2,1,0:T(8,128)S(1)} %get-tuple-element.56.own1, f32[4,8,128]{2,1,0:T(8,128)S(1)} %get-tuple-element.57.own2, f32[2,8,128]{2,1,0:T(8,128)S(1)} %get-tuple-element.58.own3), custom_call_target="tpu_custom_call" | custom-call | flops 2000000 | bytes 2000000 | tf_op jit(solution)/shard_map/unfold/pallas_call | solution.py:554
  48.5 0.0 collective-permute-done.10.x_before
  48.5 2.7 %collective-permute-done.11.x_after = f32[8,128]{1,0:T(8,128)S(1)} collective-permute-done((f32[8,128]{1,0:T(8,128)S(1)}, f32[8,128]{1,0:T(8,128)S(1)}, u32[]{:S(2)}, u32[]{:S(2)}) %collective-permute-start.11) | collective-permute-done | bytes 4128 | tf_op jit(solution)/shard_map/ppermute | solution.py:478
  51.1 1.1 %last.1 = (f32[2,2,8]{2,1,0:T(2,128)}, f32[2,2,8]{2,1,0:T(2,128)}) custom-call(f32[8,128]{1,0:T(8,128)S(1)} %pack_last.1.own, f32[8,128]{1,0:T(8,128)S(1)} %collective-permute-done.10.x_before, f32[8,128]{1,0:T(8,128)S(1)} %collective-permute-done.11.x_after, f32[2,8,128]{2,1,0:T(8,128)S(1)} %get-tuple-element.63.k4), custom_call_target="tpu_custom_call" | custom-call | tf_op jit(solution)/shard_map/last/pallas_call | solution.py:560
  (8 shorter events, 0.2 us)
Async XLA Ops:
  2.0 8.1 %collective-permute-start = (f32[32,8,128]{2,1,0:T(8,128)S(1)}, f32[32,8,128]{2,1,0:T(8,128)S(1)}, u32[]{:S(2)}, u32[]{:S(2)}) collective-permute-start(f32[32,8,128]{2,1,0:T(8,128)S(1)} %get-tuple-element.36.own), channel_id=1, source_target_pairs={{0,1},{1,2},{2,3},{3,4},{4,5},{5,6},{6,7},{7,8},{8,9},{9,10},{10,1... | collective-permute-start | bytes 393224 | tf_op jit(solution)/shard_map/ppermute | solution.py:478
  3.3 6.8 %collective-permute-start.1 = (f32[32,8,128]{2,1,0:T(8,128)S(1)}, f32[32,8,128]{2,1,0:T(8,128)S(1)}, u32[]{:S(2)}, u32[]{:S(2)}) collective-permute-start(f32[32,8,128]{2,1,0:T(8,128)S(1)} %get-tuple-element.37), channel_id=1, source_target_pairs={{0,15},{1,0},{2,1},{3,2},{4,3},{5,4},{6,5},{7,6},{8,7},{9,8},{10,9... | collective-permute-start | bytes 393224 | tf_op jit(solution)/shard_map/ppermute | solution.py:478
  10.1 7.4 %collective-permute-start.2 = (f32[8,40,128]{2,1,0:T(8,128)S(1)}, f32[8,40,128]{2,1,0:T(8,128)S(1)}, u32[]{:S(2)}, u32[]{:S(2)}) collective-permute-start(f32[8,40,128]{2,1,0:T(8,128)S(1)} %get-tuple-element.40.packed), channel_id=1, source_target_pairs={{0,16},{16,32},{32,48},{48,64},{64,80},{80,96},{96,112},{112,128},... | collective-permute-start | bytes 491528 | tf_op jit(solution)/shard_map/ppermute | solution.py:478
  14.3 6.0 %collective-permute-start.3 = (f32[8,40,128]{2,1,0:T(8,128)S(1)}, f32[8,40,128]{2,1,0:T(8,128)S(1)}, u32[]{:S(2)}, u32[]{:S(2)}) collective-permute-start(f32[8,40,128]{2,1,0:T(8,128)S(1)} %get-tuple-element.41), channel_id=1, source_target_pairs={{0,240},{16,0},{32,16},{48,32},{64,48},{80,64},{96,80},{112,96},{1... | collective-permute-start | bytes 491528 | tf_op jit(solution)/shard_map/ppermute | solution.py:478
  20.9 7.3 %collective-permute-start.4 = (f32[16,16,128]{2,1,0:T(8,128)S(1)}, f32[16,16,128]{2,1,0:T(8,128)S(1)}, u32[]{:S(2)}, u32[]{:S(2)}) collective-permute-start(f32[16,16,128]{2,1,0:T(8,128)S(1)} %get-tuple-element.50.own), channel_id=1, source_target_pairs={{0,1},{1,2},{2,3},{3,4},{4,5},{5,6},{6,7},{7,8},{8,9},{9,10},{10,1... | collective-permute-start | bytes 393224 | tf_op jit(solution)/shard_map/ppermute | solution.py:478
  21.0 7.2 %collective-permute-start.5 = (f32[16,16,128]{2,1,0:T(8,128)S(1)}, f32[16,16,128]{2,1,0:T(8,128)S(1)}, u32[]{:S(2)}, u32[]{:S(2)}) collective-permute-start(f32[16,16,128]{2,1,0:T(8,128)S(1)} %get-tuple-element.50.own), channel_id=1, source_target_pairs={{0,15},{1,0},{2,1},{3,2},{4,3},{5,4},{6,5},{7,6},{8,7},{9,8},{10,9... | collective-permute-start | bytes 393224 | tf_op jit(solution)/shard_map/ppermute | solution.py:478
  28.3 5.9 %collective-permute-start.6 = (f32[14,48,128]{2,1,0:T(8,128)S(1)}, f32[14,48,128]{2,1,0:T(8,128)S(1)}, u32[]{:S(2)}, u32[]{:S(2)}) collective-permute-start(f32[14,48,128]{2,1,0:T(8,128)S(1)} %get-tuple-element.67), channel_id=1, source_target_pairs={{0,16},{16,32},{32,48},{48,64},{64,80},{80,96},{96,112},{112,128},... | collective-permute-start | bytes 1032200 | tf_op jit(solution)/shard_map/ppermute | solution.py:478
  30.0 7.9 %collective-permute-start.7 = (f32[14,48,128]{2,1,0:T(8,128)S(1)}, f32[14,48,128]{2,1,0:T(8,128)S(1)}, u32[]{:S(2)}, u32[]{:S(2)}) collective-permute-start(f32[14,48,128]{2,1,0:T(8,128)S(1)} %get-tuple-element.66), channel_id=1, source_target_pairs={{0,240},{16,0},{32,16},{48,32},{64,48},{80,64},{96,80},{112,96},{1... | collective-permute-start | bytes 1032200 | tf_op jit(solution)/shard_map/ppermute | solution.py:478
  39.9 5.8 %collective-permute-start.8 = (f32[8,128]{1,0:T(8,128)S(1)}, f32[8,128]{1,0:T(8,128)S(1)}, u32[]{:S(2)}, u32[]{:S(2)}) collective-permute-start(f32[8,128]{1,0:T(8,128)S(1)} %get-tuple-element.62.own), channel_id=1, source_target_pairs={{0,1},{1,2},{2,3},{3,4},{4,5},{5,6},{6,7},{7,8},{8,9},{9,10},{10,1... | collective-permute-start | bytes 12296 | tf_op jit(solution)/shard_map/ppermute | solution.py:478
  39.9 5.8 %collective-permute-start.9 = (f32[8,128]{1,0:T(8,128)S(1)}, f32[8,128]{1,0:T(8,128)S(1)}, u32[]{:S(2)}, u32[]{:S(2)}) collective-permute-start(f32[8,128]{1,0:T(8,128)S(1)} %get-tuple-element.62.own), channel_id=1, source_target_pairs={{0,15},{1,0},{2,1},{3,2},{4,3},{5,4},{6,5},{7,6},{8,7},{9,8},{10,9... | collective-permute-start | bytes 12296 | tf_op jit(solution)/shard_map/ppermute | solution.py:478
  45.8 2.7 %collective-permute-start.10 = (f32[8,128]{1,0:T(8,128)S(1)}, f32[8,128]{1,0:T(8,128)S(1)}, u32[]{:S(2)}, u32[]{:S(2)}) collective-permute-start(f32[8,128]{1,0:T(8,128)S(1)} %pack_last.1.own), channel_id=1, source_target_pairs={{0,16},{16,32},{32,48},{48,64},{64,80},{80,96},{96,112},{112,128},... | collective-permute-start | bytes 12296 | tf_op jit(solution)/shard_map/ppermute | solution.py:478
  46.9 4.2 %collective-permute-start.11 = (f32[8,128]{1,0:T(8,128)S(1)}, f32[8,128]{1,0:T(8,128)S(1)}, u32[]{:S(2)}, u32[]{:S(2)}) collective-permute-start(f32[8,128]{1,0:T(8,128)S(1)} %pack_last.1.own), channel_id=1, source_target_pairs={{0,240},{16,0},{32,16},{48,32},{64,48},{80,64},{96,80},{112,96},{1... | collective-permute-start | bytes 12296 | tf_op jit(solution)/shard_map/ppermute | solution.py:478

commit v5 on v4

--- a/solution.py
+++ b/solution.py
@@ -34,54 +34,33 @@
     return before, after
 
 
-def blurred(planes, blur_z):
+def blurred(planes, stride):
     sums = [a + b for a, b in zip(planes[:-1], planes[1:])]
     out = []
     for low, high in zip(sums[:-1], sums[1:]):
         total = low + high
-        part = total + pltpu.roll(total, 1, 0)
-        out.append(blur_z(part + pltpu.roll(part, part.shape[0] - 1, 0)))
+        beside = pltpu.roll(total, 1, 0) + pltpu.roll(total, total.shape[0] - 1, 0)
+        out.append(blur_z((total + total) + beside, stride))
     return out
 
 
-def blur_z_full(values):
+def blur_z(values, stride):
     lane = iota(values.shape, 1)
-    part = values + jnp.where(lane == 0, 0.0, pltpu.roll(values, 1, 1))
-    return part + jnp.where(lane == LANES - 1, values, pltpu.roll(part, LANES - 1, 1))
-
-
-def blur_z_halves(values):
-    lane = iota(values.shape, 1) & 63
-    part = values + jnp.where(lane == 0, 0.0, pltpu.roll(values, 1, 1))
-    return part + jnp.where(lane == 63, values, pltpu.roll(part, LANES - 1, 1))
-
-
-def blur_z_part(values):
-    part = values + pltpu.roll(values, 1, 1)
-    return part + pltpu.roll(part, LANES - 1, 1)
+    left = jnp.where(lane < stride, 0.0, pltpu.roll(values, stride, 1))
+    right = jnp.where(lane >= LANES - stride, 0.0, pltpu.roll(values, LANES - stride, 1))
+    return (values + values) + (left + right)
 
 
 def pair_rows(values):
     return values + pltpu.roll(values, values.shape[0] - 1, 0)
 
 
-def pair_matrix(first):
-    source = iota((2 * LANES, LANES), 0) & (LANES - 1)
-    target = iota((2 * LANES, LANES), 1)
-    return jnp.where((source >> 1) + first == target, 0.5, 0.0).astype(jnp.bfloat16)
-
-
-def pair_matrix_halves():
-    source = iota((2 * LANES, LANES), 0) & (LANES - 1)
-    target = iota((2 * LANES, LANES), 1)
-    hit = ((source & 64) == (target & 64)) & ((source & 63) >> 1 == (target & 63))
-    return jnp.where(hit, 0.5, 0.0).astype(jnp.bfloat16)
-
-
-def paired(values, matrix):
-    coarse = values.astype(jnp.bfloat16)
-    fine = (values - coarse.astype(F32)).astype(jnp.bfloat16)
-    return jnp.dot(jnp.concatenate([coarse, fine], axis=1), matrix, preferred_element_type=F32)
+def halved(values, stride):
+    return (values + pltpu.roll(values, LANES - stride, 1)) * 0.5
+
+
+def even_lanes(shape):
+    return (iota(shape, len(shape) - 1) & 1) == 0
 
 
 def loop(first, stop, size, body):
@@ -190,8 +169,8 @@
 SHIFT = 8.0 / 7.0
 
 
-def compact(values, ref, rows):
-    return jnp.concatenate([ref[i, pl.ds(0, rows, stride=2), :] for i in values], axis=0)
+def even_rows(ref, i, rows):
+    return ref[i, pl.ds(0, rows, stride=2), :]
 
 
 def fine_inner(
@@ -220,7 +199,7 @@
         planes = [field[x + i] for i in range(-1, size + 1)]
         mask = packed[7]
         out = []
-        for i, q in enumerate(blurred(planes, blur_z_full)):
+        for i, q in enumerate(blurred(planes, 1)):
             r = mask * (s[x + i] - (k[x + i] + SHIFT) * planes[i + 1] + q * (1.0 / 56.0))
             out.append((r, planes[i + 1]))
         return out
@@ -249,17 +228,14 @@
 
     loop(4, 28, 24, third)
 
-    def fourth(i):
-        out = [pair_rows(k[2 * i + 2 * j, 0:32, :] + k[2 * i + 2 * j + 1, 0:32, :]) for j in range(16)]
-        for j, value in enumerate(out):
-            kpairs[i + j] = value
-
-    loop(0, 16, 16, fourth)
-    rk = paired(compact(range(16), kpairs, 16), pair_matrix(64)).reshape(16, 16, LANES)
-    rf = paired(compact(range(12), pairs, 16), pair_matrix(0)).reshape(12, 16, LANES)
-    coarse[0:2] = rk[0:2]
-    coarse[2:14] = rk[2:14] + rf
-    coarse[14:16] = rk[14:16]
+    for i in range(16):
+        kpairs[i] = pair_rows(k[2 * i, 0:32, :] + k[2 * i + 1, 0:32, :])
+    even = even_lanes((16, LANES))
+    for i in range(16):
+        value = pltpu.roll(halved(even_rows(kpairs, i, 16), 1), 1, 1)
+        if 2 <= i < 14:
+            value = jnp.where(even, halved(even_rows(pairs, i - 2, 16), 1), value)
+        coarse[i] = value
 
 
 def fine_outer(packed, x_before, x_after, g, s, k, d, u, w, inner, coarse, edge, pairs):
@@ -285,7 +261,7 @@
     def remainders(field, first, size):
         planes = [field(x) for x in range(first - 1, first + size + 1)]
         out = []
-        for i, q in enumerate(blurred(planes, blur_z_full)):
+        for i, q in enumerate(blurred(planes, 1)):
             x = first + i
             r = mask_at(x) * (source_at(x) - (reaction_at(x) + SHIFT) * planes[i + 1] + q * (1.0 / 56.0))
             out.append((x, r, planes[i + 1]))
@@ -305,10 +281,10 @@
         out = [r for _, r, _ in remainders(lambda i: new_w[i] if i in new_w else w[i], first, 4)]
         pairs[2 * at] = pair_rows(out[0] + out[1])
         pairs[2 * at + 1] = pair_rows(out[2] + out[3])
-    rf = paired(compact(range(4), pairs, 16), pair_matrix(0)).reshape(4, 16, LANES)
-    coarse[0:2] = inner[0:2] + rf[0:2]
+    even = even_lanes((16, LANES))
+    for at, x in enumerate((0, 1, 14, 15)):
+        coarse[x] = jnp.where(even, halved(even_rows(pairs, at, 16), 1), inner[x])
     coarse[2:14] = inner[2:14]
-    coarse[14:16] = inner[14:16] + rf[2:4]
 
 
 def level_constants(level):
@@ -316,132 +292,139 @@
     return (1.0 + c1) / theta + c2, c2 / theta
 
 
-def low_half(shape):
-    return iota(shape, len(shape) - 1) < 64
-
-
-def masks_of(rows, lo, hi, lanes):
+def masks_of(rows, lo, hi):
     before, after = edges("agg")
     xbefore, xafter = edges("box")
     shape = (rows, LANES)
     row = iota(shape, 0)
     inside = jnp.where(row < lo, before, jnp.where(row >= hi, after, 1.0))
-    inside = jnp.where((iota(shape, 1) & 63) < lanes, inside, 0.0)
-    return inside * jnp.where(low_half(shape), xbefore, xafter), inside
-
-
-def corrections(level, planes, reactions, masks, blur_z):
+    return inside * jnp.where(even_lanes(shape), xbefore, xafter), inside
+
+
+def corrections(level, planes, reactions, masks):
     alpha, beta = level_constants(level)
     return [
         m * (f * (alpha - beta * (k + SHIFT)) + q * (beta / 56.0))
-        for f, k, m, q in zip(planes[1:-1], reactions, masks, blurred(planes, blur_z))
+        for f, k, m, q in zip(planes[1:-1], reactions, masks, blurred(planes, 2**level))
     ]
 
 
-def coarse_remainders(planes, fields, reactions, blur_z):
+def coarse_remainders(level, planes, fields, reactions):
     return [
         f - (k + SHIFT) * e + q * (1.0 / 56.0)
-        for f, k, e, q in zip(fields, reactions, planes[1:-1], blurred(planes, blur_z))
+        for f, k, e, q in zip(fields, reactions, planes[1:-1], blurred(planes, 2**level))
     ]
 
 
+def to_left(values):
+    return pltpu.roll(values, LANES - 1, 1)
+
+
+def to_right(values):
+    return pltpu.roll(values, 1, 1)
+
+
 def swap(values):
-    return pltpu.roll(values, 64, 1)
+    return jnp.where(even_lanes(values.shape), to_left(values), to_right(values))
+
+
+def folded(lo, hi):
+    even = even_lanes(lo.shape)
+    return jnp.where(even, lo, to_right(hi)), jnp.where(even, to_left(lo), hi)
 
 
 def coarse_inner(y_before, own, y_after, f, k, e, f2, k2, pairs, kpairs):
-    _, inside = masks_of(48, 16, 32, 64)
-    low = low_half((48, LANES))
+    _, inside = masks_of(48, 16, 32)
+    fields, reactions = [], []
     for j in range(8):
         lo = jnp.concatenate([y_before[j], own[j], y_after[j]], axis=0)
         hi = jnp.concatenate([y_before[15 - j], own[15 - j], y_after[15 - j]], axis=0)
-        f[j] = jnp.where(low, lo, swap(hi)) * inside
-        k[j] = jnp.where(low, swap(lo), hi)
-    fields = [f[j] for j in range(8)]
-    reactions = [k[j] for j in range(8)]
-    value = corrections(1, fields + [swap(fields[7])], reactions[1:], [inside] * 7, blur_z_halves)
+        field, reaction = folded(lo, hi)
+        fields.append(field * inside)
+        reactions.append(reaction)
+    for j in range(2):
+        f[j], k[j] = fields[j], reactions[j]
+    for j in range(3):
+        kpairs[j] = pair_rows(reactions[2 * j + 2] + reactions[2 * j + 3])
+    value = corrections(1, fields + [swap(fields[7])], reactions[1:], [inside] * 7)
     for j in range(7):
         e[j + 1] = value[j]
-    rest = coarse_remainders(value + [swap(value[6])], fields[2:], reactions[2:], blur_z_halves)
+    rest = coarse_remainders(1, value + [swap(value[6])], fields[2:], reactions[2:])
     for j in range(3):
         pairs[j] = pair_rows(rest[2 * j] + rest[2 * j + 1])
-        kpairs[j] = pair_rows(reactions[2 * j + 2] + reactions[2 * j + 3])
-    halve = pair_matrix_halves()
-    _, inside = masks_of(24, 8, 16, 32)
-    both = jnp.concatenate([compact(range(3), pairs, 24), compact(range(3), kpairs, 24)], axis=0)
-    both = paired(both, halve).reshape(6, 24, LANES)
+    _, inside = masks_of(24, 8, 16)
     for j in range(3):
-        f2[j] = both[j] * inside
-    k2[...] = both[3:6]
+        f2[j] = halved(even_rows(pairs, j, 24), 2) * inside
+        k2[j] = halved(even_rows(kpairs, j, 24), 2)
 
 
 def coarse_outer(
     x_before, x_after, f_in, k_in, e_in, f2_in, k2_in, own1, own2, own3, f4, k4,
     pairs, kpairs,
 ):
-    outside, inside = masks_of(48, 16, 32, 64)
-    low = low_half((48, LANES))
-    halve = pair_matrix_halves()
-
-    def both(fields, reactions, rows):
-        values = [compact(range(fields), pairs, rows), compact(range(reactions), kpairs, rows)]
-        out = paired(jnp.concatenate(values, axis=0), halve).reshape(fields + reactions, rows, LANES)
-        return [out[i] for i in range(fields)], [out[fields + i] for i in range(reactions)]
-
+    outside, inside = masks_of(48, 16, 32)
     fields, reactions = [], []
     for j in range(FAR):
-        lo, hi = x_before[j], x_after[FAR - 1 - j]
-        fields.append(jnp.where(low, lo, swap(hi)) * outside)
-        reactions.append(jnp.where(low, swap(lo), hi))
+        field, reaction = folded(x_before[j], x_after[FAR - 1 - j])
+        fields.append(field * outside)
+        reactions.append(reaction)
     for j in range(2):
         fields.append(f_in[j])
         reactions.append(k_in[j])
     for j in range(7):
         kpairs[j] = pair_rows(reactions[2 * j + 2] + reactions[2 * j + 3])
-    value = corrections(1, fields, reactions[1:15], [outside] * 13 + [inside], blur_z_halves)
+    value = corrections(1, fields, reactions[1:15], [outside] * 13 + [inside])
     own1[0] = value[13][16:32]
     for j in range(1, 8):
         own1[j] = e_in[j, 16:32, :]
-    rest = coarse_remainders(value + [e_in[1], e_in[2]], fields[2:], reactions[2:], blur_z_halves)
+    rest = coarse_remainders(1, value + [e_in[1], e_in[2]], fields[2:], reactions[2:])
     for j in range(7):
         pairs[j] = pair_rows(rest[2 * j] + rest[2 * j + 1])
-    rf, rk = both(7, 7, 24)
-    outside, inside = masks_of(24, 8, 16, 32)
-    fields = [rf[j] * (outside if j < 6 else inside) for j in range(7)] + [f2_in[j] for j in range(3)]
-    reactions = rk + [k2_in[j] for j in range(3)]
+    outside, inside = masks_of(24, 8, 16)
+    fields = [halved(even_rows(pairs, j, 24), 2) * (outside if j < 6 else inside) for j in range(7)]
+    fields += [f2_in[j] for j in range(3)]
+    reactions = [halved(even_rows(kpairs, j, 24), 2) for j in range(7)] + [k2_in[j] for j in range(3)]
     for p in range(4):
         kpairs[p, 0:24, :] = pair_rows(reactions[2 * p + 2] + reactions[2 * p + 3])
-    value = corrections(
-        2, fields + [swap(fields[9])], reactions[1:], [outside] * 5 + [inside] * 4, blur_z_part
-    )
+    value = corrections(2, fields + [swap(fields[9])], reactions[1:], [outside] * 5 + [inside] * 4)
     for j in range(4):
         own2[j] = value[5 + j][8:16]
-    rest = coarse_remainders(value + [swap(value[8])], fields[2:], reactions[2:], blur_z_part)
+    rest = coarse_remainders(2, value + [swap(value[8])], fields[2:], reactions[2:])
     for p in range(4):
         pairs[p, 0:24, :] = pair_rows(rest[2 * p] + rest[2 * p + 1])
-    rf, rk = both(4, 4, 16)
-    outside, inside = masks_of(16, 4, 8, 16)
-    fields = [rf[0] * outside, rf[1] * outside, rf[2] * inside, rf[3] * inside]
+    outside, inside = masks_of(16, 4, 8)
+    fields = [halved(even_rows(pairs, j, 16), 4) * (outside if j < 2 else inside) for j in range(4)]
+    reactions = [halved(even_rows(kpairs, j, 16), 4) for j in range(4)]
     for p in range(2):
-        kpairs[p, 0:16, :] = pair_rows(rk[2 * p] + rk[2 * p + 1])
-    value = corrections(3, fields + [swap(fields[3])], rk[1:], [outside, inside, inside], blur_z_part)
+        kpairs[p, 0:16, :] = pair_rows(reactions[2 * p] + reactions[2 * p + 1])
+    value = corrections(3, fields + [swap(fields[3])], reactions[1:], [outside, inside, inside])
     for j in range(2):
         own3[j] = value[1 + j][0:8]
-    rest = coarse_remainders(value + [swap(value[2])], fields[2:], rk[2:], blur_z_part)
+    rest = coarse_remainders(3, value + [swap(value[2])], fields[2:], reactions[2:])
     pairs[0, 0:16, :] = pair_rows(rest[0] + rest[1])
-    rf, rk = both(1, 2, 8)
-    f4[...] = rf[0]
-    k4[0] = rk[0]
-    k4[1] = rk[1]
+    f4[...] = halved(even_rows(pairs, 0, 8), 8)
+    for p in range(2):
+        k4[p] = halved(even_rows(kpairs, p, 8), 8)
 
 
 def unfold(own1, own2, own3, e1, e2, e3):
-    for own, out, rows in ((own1, e1, slice(0, 16)), (own2, e2, slice(0, 8)), (own3, e3, slice(4, 8))):
+    rows = (slice(0, 16), slice(0, 8), slice(4, 8))
+    for level, own, out, part in zip((1, 2, 3), (own1, own2, own3), (e1, e2, e3), rows):
         planes, _, lanes = out.shape
+        source = iota((LANES, LANES), 0)
+        target = iota((LANES, LANES), 1)
+        hit = source == ((target & 63) << level) + (target >> 6)
+        values = own[...].reshape(-1, LANES)
+        values = jnp.dot(
+            values,
+            jnp.where(hit, 1.0, 0.0).astype(F32),
+            precision=lax.Precision.HIGHEST,
+            preferred_element_type=F32,
+        ).reshape(own.shape)
         for j in range(planes // 2):
-            value = own[j]
-            out[j] = value[rows, 0:lanes]
-            out[planes - 1 - j] = swap(value)[rows, 0:lanes]
+            value = values[j]
+            out[j] = value[part, 0:lanes]
+            out[planes - 1 - j] = pltpu.roll(value, 64, 1)[part, 0:lanes]
 
 
 def pack_last(y_before, own, y_after, out):
@@ -453,22 +436,30 @@
 
 
 def last_kernel(own, x_before, x_after, k4, e4, rest):
-    outside, inside = masks_of(8, 2, 4, 8)
-    low = low_half(own.shape)
-    inside = jnp.where(iota(own.shape, 0) < 6, inside, 0.0)
-    outside = jnp.where(iota(own.shape, 0) < 6, outside, 0.0)
+    outside, inside = masks_of(8, 2, 4)
+    even = even_lanes(own.shape)
+    row = iota(own.shape, 0)
+    inside = jnp.where(row < 6, inside, 0.0)
+    outside = jnp.where(row < 6, outside, 0.0)
     middle = own[...] * inside
     fields = [
-        jnp.where(low, x_before[...], x_after[...]) * outside,
-        swap(jnp.where(low, x_after[...], x_before[...])) * outside,
+        jnp.where(even, x_before[...], x_after[...]) * outside,
+        swap(jnp.where(even, x_after[...], x_before[...])) * outside,
         middle,
         swap(middle),
     ]
-    value = corrections(4, fields, [k4[0], k4[1]], [outside, inside], blur_z_part)
-    left = coarse_remainders(value + [swap(value[1])], [middle], [k4[1]], blur_z_part)[0]
+    value = corrections(4, fields, [k4[0], k4[1]], [outside, inside])
+    left = coarse_remainders(4, value + [swap(value[1])], [middle], [k4[1]])[0]
+    lane = iota(own.shape, 1)
     for out, here in ((e4, value[1]), (rest, left)):
-        out[0] = here[2:4, 0:8]
-        out[1] = swap(here)[2:4, 0:8]
+        for side, folded_plane in enumerate((here, to_left(here))):
+            cells = [
+                jnp.where(lane == z, pltpu.roll(folded_plane, (LANES - 15 * z) % LANES, 1), 0.0)
+                for z in range(8)
+            ]
+            while len(cells) > 1:
+                cells = [a + b for a, b in zip(cells[::2], cells[1::2])]
+            out[side] = cells[0][2:4, 0:8]
 
 
 def neighbours_of(up, down, axis):
@@ -533,12 +524,13 @@
     )(packed, x_before, x_after, *fields, inner)
     iterate = jnp.concatenate([edge[0:2], fields[5][2:30, 0:32], edge[2:4]], axis=0)
     y_before, y_after = neighbours_of(coarse, coarse, "agg")
+    y_before, iterate = lax.optimization_barrier((y_before, iterate))
     extended = jnp.concatenate([y_before, coarse, y_after], axis=1)
     x_before, x_after = neighbours_of(extended[16 - FAR :], extended[:FAR], "box")
     plane = (48, LANES)
     inner = call(
         coarse_inner,
-        [(8,) + plane] * 3 + [(3, 24, LANES)] * 2,
+        [(2,) + plane] * 2 + [(8,) + plane] + [(3, 24, LANES)] * 2,
         [VMEM] * 3,
         scratch=[(3,) + plane] * 2,
         flops=4000000,
@@ -555,6 +547,7 @@
         unfold, [(16, 16, 64), (8, 8, 32), (4, 4, 16)], [VMEM] * 3, flops=2000000, name="unfold"
     )(*owns)
     y_before, y_after = neighbours_of(f4, f4, "agg")
+    y_before, e1, e2, e3 = lax.optimization_barrier((y_before, e1, e2, e3))
     (last,) = call(pack_last, [(8, LANES)], [VMEM] * 3, name="pack_last")(y_before, f4, y_after)
     x_before, x_after = neighbours_of(last, last, "box")
     e4, rest = call(

time: 52.5 us -> 51.5 us (0.981)
  Pallas kernels: 9.84 us -> 9.06 us
    pallas_call x1, Pallas kernels: 1.98 us -> 1.33 us  [per_device(): call(coarse_outer, [(8, 16, LANES), (4, 8, LANES), (2, 8, LANES), (8, LAN...]
where the time goes in v5:
time: 51.5 us; the launch traced here: 51.3 us
  starting transfers between devices  21.9 us (43%)
  waiting for transfers between devices  18.6 us (36%)
  Pallas kernels  9.06 us (18%)
  other arithmetic  0.83 us (2%)
  between operations  0.74 us (1%)
    ppermute x12, starting transfers between devices, neighbours_of(): return (lax.ppermute(up, axis, ahead), lax.ppermute(down, axis, back))  21.9 us
    ppermute x12, waiting for transfers between devices, neighbours_of(): return (lax.ppermute(up, axis, ahead), lax.ppermute(down, axis, back))  18.6 us
    pallas_call x1, Pallas kernels, per_device(): call(fine_inner, [big] * 6 + [(16, 16, LANES)], [VMEM] * 3 + [HBM] * 3, s...  3.26 us
    pallas_call x1, Pallas kernels, per_device(): call(pack_rows, [tile, tile, (7, 32, LANES), (7, 32, LANES)], [HBM] * 4,...  1.39 us
    pallas_call x1, Pallas kernels, per_device(): call(coarse_outer, [(8, 16, LANES), (4, 8, LANES), (2, 8, LANES), (8, LAN...  1.33 us
  transfers between devices with their start and end apart: 12, of which 7 were waited for; matrix products, arithmetic and copies ran while one was open for 2% of the time, Pallas kernels for 9%

profile of v5, /device:TPU:97, one launch (start us, length us, event | category | flops | bytes accessed | tf_op | source)
XLA Modules:
  0.0 51.3 jit_solution(5407567498255989113)
XLA Ops:
  0.6 1.4 %pack_rows.1 = (f32[32,8,128]{2,1,0:T(8,128)S(1)}, f32[32,8,128]{2,1,0:T(8,128)S(1)}, f32[7,32,128]{2,1,0:T(8,128)S(1)}, f32[7,32,128]{2,1,0:T(8,128)S(1)}) custom-call(s32[1,1,4]{2,1,0:T(1,128)} %flags.1, f32[32,32,128]{2,1,0:T(8,128)} %guess.3, f32[32,32,128]{2,1,0:T(8,128)} %source.3, f32[32,32,128]{2,1,0:T(8,128)} %reaction.3), custom_call_target="tpu_custom_call" | custom-call | tf_op jit(solution)/shard_map/pack_rows/pallas_call | solution.py:495
  2.0 1.3 %collective-permute-start = (f32[32,8,128]{2,1,0:T(8,128)S(1)}, f32[32,8,128]{2,1,0:T(8,128)S(1)}, u32[]{:S(2)}, u32[]{:S(2)}) collective-permute-start(f32[32,8,128]{2,1,0:T(8,128)S(1)} %get-tuple-element.42.own), channel_id=1, source_target_pairs={{0,1},{1,2},{2,3},{3,4},{4,5},{5,6},{6,7},{7,8},{8,9},{9,10},{10,1... | collective-permute-start | bytes 393224 | tf_op jit(solution)/shard_map/ppermute | solution.py:469
  3.3 3.8 %collective-permute-start.1 = (f32[32,8,128]{2,1,0:T(8,128)S(1)}, f32[32,8,128]{2,1,0:T(8,128)S(1)}, u32[]{:S(2)}, u32[]{:S(2)}) collective-permute-start(f32[32,8,128]{2,1,0:T(8,128)S(1)} %get-tuple-element.43), channel_id=1, source_target_pairs={{0,15},{1,0},{2,1},{3,2},{4,3},{5,4},{6,5},{7,6},{8,7},{9,8},{10,9... | collective-permute-start | bytes 393224 | tf_op jit(solution)/shard_map/ppermute | solution.py:469
  7.1 3.0 %collective-permute-done.from_before = f32[32,8,128]{2,1,0:T(8,128)S(1)} collective-permute-done((f32[32,8,128]{2,1,0:T(8,128)S(1)}, f32[32,8,128]{2,1,0:T(8,128)S(1)}, u32[]{:S(2)}, u32[]{:S(2)}) %collective-permute-start) | collective-permute-done | bytes 131104 | tf_op jit(solution)/shard_map/ppermute | solution.py:469
  10.1 0.0 collective-permute-done.1.from_after
  10.1 4.1 %collective-permute-start.2 = (f32[8,40,128]{2,1,0:T(8,128)S(1)}, f32[8,40,128]{2,1,0:T(8,128)S(1)}, u32[]{:S(2)}, u32[]{:S(2)}) collective-permute-start(f32[8,40,128]{2,1,0:T(8,128)S(1)} %get-tuple-element.46.packed), channel_id=1, source_target_pairs={{0,16},{16,32},{32,48},{48,64},{64,80},{80,96},{96,112},{112,128},... | collective-permute-start | bytes 491528 | tf_op jit(solution)/shard_map/ppermute | solution.py:469
  14.3 0.0 collective-permute-start.3
  14.3 3.3 %fine_inner.1 = (f32[32,40,128]{2,1,0:T(8,128)S(1)}, f32[32,40,128]{2,1,0:T(8,128)S(1)}, f32[32,40,128]{2,1,0:T(8,128)S(1)}, f32[32,40,128]{2,1,0:T(8,128)S(1)},...) custom-call(f32[8,40,128]{2,1,0:T(8,128)S(1)} %get-tuple-element.46.packed, ...), custom_call_target="tpu_custom_call" | custom-call | flops 8000000 | bytes 8000000 | tf_op jit(solution)/shard_map/fine_inner/pallas_call | solution.py:509
  17.6 0.0 collective-permute-done.2.x_before
  17.6 2.6 %collective-permute-done.3.x_after = f32[8,40,128]{2,1,0:T(8,128)S(1)} collective-permute-done((f32[8,40,128]{2,1,0:T(8,128)S(1)}, f32[8,40,128]{2,1,0:T(8,128)S(1)}, u32[]{:S(2)}, u32[]{:S(2)}) %collective-permute-start.3) | collective-permute-done | bytes 163872 | tf_op jit(solution)/shard_map/ppermute | solution.py:469
  20.2 0.5 fine_outer.1
  20.7 0.1 collective-permute-start.4
  20.8 4.9 %collective-permute-start.5 = (f32[16,16,128]{2,1,0:T(8,128)S(1)}, f32[16,16,128]{2,1,0:T(8,128)S(1)}, u32[]{:S(2)}, u32[]{:S(2)}) collective-permute-start(f32[16,16,128]{2,1,0:T(8,128)S(1)} %get-tuple-element.55.own), channel_id=1, source_target_pairs={{0,15},{1,0},{2,1},{3,2},{4,3},{5,4},{6,5},{7,6},{8,7},{9,8},{10,9... | collective-permute-start | bytes 393224 | tf_op jit(solution)/shard_map/ppermute | solution.py:469
  25.7 0.8 %pad_maximum_fusion = f32[32,32,128]{2,1,0:T(8,128)} fusion(f32[2,32,128]{2,1,0:T(8,128)S(1)} %get-tuple-element.81, f32[28,32,128]{2,1,0:T(8,128)S(1)} %slice.16, f32[2,32,128]{2,1,0:T(8,128)S(1)} %get-tuple-element.80), kind=kLoop, calls=%fused_computation | loop fusion | flops 262144 | bytes 1048576 | tf_op jit(solution)/shard_map/concatenate | solution.py:525
  26.5 1.4 %collective-permute-done.4.y_before = f32[16,16,128]{2,1,0:T(8,128)S(1)} collective-permute-done((f32[16,16,128]{2,1,0:T(8,128)S(1)}, f32[16,16,128]{2,1,0:T(8,128)S(1)}, u32[]{:S(2)}, u32[]{:S(2)}) %collective-permute-start.4) | collective-permute-done | bytes 131104 | tf_op jit(solution)/shard_map/ppermute | solution.py:469
  28.0 0.0 collective-permute-done.5.y_after
  28.1 1.7 %collective-permute-start.6 = (f32[14,48,128]{2,1,0:T(8,128)S(1)}, f32[14,48,128]{2,1,0:T(8,128)S(1)}, u32[]{:S(2)}, u32[]{:S(2)}) collective-permute-start(f32[14,48,128]{2,1,0:T(8,128)S(1)} %get-tuple-element.79), channel_id=1, source_target_pairs={{0,16},{16,32},{32,48},{48,64},{64,80},{80,96},{96,112},{112,128},... | collective-permute-start | bytes 1032200 | tf_op jit(solution)/shard_map/ppermute | solution.py:469
  29.8 0.0 collective-permute-start.7
  29.8 0.6 %coarse_inner.1 = (f32[2,48,128]{2,1,0:T(8,128)S(1)}, f32[2,48,128]{2,1,0:T(8,128)S(1)}, f32[8,48,128]{2,1,0:T(8,128)S(1)}, f32[3,24,128]{2,1,0:T(8,128)S(1)}, f32[3,24,128]{2,1,0:T(8,128)S(1)}) custom-call(f32[16,16,128]{2,1,0:T(8,128)S(1)} %collective-permute-done.4.y_before, f32[16,16,128]{2,1,0:T(8,128)S(1)} %get-tuple-element.55.own, ...), custom_call_target="tpu_custom_call" | custom-call | flops 4000000 | bytes 4000000 | tf_op jit(solution)/shard_map/coarse_inner/pallas_call | solution.py:531
  30.4 3.6 %collective-permute-done.6.x_before = f32[14,48,128]{2,1,0:T(8,128)S(1)} collective-permute-done((f32[14,48,128]{2,1,0:T(8,128)S(1)}, f32[14,48,128]{2,1,0:T(8,128)S(1)}, u32[]{:S(2)}, u32[]{:S(2)}) %collective-permute-start.6) | collective-permute-done | bytes 344096 | tf_op jit(solution)/shard_map/ppermute | solution.py:469
  34.0 3.7 %collective-permute-done.7.x_after = f32[14,48,128]{2,1,0:T(8,128)S(1)} collective-permute-done((f32[14,48,128]{2,1,0:T(8,128)S(1)}, f32[14,48,128]{2,1,0:T(8,128)S(1)}, u32[]{:S(2)}, u32[]{:S(2)}) %collective-permute-start.7) | collective-permute-done | bytes 344096 | tf_op jit(solution)/shard_map/ppermute | solution.py:469
  37.7 1.3 %coarse_outer.1 = (f32[8,16,128]{2,1,0:T(8,128)S(1)}, f32[4,8,128]{2,1,0:T(8,128)S(1)}, f32[2,8,128]{2,1,0:T(8,128)S(1)}, f32[8,128]{1,0:T(8,128)S(1)}, f32[2,8,128]{2,1,0:T(8,128)S(1)}) custom-call(f32[14,48,128]{2,1,0:T(8,128)S(1)} %collective-permute-done.6.x_before, f32[14,48,128]{2,1,0:T(8,128)S(1)} %collective-permute-done.7.x_after, ...), custom_call_target="tpu_custom_call" | custom-call | tf_op jit(solution)/shard_map/coarse_outer/pallas_call | solution.py:539
  39.0 0.0 collective-permute-start.8
  39.1 4.9 %collective-permute-start.9 = (f32[8,128]{1,0:T(8,128)S(1)}, f32[8,128]{1,0:T(8,128)S(1)}, u32[]{:S(2)}, u32[]{:S(2)}) collective-permute-start(f32[8,128]{1,0:T(8,128)S(1)} %get-tuple-element.64.own), channel_id=1, source_target_pairs={{0,15},{1,0},{2,1},{3,2},{4,3},{5,4},{6,5},{7,6},{8,7},{9,8},{10,9... | collective-permute-start | bytes 12296 | tf_op jit(solution)/shard_map/ppermute | solution.py:469
  44.0 1.0 %unfold.1 = (f32[16,16,64]{2,1,0:T(8,128)}, f32[8,8,32]{2,1,0:T(8,128)}, f32[4,4,16]{2,1,0:T(4,128)}) custom-call(f32[8,16,128]{2,1,0:T(8,128)S(1)} %get-tuple-element.65.own1, f32[4,8,128]{2,1,0:T(8,128)S(1)} %get-tuple-element.66.own2, f32[2,8,128]{2,1,0:T(8,128)S(1)} %get-tuple-element.67.own3), custom_call_target="tpu_custom_call" | custom-call | flops 2000000 | bytes 2000000 | tf_op jit(solution)/shard_map/unfold/pallas_call | solution.py:546
  44.9 0.0 collective-permute-done.8.y_before
  44.9 0.0 collective-permute-done.9.y_after
  44.9 1.1 %collective-permute-start.10 = (f32[8,128]{1,0:T(8,128)S(1)}, f32[8,128]{1,0:T(8,128)S(1)}, u32[]{:S(2)}, u32[]{:S(2)}) collective-permute-start(f32[8,128]{1,0:T(8,128)S(1)} %pack_last.1.own), channel_id=1, source_target_pairs={{0,16},{16,32},{32,48},{48,64},{64,80},{80,96},{96,112},{112,128},... | collective-permute-start | bytes 12296 | tf_op jit(solution)/shard_map/ppermute | solution.py:469
  46.0 0.0 collective-permute-start.11
  46.0 0.8 %collective-permute-done.10.x_before = f32[8,128]{1,0:T(8,128)S(1)} collective-permute-done((f32[8,128]{1,0:T(8,128)S(1)}, f32[8,128]{1,0:T(8,128)S(1)}, u32[]{:S(2)}, u32[]{:S(2)}) %collective-permute-start.10) | collective-permute-done | bytes 4128 | tf_op jit(solution)/shard_map/ppermute | solution.py:469
  46.8 3.5 %collective-permute-done.11.x_after = f32[8,128]{1,0:T(8,128)S(1)} collective-permute-done((f32[8,128]{1,0:T(8,128)S(1)}, f32[8,128]{1,0:T(8,128)S(1)}, u32[]{:S(2)}, u32[]{:S(2)}) %collective-permute-start.11) | collective-permute-done | bytes 4128 | tf_op jit(solution)/shard_map/ppermute | solution.py:469
  50.2 1.0 %last.1 = (f32[2,2,8]{2,1,0:T(2,128)}, f32[2,2,8]{2,1,0:T(2,128)}) custom-call(f32[8,128]{1,0:T(8,128)S(1)} %pack_last.1.own, f32[8,128]{1,0:T(8,128)S(1)} %collective-permute-done.10.x_before, f32[8,128]{1,0:T(8,128)S(1)} %collective-permute-done.11.x_after, f32[2,8,128]{2,1,0:T(8,128)S(1)} %get-tuple-element.75.k4), custom_call_target="tpu_custom_call" | custom-call | tf_op jit(solution)/shard_map/last/pallas_call | solution.py:553
  (8 shorter events, 0.2 us)
Async XLA Ops:
  2.0 8.1 %collective-permute-start = (f32[32,8,128]{2,1,0:T(8,128)S(1)}, f32[32,8,128]{2,1,0:T(8,128)S(1)}, u32[]{:S(2)}, u32[]{:S(2)}) collective-permute-start(f32[32,8,128]{2,1,0:T(8,128)S(1)} %get-tuple-element.42.own), channel_id=1, source_target_pairs={{0,1},{1,2},{2,3},{3,4},{4,5},{5,6},{6,7},{7,8},{8,9},{9,10},{10,1... | collective-permute-start | bytes 393224 | tf_op jit(solution)/shard_map/ppermute | solution.py:469
  3.3 6.8 %collective-permute-start.1 = (f32[32,8,128]{2,1,0:T(8,128)S(1)}, f32[32,8,128]{2,1,0:T(8,128)S(1)}, u32[]{:S(2)}, u32[]{:S(2)}) collective-permute-start(f32[32,8,128]{2,1,0:T(8,128)S(1)} %get-tuple-element.43), channel_id=1, source_target_pairs={{0,15},{1,0},{2,1},{3,2},{4,3},{5,4},{6,5},{7,6},{8,7},{9,8},{10,9... | collective-permute-start | bytes 393224 | tf_op jit(solution)/shard_map/ppermute | solution.py:469
  10.1 7.5 %collective-permute-start.2 = (f32[8,40,128]{2,1,0:T(8,128)S(1)}, f32[8,40,128]{2,1,0:T(8,128)S(1)}, u32[]{:S(2)}, u32[]{:S(2)}) collective-permute-start(f32[8,40,128]{2,1,0:T(8,128)S(1)} %get-tuple-element.46.packed), channel_id=1, source_target_pairs={{0,16},{16,32},{32,48},{48,64},{64,80},{80,96},{96,112},{112,128},... | collective-permute-start | bytes 491528 | tf_op jit(solution)/shard_map/ppermute | solution.py:469
  14.3 6.0 %collective-permute-start.3 = (f32[8,40,128]{2,1,0:T(8,128)S(1)}, f32[8,40,128]{2,1,0:T(8,128)S(1)}, u32[]{:S(2)}, u32[]{:S(2)}) collective-permute-start(f32[8,40,128]{2,1,0:T(8,128)S(1)} %get-tuple-element.47), channel_id=1, source_target_pairs={{0,240},{16,0},{32,16},{48,32},{64,48},{80,64},{96,80},{112,96},{1... | collective-permute-start | bytes 491528 | tf_op jit(solution)/shard_map/ppermute | solution.py:469
  20.7 7.3 %collective-permute-start.4 = (f32[16,16,128]{2,1,0:T(8,128)S(1)}, f32[16,16,128]{2,1,0:T(8,128)S(1)}, u32[]{:S(2)}, u32[]{:S(2)}) collective-permute-start(f32[16,16,128]{2,1,0:T(8,128)S(1)} %get-tuple-element.55.own), channel_id=1, source_target_pairs={{0,1},{1,2},{2,3},{3,4},{4,5},{5,6},{6,7},{7,8},{8,9},{9,10},{10,1... | collective-permute-start | bytes 393224 | tf_op jit(solution)/shard_map/ppermute | solution.py:469
  20.8 7.2 %collective-permute-start.5 = (f32[16,16,128]{2,1,0:T(8,128)S(1)}, f32[16,16,128]{2,1,0:T(8,128)S(1)}, u32[]{:S(2)}, u32[]{:S(2)}) collective-permute-start(f32[16,16,128]{2,1,0:T(8,128)S(1)} %get-tuple-element.55.own), channel_id=1, source_target_pairs={{0,15},{1,0},{2,1},{3,2},{4,3},{5,4},{6,5},{7,6},{8,7},{9,8},{10,9... | collective-permute-start | bytes 393224 | tf_op jit(solution)/shard_map/ppermute | solution.py:469
  28.1 5.9 %collective-permute-start.6 = (f32[14,48,128]{2,1,0:T(8,128)S(1)}, f32[14,48,128]{2,1,0:T(8,128)S(1)}, u32[]{:S(2)}, u32[]{:S(2)}) collective-permute-start(f32[14,48,128]{2,1,0:T(8,128)S(1)} %get-tuple-element.79), channel_id=1, source_target_pairs={{0,16},{16,32},{32,48},{48,64},{64,80},{80,96},{96,112},{112,128},... | collective-permute-start | bytes 1032200 | tf_op jit(solution)/shard_map/ppermute | solution.py:469
  29.8 7.9 %collective-permute-start.7 = (f32[14,48,128]{2,1,0:T(8,128)S(1)}, f32[14,48,128]{2,1,0:T(8,128)S(1)}, u32[]{:S(2)}, u32[]{:S(2)}) collective-permute-start(f32[14,48,128]{2,1,0:T(8,128)S(1)} %get-tuple-element.78), channel_id=1, source_target_pairs={{0,240},{16,0},{32,16},{48,32},{64,48},{80,64},{96,80},{112,96},{1... | collective-permute-start | bytes 1032200 | tf_op jit(solution)/shard_map/ppermute | solution.py:469
  39.0 5.9 %collective-permute-start.8 = (f32[8,128]{1,0:T(8,128)S(1)}, f32[8,128]{1,0:T(8,128)S(1)}, u32[]{:S(2)}, u32[]{:S(2)}) collective-permute-start(f32[8,128]{1,0:T(8,128)S(1)} %get-tuple-element.64.own), channel_id=1, source_target_pairs={{0,1},{1,2},{2,3},{3,4},{4,5},{5,6},{6,7},{7,8},{8,9},{9,10},{10,1... | collective-permute-start | bytes 12296 | tf_op jit(solution)/shard_map/ppermute | solution.py:469
  39.1 5.9 %collective-permute-start.9 = (f32[8,128]{1,0:T(8,128)S(1)}, f32[8,128]{1,0:T(8,128)S(1)}, u32[]{:S(2)}, u32[]{:S(2)}) collective-permute-start(f32[8,128]{1,0:T(8,128)S(1)} %get-tuple-element.64.own), channel_id=1, source_target_pairs={{0,15},{1,0},{2,1},{3,2},{4,3},{5,4},{6,5},{7,6},{8,7},{9,8},{10,9... | collective-permute-start | bytes 12296 | tf_op jit(solution)/shard_map/ppermute | solution.py:469
  44.9 1.8 %collective-permute-start.10 = (f32[8,128]{1,0:T(8,128)S(1)}, f32[8,128]{1,0:T(8,128)S(1)}, u32[]{:S(2)}, u32[]{:S(2)}) collective-permute-start(f32[8,128]{1,0:T(8,128)S(1)} %pack_last.1.own), channel_id=1, source_target_pairs={{0,16},{16,32},{32,48},{48,64},{64,80},{80,96},{96,112},{112,128},... | collective-permute-start | bytes 12296 | tf_op jit(solution)/shard_map/ppermute | solution.py:469
  46.0 4.2 %collective-permute-start.11 = (f32[8,128]{1,0:T(8,128)S(1)}, f32[8,128]{1,0:T(8,128)S(1)}, u32[]{:S(2)}, u32[]{:S(2)}) collective-permute-start(f32[8,128]{1,0:T(8,128)S(1)} %pack_last.1.own), channel_id=1, source_target_pairs={{0,240},{16,0},{32,16},{48,32},{64,48},{80,64},{96,80},{112,96},{1... | collective-permute-start | bytes 12296 | tf_op jit(solution)/shard_map/ppermute | solution.py:469

commit v6 on v5

--- a/solution.py
+++ b/solution.py
@@ -44,6 +44,20 @@
     return out
 
 
+def across_of(axis):
+    return ("box", 2) if axis == "agg" else ("agg", 1)
+
+
+def moves_up(axis):
+    name, width = across_of(axis)
+    return lax.axis_index(name) // width % 2 == 0
+
+
+def in_order(axis, first, second):
+    up = moves_up(axis)
+    return jnp.where(up, first, second), jnp.where(up, second, first)
+
+
 def blur_z(values, stride):
     lane = iota(values.shape, 1)
     left = jnp.where(lane < stride, 0.0, pltpu.roll(values, stride, 1))
@@ -84,7 +98,7 @@
 
 
 def pack_rows(
-    flags, guess, source, reaction, up, down, strip_up, strip_down,
+    flags, guess, source, reaction, first, second, strip_up, strip_down,
     flag_smem, guess_lo, guess_hi, source_lo, source_hi, reaction_lo, reaction_hi, sems,
 ):
     lo, hi = pl.ds(0, 8), pl.ds(24, 8)
@@ -112,8 +126,8 @@
     for i in range(boxes):
         flag = jnp.where(lane // (LANES // boxes) == i, flag_smem[0, 0, i].astype(F32), flag)
     flag = flag[None]
-    row = iota(up.shape, 1)
-    up[...] = jnp.where(
+    row = iota(first.shape, 1)
+    up = jnp.where(
         row >= 5,
         guess_hi[...],
         jnp.where(
@@ -122,7 +136,7 @@
             jnp.where(row >= 1, pltpu.roll(reaction_hi[...], 3, 1), flag),
         ),
     )
-    down[...] = jnp.where(
+    down = jnp.where(
         row < 3,
         guess_lo[...],
         jnp.where(
@@ -131,6 +145,7 @@
             jnp.where(row < 7, pltpu.roll(reaction_lo[...], 5, 1), flag),
         ),
     )
+    first[...], second[...] = in_order("agg", up, down)
     for copy in copies[7:]:
         copy.wait()
 
@@ -144,26 +159,32 @@
     return guess, source, reaction
 
 
-def pack_planes(own, from_before, from_after, strip_up, strip_down, up, down):
+def flag_plane(own, lo, hi):
+    tile = (8, LANES)
+    halo = jnp.where(iota(tile, 0) < 4, jnp.broadcast_to(hi, tile), jnp.broadcast_to(lo, tile))
+    return jnp.concatenate([jnp.broadcast_to(own, (32, LANES)), halo], axis=0)
+
+
+def pack_planes(own_first, own_second, from_first, from_second, strip_up, strip_down, first, second, mask):
     before, after = edges("agg")
-    tile = (8, LANES)
-    own_mask = jnp.broadcast_to(own[0, 0:1, :], (32, LANES))
-    lo_mask = jnp.broadcast_to(from_before[0, 0:1, :] * before, tile)
-    hi_mask = jnp.broadcast_to(from_after[0, 7:8, :] * after, tile)
-    halo_mask = jnp.where(iota(tile, 0) < 4, hi_mask, lo_mask)
+    own, _ = in_order("agg", own_first[0, 0:1, :], own_second[0, 0:1, :])
+    from_before, from_after = in_order("agg", from_first[...], from_second[...])
+    lo = from_before[0, 0:1, :] * before
+    hi = from_after[0, 7:8, :] * after
+    mask[...] = flag_plane(own, lo, hi)
     planes = from_before.shape[0]
-    for target, strip, first, local in (
-        (up, strip_up, planes - 4, (1, 2, 2)),
-        (down, strip_down, 0, (0, 0, 0)),
-    ):
-        tiles = halo_tiles(from_before[first : first + 4], from_after[first : first + 4], before, after)
-        target[0:7, 0:32, :] = strip[...]
-        at = 0
-        for tile, start, count in zip(tiles, local, (3, 2, 2)):
-            target[at : at + count, 32:40, :] = tile[start : start + count]
-            at += count
-        target[7, 0:32, :] = own_mask
-        target[7, 32:40, :] = halo_mask
+    strips, tiles = [], []
+    for strip, at, local in ((strip_up, planes - 4, (1, 2, 2)), (strip_down, 0, (0, 0, 0))):
+        fields = halo_tiles(from_before[at : at + 4], from_after[at : at + 4], before, after)
+        rows = [tile[i] for tile, start, count in zip(fields, local, (3, 2, 2)) for i in range(start, start + count)]
+        row = iota(rows[0].shape, 0)
+        rows[0] = jnp.where(row == 3, own, jnp.where(row == 4, lo, rows[0]))
+        rows[1] = jnp.where(row == 3, hi, rows[1])
+        strips.append(strip[...])
+        tiles.append(rows)
+    first[:, 0:32, :], second[:, 0:32, :] = in_order("box", *strips)
+    for i, (up, down) in enumerate(zip(*tiles)):
+        first[i, 32:40, :], second[i, 32:40, :] = in_order("box", up, down)
 
 
 SHIFT = 8.0 / 7.0
@@ -174,7 +195,7 @@
 
 
 def fine_inner(
-    packed, from_before, from_after, guess, source, reaction,
+    mask_ref, from_first, from_second, guess, source, reaction,
     g, s, k, d, u, w, coarse, pairs, kpairs, sems,
 ):
     rows = pl.ds(0, 32)
@@ -186,7 +207,8 @@
 
     def assemble(x):
         at = pl.ds(x, 32)
-        tiles = halo_tiles(from_before[at], from_after[at], before, after)
+        sides = in_order("agg", from_first[at], from_second[at])
+        tiles = halo_tiles(*sides, before, after)
         g[at, 32:40, :] = tiles[0]
         s[at, 32:40, :] = tiles[1]
         k[at, 32:40, :] = tiles[2]
@@ -197,7 +219,7 @@
 
     def remainders(field, x, size):
         planes = [field[x + i] for i in range(-1, size + 1)]
-        mask = packed[7]
+        mask = mask_ref[...]
         out = []
         for i, q in enumerate(blurred(planes, 1)):
             r = mask * (s[x + i] - (k[x + i] + SHIFT) * planes[i + 1] + q * (1.0 / 56.0))
@@ -238,8 +260,12 @@
         coarse[i] = value
 
 
-def fine_outer(packed, x_before, x_after, g, s, k, d, u, w, inner, coarse, edge, pairs):
+def fine_outer(mask_ref, from_first, from_second, g, s, k, d, u, w, inner, coarse, edge, pairs):
     xbefore, xafter = edges("box")
+    x_before, x_after = in_order("box", from_first[...], from_second[...])
+    mask_before, mask_after = (
+        flag_plane(x[0, 35:36], x[0, 36:37], x[1, 35:36]) * edge for x, edge in ((x_before, xbefore), (x_after, xafter))
+    )
     theta, c1, c2 = coefficients(0)
     new_d, new_u, new_w = {}, {}, {}
 
@@ -256,7 +282,7 @@
         return side(x, lambda i: x_before[i + 4], lambda i: x_after[i + 5], lambda i: k[i])
 
     def mask_at(x):
-        return side(x, lambda i: x_before[7] * xbefore, lambda i: x_after[7] * xafter, lambda i: packed[7])
+        return side(x, lambda i: mask_before, lambda i: mask_after, lambda i: mask_ref[...])
 
     def remainders(field, first, size):
         planes = [field(x) for x in range(first - 1, first + size + 1)]
@@ -359,11 +385,12 @@
 
 
 def coarse_outer(
-    x_before, x_after, f_in, k_in, e_in, f2_in, k2_in, own1, own2, own3, f4, k4,
+    from_first, from_second, f_in, k_in, e_in, f2_in, k2_in, own1, own2, own3, f4, k4,
     pairs, kpairs,
 ):
     outside, inside = masks_of(48, 16, 32)
     fields, reactions = [], []
+    x_before, x_after = in_order("box", from_first[...], from_second[...])
     for j in range(FAR):
         field, reaction = folded(x_before[j], x_after[FAR - 1 - j])
         fields.append(field * outside)
@@ -427,24 +454,26 @@
             out[planes - 1 - j] = pltpu.roll(value, 64, 1)[part, 0:lanes]
 
 
-def pack_last(y_before, own, y_after, out):
+def pack_last(from_first, own, from_second, out):
     before, after = edges("agg")
     row = iota(own.shape, 0)
-    lo = pltpu.roll(y_before[...], 6, 0) * before
-    hi = pltpu.roll(y_after[...], 2, 0) * after
+    y_before, y_after = in_order("agg", from_first[...], from_second[...])
+    lo = pltpu.roll(y_before, 6, 0) * before
+    hi = pltpu.roll(y_after, 2, 0) * after
     out[...] = jnp.where(row < 2, lo, jnp.where(row < 4, own[...], jnp.where(row < 6, hi, 0.0)))
 
 
-def last_kernel(own, x_before, x_after, k4, e4, rest):
+def last_kernel(own, from_first, from_second, k4, e4, rest):
     outside, inside = masks_of(8, 2, 4)
     even = even_lanes(own.shape)
     row = iota(own.shape, 0)
     inside = jnp.where(row < 6, inside, 0.0)
     outside = jnp.where(row < 6, outside, 0.0)
     middle = own[...] * inside
+    x_before, x_after = in_order("box", from_first[...], from_second[...])
     fields = [
-        jnp.where(even, x_before[...], x_after[...]) * outside,
-        swap(jnp.where(even, x_after[...], x_before[...])) * outside,
+        jnp.where(even, x_before, x_after) * outside,
+        swap(jnp.where(even, x_after, x_before)) * outside,
         middle,
         swap(middle),
     ]
@@ -462,11 +491,22 @@
             out[side] = cells[0][2:4, 0:8]
 
 
-def neighbours_of(up, down, axis):
-    count = lax.axis_size(axis)
-    ahead = [(i, (i + 1) % count) for i in range(count)]
-    back = [(i, (i - 1) % count) for i in range(count)]
-    return lax.ppermute(up, axis, ahead), lax.ppermute(down, axis, back)
+def exchanged(first, second, axis):
+    names = ("box", "agg")
+    along = names.index(axis)
+    across, width = across_of(axis)
+    sizes = [lax.axis_size(name) for name in names]
+    route = []
+    for source in range(sizes[0] * sizes[1]):
+        at = list(divmod(source, sizes[1]))
+        step = 1 if at[names.index(across)] // width % 2 == 0 else -1
+        if 0 <= at[along] + step < sizes[along]:
+            at[along] += step
+        else:
+            at[1 - along] += step * width
+        route.append((source, at[0] * sizes[1] + at[1]))
+    inverse = [(target, source) for source, target in route]
+    return lax.ppermute(first, names, route), lax.ppermute(second, names, inverse)
 
 
 VMEM = pl.BlockSpec(memory_space=pltpu.VMEM)
@@ -492,7 +532,7 @@
     flags, guess, source, reaction = (
         pltpu.with_memory_space_constraint(v, pltpu.HBM) for v in (flags, guess, source, reaction)
     )
-    own, down, strip_up, strip_down = call(
+    *packed, strip_up, strip_down = call(
         pack_rows,
         [tile, tile, (7, 32, LANES), (7, 32, LANES)],
         [HBM] * 4,
@@ -500,11 +540,11 @@
         copies=13,
         name="pack_rows",
     )(flags, guess, source, reaction)
-    y_before, y_after = neighbours_of(own, down, "agg")
-    packed, down = call(
-        pack_planes, [(8, 40, LANES)] * 2, [VMEM] * 5, name="pack_planes"
-    )(own, y_before, y_after, strip_up, strip_down)
-    x_before, x_after = neighbours_of(packed, down, "box")
+    y_sides = exchanged(*packed, "agg")
+    *packed, mask = call(
+        pack_planes, [(7, 40, LANES)] * 2 + [(40, LANES)], [VMEM] * 6, name="pack_planes"
+    )(*packed, *y_sides, strip_up, strip_down)
+    x_sides = exchanged(*packed, "box")
     big = (32, 40, LANES)
     *fields, inner = call(
         fine_inner,
@@ -514,19 +554,20 @@
         copies=3,
         flops=8000000,
         name="fine_inner",
-    )(packed, y_before, y_after, guess, source, reaction)
+    )(mask, *y_sides, guess, source, reaction)
     coarse, edge = call(
         fine_outer,
         [(16, 16, LANES), (4, 32, LANES)],
         [VMEM] * 10,
         scratch=[(4, 40, LANES)],
         name="fine_outer",
-    )(packed, x_before, x_after, *fields, inner)
+    )(mask, *x_sides, *fields, inner)
     iterate = jnp.concatenate([edge[0:2], fields[5][2:30, 0:32], edge[2:4]], axis=0)
-    y_before, y_after = neighbours_of(coarse, coarse, "agg")
-    y_before, iterate = lax.optimization_barrier((y_before, iterate))
+    y_first, y_second = exchanged(coarse, coarse, "agg")
+    y_first, iterate = lax.optimization_barrier((y_first, iterate))
+    y_before, y_after = in_order("agg", y_first, y_second)
     extended = jnp.concatenate([y_before, coarse, y_after], axis=1)
-    x_before, x_after = neighbours_of(extended[16 - FAR :], extended[:FAR], "box")
+    x_sides = exchanged(*in_order("box", extended[16 - FAR :], extended[:FAR]), "box")
     plane = (48, LANES)
     inner = call(
         coarse_inner,
@@ -542,17 +583,17 @@
         [VMEM] * 7,
         scratch=[(7,) + plane] * 2,
         name="coarse_outer",
-    )(x_before, x_after, *inner)
+    )(*x_sides, *inner)
     e1, e2, e3 = call(
         unfold, [(16, 16, 64), (8, 8, 32), (4, 4, 16)], [VMEM] * 3, flops=2000000, name="unfold"
     )(*owns)
-    y_before, y_after = neighbours_of(f4, f4, "agg")
-    y_before, e1, e2, e3 = lax.optimization_barrier((y_before, e1, e2, e3))
-    (last,) = call(pack_last, [(8, LANES)], [VMEM] * 3, name="pack_last")(y_before, f4, y_after)
-    x_before, x_after = neighbours_of(last, last, "box")
+    y_first, y_second = exchanged(f4, f4, "agg")
+    y_first, e1, e2, e3 = lax.optimization_barrier((y_first, e1, e2, e3))
+    (last,) = call(pack_last, [(8, LANES)], [VMEM] * 3, name="pack_last")(y_first, f4, y_second)
+    x_sides = exchanged(last, last, "box")
     e4, rest = call(
         last_kernel, [(2, 2, 8), (2, 2, 8)], [VMEM] * 4, name="last"
-    )(last, x_before, x_after, k4)
+    )(last, *x_sides, k4)
     return iterate, e1, e2, e3, e4, rest
 
 

time: 51.5 us -> 49.4 us (0.959)
  the two profiles are of different devices: /device:TPU:97 before, /device:TPU:101 now
where the time goes in v6:
time: 49.4 us; the launch traced here: 49.3 us
  starting transfers between devices  19.9 us (40%)
  waiting for transfers between devices  18.5 us (37%)
  Pallas kernels  9.19 us (19%)
  other arithmetic  0.93 us (2%)
  between operations  0.72 us (1%)
    ppermute x6, starting transfers between devices, exchanged(): lax.ppermute(first, names, route)  15.7 us
    ppermute x6, waiting for transfers between devices, exchanged(): lax.ppermute(second, names, inverse)  9.71 us
    ppermute x6, waiting for transfers between devices, exchanged(): lax.ppermute(first, names, route)  8.8 us
    ppermute x6, starting transfers between devices, exchanged(): lax.ppermute(second, names, inverse)  4.12 us
    pallas_call x1, Pallas kernels, per_device(): call(fine_inner, [big] * 6 + [(16, 16, LANES)], [VMEM] * 3 + [HBM] * 3, s...  3.32 us
    pallas_call x1, Pallas kernels, per_device(): call(pack_rows, [tile, tile, (7, 32, LANES), (7, 32, LANES)], [HBM] * 4,...  1.4 us
    pallas_call x1, Pallas kernels, per_device(): call(coarse_outer, [(8, 16, LANES), (4, 8, LANES), (2, 8, LANES), (8, LAN...  1.33 us
    pallas_call x1, Pallas kernels, per_device(): call(last_kernel, [(2, 2, 8), (2, 2, 8)], [VMEM] * 4, name='last')  1.03 us
  transfers between devices with their start and end apart: 12, of which 9 were waited for; matrix products, arithmetic and copies ran while one was open for 2% of the time, Pallas kernels for 10%

profile of v6, /device:TPU:101, one launch (start us, length us, event | category | flops | bytes accessed | tf_op | source)
XLA Modules:
  0.0 49.3 jit_solution(15463177473065274755)
XLA Ops:
  0.6 1.4 %pack_rows.1 = (f32[32,8,128]{2,1,0:T(8,128)S(1)}, f32[32,8,128]{2,1,0:T(8,128)S(1)}, f32[7,32,128]{2,1,0:T(8,128)S(1)}, f32[7,32,128]{2,1,0:T(8,128)S(1)}) custom-call(s32[1,1,4]{2,1,0:T(1,128)} %flags.1, f32[32,32,128]{2,1,0:T(8,128)} %guess.3, f32[32,32,128]{2,1,0:T(8,128)} %source.3, f32[32,32,128]{2,1,0:T(8,128)} %reaction.3), custom_call_target="tpu_custom_call" | custom-call | tf_op jit(solution)/shard_map/pack_rows/pallas_call | solution.py:535
  2.0 0.3 collective-permute-start
  2.4 1.2 %collective-permute-start.1 = (f32[32,8,128]{2,1,0:T(8,128)S(1)}, f32[32,8,128]{2,1,0:T(8,128)S(1)}, u32[]{:S(2)}, u32[]{:S(2)}) collective-permute-start(f32[32,8,128]{2,1,0:T(8,128)S(1)} %get-tuple-element.44.own_second), channel_id=1, source_target_pairs={{1,0},{2,1},{3,2},{4,3},{5,4},{6,5},{7,6},{8,7},{9,8},{10,9},{11,1... | collective-permute-start | bytes 393224 | tf_op jit(solution)/shard_map/ppermute | solution.py:509
  3.6 2.9 %collective-permute-done.from_first = f32[32,8,128]{2,1,0:T(8,128)S(1)} collective-permute-done((f32[32,8,128]{2,1,0:T(8,128)S(1)}, f32[32,8,128]{2,1,0:T(8,128)S(1)}, u32[]{:S(2)}, u32[]{:S(2)}) %collective-permute-start) | collective-permute-done | bytes 131104 | tf_op jit(solution)/shard_map/ppermute | solution.py:509
  6.5 0.0 collective-permute-done.1.from_second
  6.5 5.3 %collective-permute-start.2 = (f32[7,40,128]{2,1,0:T(8,128)S(1)}, f32[7,40,128]{2,1,0:T(8,128)S(1)}, u32[]{:S(2)}, u32[]{:S(2)}) collective-permute-start(f32[7,40,128]{2,1,0:T(8,128)S(1)} %get-tuple-element.48), channel_id=1, source_target_pairs={{0,16},{1,0},{2,18},{3,2},{4,20},{5,4},{6,22},{7,6},{8,24},{9,8},{... | collective-permute-start | bytes 430088 | tf_op jit(solution)/shard_map/ppermute | solution.py:509
  11.8 0.0 collective-permute-start.3
  11.8 3.3 %fine_inner.1 = (f32[32,40,128]{2,1,0:T(8,128)S(1)}, f32[32,40,128]{2,1,0:T(8,128)S(1)}, f32[32,40,128]{2,1,0:T(8,128)S(1)}, f32[32,40,128]{2,1,0:T(8,128)S(1)},...) custom-call(f32[40,128]{1,0:T(8,128)S(1)} %get-tuple-element.47.mask_ref, ...), custom_call_target="tpu_custom_call" | custom-call | flops 8000000 | bytes 8000000 | tf_op jit(solution)/shard_map/fine_inner/pallas_call | solution.py:549
  15.2 0.0 collective-permute-done.2.from_first
  15.2 2.3 %collective-permute-done.3.from_second = f32[7,40,128]{2,1,0:T(8,128)S(1)} collective-permute-done((f32[7,40,128]{2,1,0:T(8,128)S(1)}, f32[7,40,128]{2,1,0:T(8,128)S(1)}, u32[]{:S(2)}, u32[]{:S(2)}) %collective-permute-start.3) | collective-permute-done | bytes 143392 | tf_op jit(solution)/shard_map/ppermute | solution.py:509
  17.6 0.5 %fine_outer.1 = (f32[16,16,128]{2,1,0:T(8,128)S(1)}, f32[4,32,128]{2,1,0:T(8,128)S(1)}) custom-call(f32[40,128]{1,0:T(8,128)S(1)} %get-tuple-element.47.mask_ref, f32[7,40,128]{2,1,0:T(8,128)S(1)} %collective-permute-done.2.from_first, f32[7,40,128]{2,1,0:T(8,128)S(1)} %collective-permute-done.3.from_second, f32[32,40,128]{2,1,0:T(8,128)S(1)} %get-tuple-element.50.g, ...), custom_call_target="tpu_custom_call" | custom-call | tf_op jit(solution)/shard_map/fine_outer/pallas_call | solution.py:558
  18.1 0.1 collective-permute-start.4
  18.1 1.5 %collective-permute-start.5 = (f32[16,16,128]{2,1,0:T(8,128)S(1)}, f32[16,16,128]{2,1,0:T(8,128)S(1)}, u32[]{:S(2)}, u32[]{:S(2)}) collective-permute-start(f32[16,16,128]{2,1,0:T(8,128)S(1)} %get-tuple-element.57.own), channel_id=1, source_target_pairs={{1,0},{2,1},{3,2},{4,3},{5,4},{6,5},{7,6},{8,7},{9,8},{10,9},{11,1... | collective-permute-start | bytes 393224 | tf_op jit(solution)/shard_map/ppermute | solution.py:509
  19.6 0.8 %pad_maximum_fusion = f32[32,32,128]{2,1,0:T(8,128)} fusion(f32[2,32,128]{2,1,0:T(8,128)S(1)} %get-tuple-element.85, f32[28,32,128]{2,1,0:T(8,128)S(1)} %slice.16, f32[2,32,128]{2,1,0:T(8,128)S(1)} %get-tuple-element.84), kind=kLoop, calls=%fused_computation | loop fusion | flops 262144 | bytes 1048576 | tf_op jit(solution)/shard_map/concatenate | solution.py:565
  20.4 1.5 %collective-permute-done.4 = f32[16,16,128]{2,1,0:T(8,128)S(1)} collective-permute-done((f32[16,16,128]{2,1,0:T(8,128)S(1)}, f32[16,16,128]{2,1,0:T(8,128)S(1)}, u32[]{:S(2)}, u32[]{:S(2)}) %collective-permute-start.4) | collective-permute-done | bytes 131104 | tf_op jit(solution)/shard_map/ppermute | solution.py:509
  21.9 0.1 collective-permute-done.5
  22.1 5.7 %collective-permute-start.6 = (f32[14,48,128]{2,1,0:T(8,128)S(1)}, f32[14,48,128]{2,1,0:T(8,128)S(1)}, u32[]{:S(2)}, u32[]{:S(2)}) collective-permute-start(f32[14,48,128]{2,1,0:T(8,128)S(1)} %get-tuple-element.81), channel_id=1, source_target_pairs={{0,16},{1,0},{2,18},{3,2},{4,20},{5,4},{6,22},{7,6},{8,24},{9,8},{... | collective-permute-start | bytes 1032200 | tf_op jit(solution)/shard_map/ppermute | solution.py:509
  27.9 0.0 collective-permute-start.7
  27.9 0.6 %coarse_inner.1 = (f32[2,48,128]{2,1,0:T(8,128)S(1)}, f32[2,48,128]{2,1,0:T(8,128)S(1)}, f32[8,48,128]{2,1,0:T(8,128)S(1)}, f32[3,24,128]{2,1,0:T(8,128)S(1)}, f32[3,24,128]{2,1,0:T(8,128)S(1)}) custom-call(f32[16,16,128]{2,1,0:T(8,128)S(1)} %get-tuple-element.82.y_before, f32[16,16,128]{2,1,0:T(8,128)S(1)} %get-tuple-element.57.own, ...), custom_call_target="tpu_custom_call" | custom-call | flops 4000000 | bytes 4000000 | tf_op jit(solution)/shard_map/coarse_inner/pallas_call | solution.py:572
  28.5 3.6 %collective-permute-done.6.from_first = f32[14,48,128]{2,1,0:T(8,128)S(1)} collective-permute-done((f32[14,48,128]{2,1,0:T(8,128)S(1)}, f32[14,48,128]{2,1,0:T(8,128)S(1)}, u32[]{:S(2)}, u32[]{:S(2)}) %collective-permute-start.6) | collective-permute-done | bytes 344096 | tf_op jit(solution)/shard_map/ppermute | solution.py:509
  32.1 3.7 %collective-permute-done.7.from_second = f32[14,48,128]{2,1,0:T(8,128)S(1)} collective-permute-done((f32[14,48,128]{2,1,0:T(8,128)S(1)}, f32[14,48,128]{2,1,0:T(8,128)S(1)}, u32[]{:S(2)}, u32[]{:S(2)}) %collective-permute-start.7) | collective-permute-done | bytes 344096 | tf_op jit(solution)/shard_map/ppermute | solution.py:509
  35.8 1.3 %coarse_outer.1 = (f32[8,16,128]{2,1,0:T(8,128)S(1)}, f32[4,8,128]{2,1,0:T(8,128)S(1)}, f32[2,8,128]{2,1,0:T(8,128)S(1)}, f32[8,128]{1,0:T(8,128)S(1)}, f32[2,8,128]{2,1,0:T(8,128)S(1)}) custom-call(f32[14,48,128]{2,1,0:T(8,128)S(1)} %collective-permute-done.6.from_first, f32[14,48,128]{2,1,0:T(8,128)S(1)} %collective-permute-done.7.from_second, ...), custom_call_target="tpu_custom_call" | custom-call | tf_op jit(solution)/shard_map/coarse_outer/pallas_call | solution.py:580
  37.1 0.0 collective-permute-start.8
  37.1 1.5 %collective-permute-start.9 = (f32[8,128]{1,0:T(8,128)S(1)}, f32[8,128]{1,0:T(8,128)S(1)}, u32[]{:S(2)}, u32[]{:S(2)}) collective-permute-start(f32[8,128]{1,0:T(8,128)S(1)} %get-tuple-element.66.own), channel_id=1, source_target_pairs={{1,0},{2,1},{3,2},{4,3},{5,4},{6,5},{7,6},{8,7},{9,8},{10,9},{11,1... | collective-permute-start | bytes 12296 | tf_op jit(solution)/shard_map/ppermute | solution.py:509
  38.6 1.0 %unfold.1 = (f32[16,16,64]{2,1,0:T(8,128)}, f32[8,8,32]{2,1,0:T(8,128)}, f32[4,4,16]{2,1,0:T(4,128)}) custom-call(f32[8,16,128]{2,1,0:T(8,128)S(1)} %get-tuple-element.67.own1, f32[4,8,128]{2,1,0:T(8,128)S(1)} %get-tuple-element.68.own2, f32[2,8,128]{2,1,0:T(8,128)S(1)} %get-tuple-element.69.own3), custom_call_target="tpu_custom_call" | custom-call | flops 2000000 | bytes 2000000 | tf_op jit(solution)/shard_map/unfold/pallas_call | solution.py:587
  39.5 0.0 collective-permute-done.8.from_first
  39.6 0.1 collective-permute-done.9.from_second
  39.7 4.3 %collective-permute-start.10 = (f32[8,128]{1,0:T(8,128)S(1)}, f32[8,128]{1,0:T(8,128)S(1)}, u32[]{:S(2)}, u32[]{:S(2)}) collective-permute-start(f32[8,128]{1,0:T(8,128)S(1)} %pack_last.1.own), channel_id=1, source_target_pairs={{0,16},{1,0},{2,18},{3,2},{4,20},{5,4},{6,22},{7,6},{8,24},{9,8},{... | collective-permute-start | bytes 12296 | tf_op jit(solution)/shard_map/ppermute | solution.py:509
  44.0 0.0 collective-permute-start.11
  44.0 0.8 %collective-permute-done.10.from_first = f32[8,128]{1,0:T(8,128)S(1)} collective-permute-done((f32[8,128]{1,0:T(8,128)S(1)}, f32[8,128]{1,0:T(8,128)S(1)}, u32[]{:S(2)}, u32[]{:S(2)}) %collective-permute-start.10) | collective-permute-done | bytes 4128 | tf_op jit(solution)/shard_map/ppermute | solution.py:509
  44.7 3.5 %collective-permute-done.11.from_second = f32[8,128]{1,0:T(8,128)S(1)} collective-permute-done((f32[8,128]{1,0:T(8,128)S(1)}, f32[8,128]{1,0:T(8,128)S(1)}, u32[]{:S(2)}, u32[]{:S(2)}) %collective-permute-start.11) | collective-permute-done | bytes 4128 | tf_op jit(solution)/shard_map/ppermute | solution.py:509
  48.2 1.0 %last.1 = (f32[2,2,8]{2,1,0:T(2,128)}, f32[2,2,8]{2,1,0:T(2,128)}) custom-call(f32[8,128]{1,0:T(8,128)S(1)} %pack_last.1.own, f32[8,128]{1,0:T(8,128)S(1)} %collective-permute-done.10.from_first, f32[8,128]{1,0:T(8,128)S(1)} %collective-permute-done.11.from_second, f32[2,8,128]{2,1,0:T(8,128)S(1)} %get-tuple-element.77.k4), custom_call_target="tpu_custom_call" | custom-call | tf_op jit(solution)/shard_map/last/pallas_call | solution.py:594
  (7 shorter events, 0.2 us)
Async XLA Ops:
  2.0 4.4 %collective-permute-start = (f32[32,8,128]{2,1,0:T(8,128)S(1)}, f32[32,8,128]{2,1,0:T(8,128)S(1)}, u32[]{:S(2)}, u32[]{:S(2)}) collective-permute-start(f32[32,8,128]{2,1,0:T(8,128)S(1)} %get-tuple-element.43.own_first), channel_id=1, source_target_pairs={{0,1},{1,2},{2,3},{3,4},{4,5},{5,6},{6,7},{7,8},{8,9},{9,10},{10,1... | collective-permute-start | bytes 393224 | tf_op jit(solution)/shard_map/ppermute | solution.py:509
  2.4 4.1 %collective-permute-start.1 = (f32[32,8,128]{2,1,0:T(8,128)S(1)}, f32[32,8,128]{2,1,0:T(8,128)S(1)}, u32[]{:S(2)}, u32[]{:S(2)}) collective-permute-start(f32[32,8,128]{2,1,0:T(8,128)S(1)} %get-tuple-element.44.own_second), channel_id=1, source_target_pairs={{1,0},{2,1},{3,2},{4,3},{5,4},{6,5},{7,6},{8,7},{9,8},{10,9},{11,1... | collective-permute-start | bytes 393224 | tf_op jit(solution)/shard_map/ppermute | solution.py:509
  6.5 8.7 %collective-permute-start.2 = (f32[7,40,128]{2,1,0:T(8,128)S(1)}, f32[7,40,128]{2,1,0:T(8,128)S(1)}, u32[]{:S(2)}, u32[]{:S(2)}) collective-permute-start(f32[7,40,128]{2,1,0:T(8,128)S(1)} %get-tuple-element.48), channel_id=1, source_target_pairs={{0,16},{1,0},{2,18},{3,2},{4,20},{5,4},{6,22},{7,6},{8,24},{9,8},{... | collective-permute-start | bytes 430088 | tf_op jit(solution)/shard_map/ppermute | solution.py:509
  11.8 5.7 %collective-permute-start.3 = (f32[7,40,128]{2,1,0:T(8,128)S(1)}, f32[7,40,128]{2,1,0:T(8,128)S(1)}, u32[]{:S(2)}, u32[]{:S(2)}) collective-permute-start(f32[7,40,128]{2,1,0:T(8,128)S(1)} %get-tuple-element.49), channel_id=1, source_target_pairs={{16,0},{0,1},{18,2},{2,3},{20,4},{4,5},{22,6},{6,7},{24,8},{8,9},{... | collective-permute-start | bytes 430088 | tf_op jit(solution)/shard_map/ppermute | solution.py:509
  18.1 3.9 %collective-permute-start.4 = (f32[16,16,128]{2,1,0:T(8,128)S(1)}, f32[16,16,128]{2,1,0:T(8,128)S(1)}, u32[]{:S(2)}, u32[]{:S(2)}) collective-permute-start(f32[16,16,128]{2,1,0:T(8,128)S(1)} %get-tuple-element.57.own), channel_id=1, source_target_pairs={{0,1},{1,2},{2,3},{3,4},{4,5},{5,6},{6,7},{7,8},{8,9},{9,10},{10,1... | collective-permute-start | bytes 393224 | tf_op jit(solution)/shard_map/ppermute | solution.py:509
  18.1 3.9 %collective-permute-start.5 = (f32[16,16,128]{2,1,0:T(8,128)S(1)}, f32[16,16,128]{2,1,0:T(8,128)S(1)}, u32[]{:S(2)}, u32[]{:S(2)}) collective-permute-start(f32[16,16,128]{2,1,0:T(8,128)S(1)} %get-tuple-element.57.own), channel_id=1, source_target_pairs={{1,0},{2,1},{3,2},{4,3},{5,4},{6,5},{7,6},{8,7},{9,8},{10,9},{11,1... | collective-permute-start | bytes 393224 | tf_op jit(solution)/shard_map/ppermute | solution.py:509
  22.1 9.9 %collective-permute-start.6 = (f32[14,48,128]{2,1,0:T(8,128)S(1)}, f32[14,48,128]{2,1,0:T(8,128)S(1)}, u32[]{:S(2)}, u32[]{:S(2)}) collective-permute-start(f32[14,48,128]{2,1,0:T(8,128)S(1)} %get-tuple-element.81), channel_id=1, source_target_pairs={{0,16},{1,0},{2,18},{3,2},{4,20},{5,4},{6,22},{7,6},{8,24},{9,8},{... | collective-permute-start | bytes 1032200 | tf_op jit(solution)/shard_map/ppermute | solution.py:509
  27.9 7.9 %collective-permute-start.7 = (f32[14,48,128]{2,1,0:T(8,128)S(1)}, f32[14,48,128]{2,1,0:T(8,128)S(1)}, u32[]{:S(2)}, u32[]{:S(2)}) collective-permute-start(f32[14,48,128]{2,1,0:T(8,128)S(1)} %get-tuple-element.80), channel_id=1, source_target_pairs={{16,0},{0,1},{18,2},{2,3},{20,4},{4,5},{22,6},{6,7},{24,8},{8,9},{... | collective-permute-start | bytes 1032200 | tf_op jit(solution)/shard_map/ppermute | solution.py:509
  37.1 2.5 %collective-permute-start.8 = (f32[8,128]{1,0:T(8,128)S(1)}, f32[8,128]{1,0:T(8,128)S(1)}, u32[]{:S(2)}, u32[]{:S(2)}) collective-permute-start(f32[8,128]{1,0:T(8,128)S(1)} %get-tuple-element.66.own), channel_id=1, source_target_pairs={{0,1},{1,2},{2,3},{3,4},{4,5},{5,6},{6,7},{7,8},{8,9},{9,10},{10,1... | collective-permute-start | bytes 12296 | tf_op jit(solution)/shard_map/ppermute | solution.py:509
  37.1 2.5 %collective-permute-start.9 = (f32[8,128]{1,0:T(8,128)S(1)}, f32[8,128]{1,0:T(8,128)S(1)}, u32[]{:S(2)}, u32[]{:S(2)}) collective-permute-start(f32[8,128]{1,0:T(8,128)S(1)} %get-tuple-element.66.own), channel_id=1, source_target_pairs={{1,0},{2,1},{3,2},{4,3},{5,4},{6,5},{7,6},{8,7},{9,8},{10,9},{11,1... | collective-permute-start | bytes 12296 | tf_op jit(solution)/shard_map/ppermute | solution.py:509
  39.7 5.1 %collective-permute-start.10 = (f32[8,128]{1,0:T(8,128)S(1)}, f32[8,128]{1,0:T(8,128)S(1)}, u32[]{:S(2)}, u32[]{:S(2)}) collective-permute-start(f32[8,128]{1,0:T(8,128)S(1)} %pack_last.1.own), channel_id=1, source_target_pairs={{0,16},{1,0},{2,18},{3,2},{4,20},{5,4},{6,22},{7,6},{8,24},{9,8},{... | collective-permute-start | bytes 12296 | tf_op jit(solution)/shard_map/ppermute | solution.py:509
  44.0 4.2 %collective-permute-start.11 = (f32[8,128]{1,0:T(8,128)S(1)}, f32[8,128]{1,0:T(8,128)S(1)}, u32[]{:S(2)}, u32[]{:S(2)}) collective-permute-start(f32[8,128]{1,0:T(8,128)S(1)} %pack_last.1.own), channel_id=1, source_target_pairs={{16,0},{0,1},{18,2},{2,3},{20,4},{4,5},{22,6},{6,7},{24,8},{8,9},{... | collective-permute-start | bytes 12296 | tf_op jit(solution)/shard_map/ppermute | solution.py:509

commit v7 on v6

--- a/solution.py
+++ b/solution.py
@@ -45,12 +45,11 @@
 
 
 def across_of(axis):
-    return ("box", 2) if axis == "agg" else ("agg", 1)
+    return "box" if axis == "agg" else "agg"
 
 
 def moves_up(axis):
-    name, width = across_of(axis)
-    return lax.axis_index(name) // width % 2 == 0
+    return lax.axis_index(across_of(axis)) % 2 == 0
 
 
 def in_order(axis, first, second):
@@ -494,16 +493,15 @@
 def exchanged(first, second, axis):
     names = ("box", "agg")
     along = names.index(axis)
-    across, width = across_of(axis)
     sizes = [lax.axis_size(name) for name in names]
     route = []
     for source in range(sizes[0] * sizes[1]):
         at = list(divmod(source, sizes[1]))
-        step = 1 if at[names.index(across)] // width % 2 == 0 else -1
+        step = 1 if at[1 - along] % 2 == 0 else -1
         if 0 <= at[along] + step < sizes[along]:
             at[along] += step
         else:
-            at[1 - along] += step * width
+            at[1 - along] += step
         route.append((source, at[0] * sizes[1] + at[1]))
     inverse = [(target, source) for source, target in route]
     return lax.ppermute(first, names, route), lax.ppermute(second, names, inverse)

time: 49.4 us -> 48.2 us (0.976)
  starting transfers between devices: 19.9 us -> 16.7 us
  waiting for transfers between devices: 18.5 us -> 20.5 us
    ppermute x6, starting transfers between devices: 15.7 us -> 12.6 us  [exchanged(): lax.ppermute(first, names, route)]
    ppermute x6, waiting for transfers between devices: 8.8 us -> 10.1 us  [exchanged(): lax.ppermute(first, names, route)]
    ppermute x6, waiting for transfers between devices: 9.71 us -> 10.4 us  [exchanged(): lax.ppermute(second, names, inverse)]
where the time goes in v7:
time: 48.2 us; the launch traced here: 48.1 us
  waiting for transfers between devices  20.5 us (43%)
  starting transfers between devices  16.7 us (35%)
  Pallas kernels  9.18 us (19%)
  other arithmetic  0.93 us (2%)
  between operations  0.72 us (1%)
    ppermute x6, starting transfers between devices, exchanged(): lax.ppermute(first, names, route)  12.6 us
    ppermute x6, waiting for transfers between devices, exchanged(): lax.ppermute(second, names, inverse)  10.4 us
    ppermute x6, waiting for transfers between devices, exchanged(): lax.ppermute(first, names, route)  10.1 us
    ppermute x6, starting transfers between devices, exchanged(): lax.ppermute(second, names, inverse)  4.12 us
    pallas_call x1, Pallas kernels, per_device(): call(fine_inner, [big] * 6 + [(16, 16, LANES)], [VMEM] * 3 + [HBM] * 3, s...  3.32 us
    pallas_call x1, Pallas kernels, per_device(): call(pack_rows, [tile, tile, (7, 32, LANES), (7, 32, LANES)], [HBM] * 4,...  1.4 us
    pallas_call x1, Pallas kernels, per_device(): call(coarse_outer, [(8, 16, LANES), (4, 8, LANES), (2, 8, LANES), (8, LAN...  1.33 us
    pallas_call x1, Pallas kernels, per_device(): call(last_kernel, [(2, 2, 8), (2, 2, 8)], [VMEM] * 4, name='last')  1.03 us
  transfers between devices with their start and end apart: 12, of which 9 were waited for; matrix products, arithmetic and copies ran while one was open for 2% of the time, Pallas kernels for 10%

profile of v7, /device:TPU:101, one launch (start us, length us, event | category | flops | bytes accessed | tf_op | source)
XLA Modules:
  0.0 48.1 jit_solution(18254620406199685689)
XLA Ops:
  0.6 1.4 %pack_rows.1 = (f32[32,8,128]{2,1,0:T(8,128)S(1)}, f32[32,8,128]{2,1,0:T(8,128)S(1)}, f32[7,32,128]{2,1,0:T(8,128)S(1)}, f32[7,32,128]{2,1,0:T(8,128)S(1)}) custom-call(s32[1,1,4]{2,1,0:T(1,128)} %flags.1, f32[32,32,128]{2,1,0:T(8,128)} %guess.3, f32[32,32,128]{2,1,0:T(8,128)} %source.3, f32[32,32,128]{2,1,0:T(8,128)} %reaction.3), custom_call_target="tpu_custom_call" | custom-call | tf_op jit(solution)/shard_map/pack_rows/pallas_call | solution.py:533
  2.0 0.3 collective-permute-start
  2.4 1.2 %collective-permute-start.1 = (f32[32,8,128]{2,1,0:T(8,128)S(1)}, f32[32,8,128]{2,1,0:T(8,128)S(1)}, u32[]{:S(2)}, u32[]{:S(2)}) collective-permute-start(f32[32,8,128]{2,1,0:T(8,128)S(1)} %get-tuple-element.44.own_second), channel_id=1, source_target_pairs={{1,0},{2,1},{3,2},{4,3},{5,4},{6,5},{7,6},{8,7},{9,8},{10,9},{11,1... | collective-permute-start | bytes 393224 | tf_op jit(solution)/shard_map/ppermute | solution.py:507
  3.6 2.6 %collective-permute-done.from_first = f32[32,8,128]{2,1,0:T(8,128)S(1)} collective-permute-done((f32[32,8,128]{2,1,0:T(8,128)S(1)}, f32[32,8,128]{2,1,0:T(8,128)S(1)}, u32[]{:S(2)}, u32[]{:S(2)}) %collective-permute-start) | collective-permute-done | bytes 131104 | tf_op jit(solution)/shard_map/ppermute | solution.py:507
  6.2 0.8 %collective-permute-done.1.from_second = f32[32,8,128]{2,1,0:T(8,128)S(1)} collective-permute-done((f32[32,8,128]{2,1,0:T(8,128)S(1)}, f32[32,8,128]{2,1,0:T(8,128)S(1)}, u32[]{:S(2)}, u32[]{:S(2)}) %collective-permute-start.1) | collective-permute-done | bytes 131104 | tf_op jit(solution)/shard_map/ppermute | solution.py:507
  7.1 4.8 %collective-permute-start.2 = (f32[7,40,128]{2,1,0:T(8,128)S(1)}, f32[7,40,128]{2,1,0:T(8,128)S(1)}, u32[]{:S(2)}, u32[]{:S(2)}) collective-permute-start(f32[7,40,128]{2,1,0:T(8,128)S(1)} %get-tuple-element.48), channel_id=1, source_target_pairs={{0,16},{1,0},{2,18},{3,2},{4,20},{5,4},{6,22},{7,6},{8,24},{9,8},{... | collective-permute-start | bytes 430088 | tf_op jit(solution)/shard_map/ppermute | solution.py:507
  11.8 0.0 collective-permute-start.3
  11.8 3.3 %fine_inner.1 = (f32[32,40,128]{2,1,0:T(8,128)S(1)}, f32[32,40,128]{2,1,0:T(8,128)S(1)}, f32[32,40,128]{2,1,0:T(8,128)S(1)}, f32[32,40,128]{2,1,0:T(8,128)S(1)},...) custom-call(f32[40,128]{1,0:T(8,128)S(1)} %get-tuple-element.47.mask_ref, ...), custom_call_target="tpu_custom_call" | custom-call | flops 8000000 | bytes 8000000 | tf_op jit(solution)/shard_map/fine_inner/pallas_call | solution.py:547
  15.2 0.0 collective-permute-done.2.from_first
  15.2 2.3 %collective-permute-done.3.from_second = f32[7,40,128]{2,1,0:T(8,128)S(1)} collective-permute-done((f32[7,40,128]{2,1,0:T(8,128)S(1)}, f32[7,40,128]{2,1,0:T(8,128)S(1)}, u32[]{:S(2)}, u32[]{:S(2)}) %collective-permute-start.3) | collective-permute-done | bytes 143392 | tf_op jit(solution)/shard_map/ppermute | solution.py:507
  17.6 0.5 %fine_outer.1 = (f32[16,16,128]{2,1,0:T(8,128)S(1)}, f32[4,32,128]{2,1,0:T(8,128)S(1)}) custom-call(f32[40,128]{1,0:T(8,128)S(1)} %get-tuple-element.47.mask_ref, f32[7,40,128]{2,1,0:T(8,128)S(1)} %collective-permute-done.2.from_first, f32[7,40,128]{2,1,0:T(8,128)S(1)} %collective-permute-done.3.from_second, f32[32,40,128]{2,1,0:T(8,128)S(1)} %get-tuple-element.50.g, ...), custom_call_target="tpu_custom_call" | custom-call | tf_op jit(solution)/shard_map/fine_outer/pallas_call | solution.py:556
  18.1 0.1 collective-permute-start.4
  18.2 1.5 %collective-permute-start.5 = (f32[16,16,128]{2,1,0:T(8,128)S(1)}, f32[16,16,128]{2,1,0:T(8,128)S(1)}, u32[]{:S(2)}, u32[]{:S(2)}) collective-permute-start(f32[16,16,128]{2,1,0:T(8,128)S(1)} %get-tuple-element.57.own), channel_id=1, source_target_pairs={{1,0},{2,1},{3,2},{4,3},{5,4},{6,5},{7,6},{8,7},{9,8},{10,9},{11,1... | collective-permute-start | bytes 393224 | tf_op jit(solution)/shard_map/ppermute | solution.py:507
  19.6 0.8 %pad_maximum_fusion = f32[32,32,128]{2,1,0:T(8,128)} fusion(f32[2,32,128]{2,1,0:T(8,128)S(1)} %get-tuple-element.85, f32[28,32,128]{2,1,0:T(8,128)S(1)} %slice.16, f32[2,32,128]{2,1,0:T(8,128)S(1)} %get-tuple-element.84), kind=kLoop, calls=%fused_computation | loop fusion | flops 262144 | bytes 1048576 | tf_op jit(solution)/shard_map/concatenate | solution.py:563
  20.4 3.0 %collective-permute-done.4 = f32[16,16,128]{2,1,0:T(8,128)S(1)} collective-permute-done((f32[16,16,128]{2,1,0:T(8,128)S(1)}, f32[16,16,128]{2,1,0:T(8,128)S(1)}, u32[]{:S(2)}, u32[]{:S(2)}) %collective-permute-start.4) | collective-permute-done | bytes 131104 | tf_op jit(solution)/shard_map/ppermute | solution.py:507
  23.5 0.0 collective-permute-done.5
  23.6 3.4 %collective-permute-start.6 = (f32[14,48,128]{2,1,0:T(8,128)S(1)}, f32[14,48,128]{2,1,0:T(8,128)S(1)}, u32[]{:S(2)}, u32[]{:S(2)}) collective-permute-start(f32[14,48,128]{2,1,0:T(8,128)S(1)} %get-tuple-element.81), channel_id=1, source_target_pairs={{0,16},{1,0},{2,18},{3,2},{4,20},{5,4},{6,22},{7,6},{8,24},{9,8},{... | collective-permute-start | bytes 1032200 | tf_op jit(solution)/shard_map/ppermute | solution.py:507
  27.0 0.0 collective-permute-start.7
  27.0 0.6 %coarse_inner.1 = (f32[2,48,128]{2,1,0:T(8,128)S(1)}, f32[2,48,128]{2,1,0:T(8,128)S(1)}, f32[8,48,128]{2,1,0:T(8,128)S(1)}, f32[3,24,128]{2,1,0:T(8,128)S(1)}, f32[3,24,128]{2,1,0:T(8,128)S(1)}) custom-call(f32[16,16,128]{2,1,0:T(8,128)S(1)} %get-tuple-element.82.y_before, f32[16,16,128]{2,1,0:T(8,128)S(1)} %get-tuple-element.57.own, ...), custom_call_target="tpu_custom_call" | custom-call | flops 4000000 | bytes 4000000 | tf_op jit(solution)/shard_map/coarse_inner/pallas_call | solution.py:570
  27.6 3.6 %collective-permute-done.6.from_first = f32[14,48,128]{2,1,0:T(8,128)S(1)} collective-permute-done((f32[14,48,128]{2,1,0:T(8,128)S(1)}, f32[14,48,128]{2,1,0:T(8,128)S(1)}, u32[]{:S(2)}, u32[]{:S(2)}) %collective-permute-start.6) | collective-permute-done | bytes 344096 | tf_op jit(solution)/shard_map/ppermute | solution.py:507
  31.2 3.7 %collective-permute-done.7.from_second = f32[14,48,128]{2,1,0:T(8,128)S(1)} collective-permute-done((f32[14,48,128]{2,1,0:T(8,128)S(1)}, f32[14,48,128]{2,1,0:T(8,128)S(1)}, u32[]{:S(2)}, u32[]{:S(2)}) %collective-permute-start.7) | collective-permute-done | bytes 344096 | tf_op jit(solution)/shard_map/ppermute | solution.py:507
  34.9 1.3 %coarse_outer.1 = (f32[8,16,128]{2,1,0:T(8,128)S(1)}, f32[4,8,128]{2,1,0:T(8,128)S(1)}, f32[2,8,128]{2,1,0:T(8,128)S(1)}, f32[8,128]{1,0:T(8,128)S(1)}, f32[2,8,128]{2,1,0:T(8,128)S(1)}) custom-call(f32[14,48,128]{2,1,0:T(8,128)S(1)} %collective-permute-done.6.from_first, f32[14,48,128]{2,1,0:T(8,128)S(1)} %collective-permute-done.7.from_second, ...), custom_call_target="tpu_custom_call" | custom-call | tf_op jit(solution)/shard_map/coarse_outer/pallas_call | solution.py:578
  36.2 0.0 collective-permute-start.8
  36.2 1.5 %collective-permute-start.9 = (f32[8,128]{1,0:T(8,128)S(1)}, f32[8,128]{1,0:T(8,128)S(1)}, u32[]{:S(2)}, u32[]{:S(2)}) collective-permute-start(f32[8,128]{1,0:T(8,128)S(1)} %get-tuple-element.66.own), channel_id=1, source_target_pairs={{1,0},{2,1},{3,2},{4,3},{5,4},{6,5},{7,6},{8,7},{9,8},{10,9},{11,1... | collective-permute-start | bytes 12296 | tf_op jit(solution)/shard_map/ppermute | solution.py:507
  37.7 1.0 %unfold.1 = (f32[16,16,64]{2,1,0:T(8,128)}, f32[8,8,32]{2,1,0:T(8,128)}, f32[4,4,16]{2,1,0:T(4,128)}) custom-call(f32[8,16,128]{2,1,0:T(8,128)S(1)} %get-tuple-element.67.own1, f32[4,8,128]{2,1,0:T(8,128)S(1)} %get-tuple-element.68.own2, f32[2,8,128]{2,1,0:T(8,128)S(1)} %get-tuple-element.69.own3), custom_call_target="tpu_custom_call" | custom-call | flops 2000000 | bytes 2000000 | tf_op jit(solution)/shard_map/unfold/pallas_call | solution.py:585
  38.7 0.0 collective-permute-done.8.from_first
  38.7 0.1 collective-permute-done.9.from_second
  38.8 4.0 %collective-permute-start.10 = (f32[8,128]{1,0:T(8,128)S(1)}, f32[8,128]{1,0:T(8,128)S(1)}, u32[]{:S(2)}, u32[]{:S(2)}) collective-permute-start(f32[8,128]{1,0:T(8,128)S(1)} %pack_last.1.own), channel_id=1, source_target_pairs={{0,16},{1,0},{2,18},{3,2},{4,20},{5,4},{6,22},{7,6},{8,24},{9,8},{... | collective-permute-start | bytes 12296 | tf_op jit(solution)/shard_map/ppermute | solution.py:507
  42.8 0.0 collective-permute-start.11
  42.8 0.8 %collective-permute-done.10.from_first = f32[8,128]{1,0:T(8,128)S(1)} collective-permute-done((f32[8,128]{1,0:T(8,128)S(1)}, f32[8,128]{1,0:T(8,128)S(1)}, u32[]{:S(2)}, u32[]{:S(2)}) %collective-permute-start.10) | collective-permute-done | bytes 4128 | tf_op jit(solution)/shard_map/ppermute | solution.py:507
  43.6 3.5 %collective-permute-done.11.from_second = f32[8,128]{1,0:T(8,128)S(1)} collective-permute-done((f32[8,128]{1,0:T(8,128)S(1)}, f32[8,128]{1,0:T(8,128)S(1)}, u32[]{:S(2)}, u32[]{:S(2)}) %collective-permute-start.11) | collective-permute-done | bytes 4128 | tf_op jit(solution)/shard_map/ppermute | solution.py:507
  47.0 1.0 %last.1 = (f32[2,2,8]{2,1,0:T(2,128)}, f32[2,2,8]{2,1,0:T(2,128)}) custom-call(f32[8,128]{1,0:T(8,128)S(1)} %pack_last.1.own, f32[8,128]{1,0:T(8,128)S(1)} %collective-permute-done.10.from_first, f32[8,128]{1,0:T(8,128)S(1)} %collective-permute-done.11.from_second, f32[2,8,128]{2,1,0:T(8,128)S(1)} %get-tuple-element.77.k4), custom_call_target="tpu_custom_call" | custom-call | tf_op jit(solution)/shard_map/last/pallas_call | solution.py:592
  (7 shorter events, 0.2 us)
Async XLA Ops:
  2.0 4.2 %collective-permute-start = (f32[32,8,128]{2,1,0:T(8,128)S(1)}, f32[32,8,128]{2,1,0:T(8,128)S(1)}, u32[]{:S(2)}, u32[]{:S(2)}) collective-permute-start(f32[32,8,128]{2,1,0:T(8,128)S(1)} %get-tuple-element.43.own_first), channel_id=1, source_target_pairs={{0,1},{1,2},{2,3},{3,4},{4,5},{5,6},{6,7},{7,8},{8,9},{9,10},{10,1... | collective-permute-start | bytes 393224 | tf_op jit(solution)/shard_map/ppermute | solution.py:507
  2.4 4.7 %collective-permute-start.1 = (f32[32,8,128]{2,1,0:T(8,128)S(1)}, f32[32,8,128]{2,1,0:T(8,128)S(1)}, u32[]{:S(2)}, u32[]{:S(2)}) collective-permute-start(f32[32,8,128]{2,1,0:T(8,128)S(1)} %get-tuple-element.44.own_second), channel_id=1, source_target_pairs={{1,0},{2,1},{3,2},{4,3},{5,4},{6,5},{7,6},{8,7},{9,8},{10,9},{11,1... | collective-permute-start | bytes 393224 | tf_op jit(solution)/shard_map/ppermute | solution.py:507
  7.1 8.2 %collective-permute-start.2 = (f32[7,40,128]{2,1,0:T(8,128)S(1)}, f32[7,40,128]{2,1,0:T(8,128)S(1)}, u32[]{:S(2)}, u32[]{:S(2)}) collective-permute-start(f32[7,40,128]{2,1,0:T(8,128)S(1)} %get-tuple-element.48), channel_id=1, source_target_pairs={{0,16},{1,0},{2,18},{3,2},{4,20},{5,4},{6,22},{7,6},{8,24},{9,8},{... | collective-permute-start | bytes 430088 | tf_op jit(solution)/shard_map/ppermute | solution.py:507
  11.8 5.7 %collective-permute-start.3 = (f32[7,40,128]{2,1,0:T(8,128)S(1)}, f32[7,40,128]{2,1,0:T(8,128)S(1)}, u32[]{:S(2)}, u32[]{:S(2)}) collective-permute-start(f32[7,40,128]{2,1,0:T(8,128)S(1)} %get-tuple-element.49), channel_id=1, source_target_pairs={{16,0},{0,1},{18,2},{2,3},{20,4},{4,5},{22,6},{6,7},{24,8},{8,9},{... | collective-permute-start | bytes 430088 | tf_op jit(solution)/shard_map/ppermute | solution.py:507
  18.1 5.4 %collective-permute-start.4 = (f32[16,16,128]{2,1,0:T(8,128)S(1)}, f32[16,16,128]{2,1,0:T(8,128)S(1)}, u32[]{:S(2)}, u32[]{:S(2)}) collective-permute-start(f32[16,16,128]{2,1,0:T(8,128)S(1)} %get-tuple-element.57.own), channel_id=1, source_target_pairs={{0,1},{1,2},{2,3},{3,4},{4,5},{5,6},{6,7},{7,8},{8,9},{9,10},{10,1... | collective-permute-start | bytes 393224 | tf_op jit(solution)/shard_map/ppermute | solution.py:507
  18.2 5.3 %collective-permute-start.5 = (f32[16,16,128]{2,1,0:T(8,128)S(1)}, f32[16,16,128]{2,1,0:T(8,128)S(1)}, u32[]{:S(2)}, u32[]{:S(2)}) collective-permute-start(f32[16,16,128]{2,1,0:T(8,128)S(1)} %get-tuple-element.57.own), channel_id=1, source_target_pairs={{1,0},{2,1},{3,2},{4,3},{5,4},{6,5},{7,6},{8,7},{9,8},{10,9},{11,1... | collective-permute-start | bytes 393224 | tf_op jit(solution)/shard_map/ppermute | solution.py:507
  23.6 7.6 %collective-permute-start.6 = (f32[14,48,128]{2,1,0:T(8,128)S(1)}, f32[14,48,128]{2,1,0:T(8,128)S(1)}, u32[]{:S(2)}, u32[]{:S(2)}) collective-permute-start(f32[14,48,128]{2,1,0:T(8,128)S(1)} %get-tuple-element.81), channel_id=1, source_target_pairs={{0,16},{1,0},{2,18},{3,2},{4,20},{5,4},{6,22},{7,6},{8,24},{9,8},{... | collective-permute-start | bytes 1032200 | tf_op jit(solution)/shard_map/ppermute | solution.py:507
  27.0 7.9 %collective-permute-start.7 = (f32[14,48,128]{2,1,0:T(8,128)S(1)}, f32[14,48,128]{2,1,0:T(8,128)S(1)}, u32[]{:S(2)}, u32[]{:S(2)}) collective-permute-start(f32[14,48,128]{2,1,0:T(8,128)S(1)} %get-tuple-element.80), channel_id=1, source_target_pairs={{16,0},{0,1},{18,2},{2,3},{20,4},{4,5},{22,6},{6,7},{24,8},{8,9},{... | collective-permute-start | bytes 1032200 | tf_op jit(solution)/shard_map/ppermute | solution.py:507
  36.2 2.5 %collective-permute-start.8 = (f32[8,128]{1,0:T(8,128)S(1)}, f32[8,128]{1,0:T(8,128)S(1)}, u32[]{:S(2)}, u32[]{:S(2)}) collective-permute-start(f32[8,128]{1,0:T(8,128)S(1)} %get-tuple-element.66.own), channel_id=1, source_target_pairs={{0,1},{1,2},{2,3},{3,4},{4,5},{5,6},{6,7},{7,8},{8,9},{9,10},{10,1... | collective-permute-start | bytes 12296 | tf_op jit(solution)/shard_map/ppermute | solution.py:507
  36.2 2.5 %collective-permute-start.9 = (f32[8,128]{1,0:T(8,128)S(1)}, f32[8,128]{1,0:T(8,128)S(1)}, u32[]{:S(2)}, u32[]{:S(2)}) collective-permute-start(f32[8,128]{1,0:T(8,128)S(1)} %get-tuple-element.66.own), channel_id=1, source_target_pairs={{1,0},{2,1},{3,2},{4,3},{5,4},{6,5},{7,6},{8,7},{9,8},{10,9},{11,1... | collective-permute-start | bytes 12296 | tf_op jit(solution)/shard_map/ppermute | solution.py:507
  38.8 4.8 %collective-permute-start.10 = (f32[8,128]{1,0:T(8,128)S(1)}, f32[8,128]{1,0:T(8,128)S(1)}, u32[]{:S(2)}, u32[]{:S(2)}) collective-permute-start(f32[8,128]{1,0:T(8,128)S(1)} %pack_last.1.own), channel_id=1, source_target_pairs={{0,16},{1,0},{2,18},{3,2},{4,20},{5,4},{6,22},{7,6},{8,24},{9,8},{... | collective-permute-start | bytes 12296 | tf_op jit(solution)/shard_map/ppermute | solution.py:507
  42.8 4.2 %collective-permute-start.11 = (f32[8,128]{1,0:T(8,128)S(1)}, f32[8,128]{1,0:T(8,128)S(1)}, u32[]{:S(2)}, u32[]{:S(2)}) collective-permute-start(f32[8,128]{1,0:T(8,128)S(1)} %pack_last.1.own), channel_id=1, source_target_pairs={{16,0},{0,1},{18,2},{2,3},{20,4},{4,5},{22,6},{6,7},{24,8},{8,9},{... | collective-permute-start | bytes 12296 | tf_op jit(solution)/shard_map/ppermute | solution.py:507

commit v8 on v7

--- a/solution.py
+++ b/solution.py
@@ -97,7 +97,7 @@
 
 
 def pack_rows(
-    flags, guess, source, reaction, first, second, strip_up, strip_down,
+    flags, guess, source, reaction, first, second,
     flag_smem, guess_lo, guess_hi, source_lo, source_hi, reaction_lo, reaction_hi, sems,
 ):
     lo, hi = pl.ds(0, 8), pl.ds(24, 8)
@@ -110,14 +110,8 @@
         (source.at[:, hi, :], source_hi),
         (reaction.at[:, lo, :], reaction_lo),
         (reaction.at[:, hi, :], reaction_hi),
-        (guess.at[29:32], strip_up.at[0:3]),
-        (source.at[30:32], strip_up.at[3:5]),
-        (reaction.at[30:32], strip_up.at[5:7]),
-        (guess.at[0:3], strip_down.at[0:3]),
-        (source.at[0:2], strip_down.at[3:5]),
-        (reaction.at[0:2], strip_down.at[5:7]),
-    )
-    for copy in copies[:7]:
+    )
+    for copy in copies:
         copy.wait()
     boxes = flags.shape[2]
     lane = iota((8, LANES), 1)
@@ -145,7 +139,19 @@
         ),
     )
     first[...], second[...] = in_order("agg", up, down)
-    for copy in copies[7:]:
+
+
+def load_strips(after, guess, source, reaction, strip_up, strip_down, sems):
+    copies = copy_all(
+        sems,
+        (guess.at[29:32], strip_up.at[0:3]),
+        (source.at[30:32], strip_up.at[3:5]),
+        (reaction.at[30:32], strip_up.at[5:7]),
+        (guess.at[0:3], strip_down.at[0:3]),
+        (source.at[0:2], strip_down.at[3:5]),
+        (reaction.at[0:2], strip_down.at[5:7]),
+    )
+    for copy in copies:
         copy.wait()
 
 
@@ -530,14 +536,17 @@
     flags, guess, source, reaction = (
         pltpu.with_memory_space_constraint(v, pltpu.HBM) for v in (flags, guess, source, reaction)
     )
-    *packed, strip_up, strip_down = call(
+    packed = call(
         pack_rows,
-        [tile, tile, (7, 32, LANES), (7, 32, LANES)],
+        [tile, tile],
         [HBM] * 4,
         scratch=[pltpu.SMEM((1, 1, flags.shape[2]), jnp.int32)] + [tile] * 6,
-        copies=13,
+        copies=7,
         name="pack_rows",
     )(flags, guess, source, reaction)
+    strip_up, strip_down = call(
+        load_strips, [(7, 32, LANES)] * 2, [VMEM] + [HBM] * 3, copies=6, name="load_strips"
+    )(packed[0], guess, source, reaction)
     y_sides = exchanged(*packed, "agg")
     *packed, mask = call(
         pack_planes, [(7, 40, LANES)] * 2 + [(40, LANES)], [VMEM] * 6, name="pack_planes"

time: 48.2 us -> 48.2 us (level)
  waiting for transfers between devices: 20.5 us -> 19.6 us
  Pallas kernels: 9.18 us -> 10 us
    ppermute x6, waiting for transfers between devices: 10.1 us -> 9.14 us  [exchanged(): lax.ppermute(first, names, route)]
    pallas_call x1 -> x2, Pallas kernels: 1.4 us -> 2.25 us  [the longest x1 1.34 us: per_device(): call(pack_rows, [tile, tile], [HBM] * 4, scratch=[pltpu.SMEM((1, 1, flags...]
  transfers between devices with their start and end apart: 12 -> 12, of which waited for: 9 -> 9; matrix products, arithmetic and copies ran while one was open for 2% -> 2% of each run, Pallas kernels for 10% -> 12%
where the time goes in v8:
time: 48.2 us; the launch traced here: 48 us
  waiting for transfers between devices  19.6 us (41%)
  starting transfers between devices  16.7 us (35%)
  Pallas kernels  10 us (21%)
  other arithmetic  0.93 us (2%)
  between operations  0.73 us (2%)
    ppermute x6, starting transfers between devices, exchanged(): lax.ppermute(first, names, route)  12.6 us
    ppermute x6, waiting for transfers between devices, exchanged(): lax.ppermute(second, names, inverse)  10.4 us
    ppermute x6, waiting for transfers between devices, exchanged(): lax.ppermute(first, names, route)  9.14 us
    ppermute x6, starting transfers between devices, exchanged(): lax.ppermute(second, names, inverse)  4.12 us
    pallas_call x1, Pallas kernels, per_device(): call(fine_inner, [big] * 6 + [(16, 16, LANES)], [VMEM] * 3 + [HBM] * 3, s...  3.32 us
    pallas_call x1, Pallas kernels, per_device(): call(pack_rows, [tile, tile], [HBM] * 4, scratch=[pltpu.SMEM((1, 1, flags...  1.34 us
    pallas_call x1, Pallas kernels, per_device(): call(coarse_outer, [(8, 16, LANES), (4, 8, LANES), (2, 8, LANES), (8, LAN...  1.33 us
    pallas_call x1, Pallas kernels, per_device(): call(last_kernel, [(2, 2, 8), (2, 2, 8)], [VMEM] * 4, name='last')  1.03 us
  transfers between devices with their start and end apart: 12, of which 9 were waited for; matrix products, arithmetic and copies ran while one was open for 2% of the time, Pallas kernels for 12%

profile of v8, /device:TPU:101, one launch (start us, length us, event | category | flops | bytes accessed | tf_op | source)
XLA Modules:
  0.0 48.0 jit_solution(14235702798501353221)
XLA Ops:
  0.6 1.3 %pack_rows.1 = (f32[32,8,128]{2,1,0:T(8,128)S(1)}, f32[32,8,128]{2,1,0:T(8,128)S(1)}) custom-call(s32[1,1,4]{2,1,0:T(1,128)} %flags.1, f32[32,32,128]{2,1,0:T(8,128)} %guess.5, f32[32,32,128]{2,1,0:T(8,128)} %source.5, f32[32,32,128]{2,1,0:T(8,128)} %reaction.5), custom_call_target="tpu_custom_call" | custom-call | tf_op jit(solution)/shard_map/pack_rows/pallas_call | solution.py:539
  2.0 0.3 collective-permute-start
  2.3 1.2 %collective-permute-start.1 = (f32[32,8,128]{2,1,0:T(8,128)S(1)}, f32[32,8,128]{2,1,0:T(8,128)S(1)}, u32[]{:S(2)}, u32[]{:S(2)}) collective-permute-start(f32[32,8,128]{2,1,0:T(8,128)S(1)} %get-tuple-element.44.own_second), channel_id=1, source_target_pairs={{1,0},{2,1},{3,2},{4,3},{5,4},{6,5},{7,6},{8,7},{9,8},{10,9},{11,1... | collective-permute-start | bytes 393224 | tf_op jit(solution)/shard_map/ppermute | solution.py:513
  3.5 0.9 %load_strips.1 = (f32[7,32,128]{2,1,0:T(8,128)S(1)}, f32[7,32,128]{2,1,0:T(8,128)S(1)}) custom-call(f32[32,8,128]{2,1,0:T(8,128)S(1)} %get-tuple-element.43.after.own_first, f32[32,32,128]{2,1,0:T(8,128)} %guess.5, f32[32,32,128]{2,1,0:T(8,128)} %source.5, f32[32,32,128]{2,1,0:T(8,128)} %reaction.5), custom_call_target="tpu_custom_call" | custom-call | tf_op jit(solution)/shard_map/load_strips/pallas_call | solution.py:547
  4.4 1.7 %collective-permute-done.from_first = f32[32,8,128]{2,1,0:T(8,128)S(1)} collective-permute-done((f32[32,8,128]{2,1,0:T(8,128)S(1)}, f32[32,8,128]{2,1,0:T(8,128)S(1)}, u32[]{:S(2)}, u32[]{:S(2)}) %collective-permute-start) | collective-permute-done | bytes 131104 | tf_op jit(solution)/shard_map/ppermute | solution.py:513
  6.2 0.8 %collective-permute-done.1.from_second = f32[32,8,128]{2,1,0:T(8,128)S(1)} collective-permute-done((f32[32,8,128]{2,1,0:T(8,128)S(1)}, f32[32,8,128]{2,1,0:T(8,128)S(1)}, u32[]{:S(2)}, u32[]{:S(2)}) %collective-permute-start.1) | collective-permute-done | bytes 131104 | tf_op jit(solution)/shard_map/ppermute | solution.py:513
  7.0 4.8 %collective-permute-start.2 = (f32[7,40,128]{2,1,0:T(8,128)S(1)}, f32[7,40,128]{2,1,0:T(8,128)S(1)}, u32[]{:S(2)}, u32[]{:S(2)}) collective-permute-start(f32[7,40,128]{2,1,0:T(8,128)S(1)} %get-tuple-element.48), channel_id=1, source_target_pairs={{0,16},{1,0},{2,18},{3,2},{4,20},{5,4},{6,22},{7,6},{8,24},{9,8},{... | collective-permute-start | bytes 430088 | tf_op jit(solution)/shard_map/ppermute | solution.py:513
  11.8 0.0 collective-permute-start.3
  11.8 3.3 %fine_inner.1 = (f32[32,40,128]{2,1,0:T(8,128)S(1)}, f32[32,40,128]{2,1,0:T(8,128)S(1)}, f32[32,40,128]{2,1,0:T(8,128)S(1)}, f32[32,40,128]{2,1,0:T(8,128)S(1)},...) custom-call(f32[40,128]{1,0:T(8,128)S(1)} %get-tuple-element.47.mask_ref, ...), custom_call_target="tpu_custom_call" | custom-call | flops 8000000 | bytes 8000000 | tf_op jit(solution)/shard_map/fine_inner/pallas_call | solution.py:556
  15.2 0.0 collective-permute-done.2.from_first
  15.2 2.3 %collective-permute-done.3.from_second = f32[7,40,128]{2,1,0:T(8,128)S(1)} collective-permute-done((f32[7,40,128]{2,1,0:T(8,128)S(1)}, f32[7,40,128]{2,1,0:T(8,128)S(1)}, u32[]{:S(2)}, u32[]{:S(2)}) %collective-permute-start.3) | collective-permute-done | bytes 143392 | tf_op jit(solution)/shard_map/ppermute | solution.py:513
  17.5 0.5 %fine_outer.1 = (f32[16,16,128]{2,1,0:T(8,128)S(1)}, f32[4,32,128]{2,1,0:T(8,128)S(1)}) custom-call(f32[40,128]{1,0:T(8,128)S(1)} %get-tuple-element.47.mask_ref, f32[7,40,128]{2,1,0:T(8,128)S(1)} %collective-permute-done.2.from_first, f32[7,40,128]{2,1,0:T(8,128)S(1)} %collective-permute-done.3.from_second, f32[32,40,128]{2,1,0:T(8,128)S(1)} %get-tuple-element.50.g, ...), custom_call_target="tpu_custom_call" | custom-call | tf_op jit(solution)/shard_map/fine_outer/pallas_call | solution.py:565
  18.0 0.1 collective-permute-start.4
  18.1 1.5 %collective-permute-start.5 = (f32[16,16,128]{2,1,0:T(8,128)S(1)}, f32[16,16,128]{2,1,0:T(8,128)S(1)}, u32[]{:S(2)}, u32[]{:S(2)}) collective-permute-start(f32[16,16,128]{2,1,0:T(8,128)S(1)} %get-tuple-element.57.own), channel_id=1, source_target_pairs={{1,0},{2,1},{3,2},{4,3},{5,4},{6,5},{7,6},{8,7},{9,8},{10,9},{11,1... | collective-permute-start | bytes 393224 | tf_op jit(solution)/shard_map/ppermute | solution.py:513
  19.6 0.8 %pad_maximum_fusion = f32[32,32,128]{2,1,0:T(8,128)} fusion(f32[2,32,128]{2,1,0:T(8,128)S(1)} %get-tuple-element.85, f32[28,32,128]{2,1,0:T(8,128)S(1)} %slice.16, f32[2,32,128]{2,1,0:T(8,128)S(1)} %get-tuple-element.84), kind=kLoop, calls=%fused_computation | loop fusion | flops 262144 | bytes 1048576 | tf_op jit(solution)/shard_map/concatenate | solution.py:572
  20.4 3.0 %collective-permute-done.4 = f32[16,16,128]{2,1,0:T(8,128)S(1)} collective-permute-done((f32[16,16,128]{2,1,0:T(8,128)S(1)}, f32[16,16,128]{2,1,0:T(8,128)S(1)}, u32[]{:S(2)}, u32[]{:S(2)}) %collective-permute-start.4) | collective-permute-done | bytes 131104 | tf_op jit(solution)/shard_map/ppermute | solution.py:513
  23.4 0.0 collective-permute-done.5
  23.5 3.4 %collective-permute-start.6 = (f32[14,48,128]{2,1,0:T(8,128)S(1)}, f32[14,48,128]{2,1,0:T(8,128)S(1)}, u32[]{:S(2)}, u32[]{:S(2)}) collective-permute-start(f32[14,48,128]{2,1,0:T(8,128)S(1)} %get-tuple-element.81), channel_id=1, source_target_pairs={{0,16},{1,0},{2,18},{3,2},{4,20},{5,4},{6,22},{7,6},{8,24},{9,8},{... | collective-permute-start | bytes 1032200 | tf_op jit(solution)/shard_map/ppermute | solution.py:513
  26.9 0.0 collective-permute-start.7
  26.9 0.6 %coarse_inner.1 = (f32[2,48,128]{2,1,0:T(8,128)S(1)}, f32[2,48,128]{2,1,0:T(8,128)S(1)}, f32[8,48,128]{2,1,0:T(8,128)S(1)}, f32[3,24,128]{2,1,0:T(8,128)S(1)}, f32[3,24,128]{2,1,0:T(8,128)S(1)}) custom-call(f32[16,16,128]{2,1,0:T(8,128)S(1)} %get-tuple-element.82.y_before, f32[16,16,128]{2,1,0:T(8,128)S(1)} %get-tuple-element.57.own, ...), custom_call_target="tpu_custom_call" | custom-call | flops 4000000 | bytes 4000000 | tf_op jit(solution)/shard_map/coarse_inner/pallas_call | solution.py:579
  27.5 3.6 %collective-permute-done.6.from_first = f32[14,48,128]{2,1,0:T(8,128)S(1)} collective-permute-done((f32[14,48,128]{2,1,0:T(8,128)S(1)}, f32[14,48,128]{2,1,0:T(8,128)S(1)}, u32[]{:S(2)}, u32[]{:S(2)}) %collective-permute-start.6) | collective-permute-done | bytes 344096 | tf_op jit(solution)/shard_map/ppermute | solution.py:513
  31.1 3.7 %collective-permute-done.7.from_second = f32[14,48,128]{2,1,0:T(8,128)S(1)} collective-permute-done((f32[14,48,128]{2,1,0:T(8,128)S(1)}, f32[14,48,128]{2,1,0:T(8,128)S(1)}, u32[]{:S(2)}, u32[]{:S(2)}) %collective-permute-start.7) | collective-permute-done | bytes 344096 | tf_op jit(solution)/shard_map/ppermute | solution.py:513
  34.8 1.3 %coarse_outer.1 = (f32[8,16,128]{2,1,0:T(8,128)S(1)}, f32[4,8,128]{2,1,0:T(8,128)S(1)}, f32[2,8,128]{2,1,0:T(8,128)S(1)}, f32[8,128]{1,0:T(8,128)S(1)}, f32[2,8,128]{2,1,0:T(8,128)S(1)}) custom-call(f32[14,48,128]{2,1,0:T(8,128)S(1)} %collective-permute-done.6.from_first, f32[14,48,128]{2,1,0:T(8,128)S(1)} %collective-permute-done.7.from_second, ...), custom_call_target="tpu_custom_call" | custom-call | tf_op jit(solution)/shard_map/coarse_outer/pallas_call | solution.py:587
  36.1 0.0 collective-permute-start.8
  36.2 1.5 %collective-permute-start.9 = (f32[8,128]{1,0:T(8,128)S(1)}, f32[8,128]{1,0:T(8,128)S(1)}, u32[]{:S(2)}, u32[]{:S(2)}) collective-permute-start(f32[8,128]{1,0:T(8,128)S(1)} %get-tuple-element.66.own), channel_id=1, source_target_pairs={{1,0},{2,1},{3,2},{4,3},{5,4},{6,5},{7,6},{8,7},{9,8},{10,9},{11,1... | collective-permute-start | bytes 12296 | tf_op jit(solution)/shard_map/ppermute | solution.py:513
  37.6 1.0 %unfold.1 = (f32[16,16,64]{2,1,0:T(8,128)}, f32[8,8,32]{2,1,0:T(8,128)}, f32[4,4,16]{2,1,0:T(4,128)}) custom-call(f32[8,16,128]{2,1,0:T(8,128)S(1)} %get-tuple-element.67.own1, f32[4,8,128]{2,1,0:T(8,128)S(1)} %get-tuple-element.68.own2, f32[2,8,128]{2,1,0:T(8,128)S(1)} %get-tuple-element.69.own3), custom_call_target="tpu_custom_call" | custom-call | flops 2000000 | bytes 2000000 | tf_op jit(solution)/shard_map/unfold/pallas_call | solution.py:594
  38.6 0.0 collective-permute-done.8.from_first
  38.6 0.1 collective-permute-done.9.from_second
  38.7 4.0 %collective-permute-start.10 = (f32[8,128]{1,0:T(8,128)S(1)}, f32[8,128]{1,0:T(8,128)S(1)}, u32[]{:S(2)}, u32[]{:S(2)}) collective-permute-start(f32[8,128]{1,0:T(8,128)S(1)} %pack_last.1.own), channel_id=1, source_target_pairs={{0,16},{1,0},{2,18},{3,2},{4,20},{5,4},{6,22},{7,6},{8,24},{9,8},{... | collective-permute-start | bytes 12296 | tf_op jit(solution)/shard_map/ppermute | solution.py:513
  42.7 0.8 %collective-permute-done.10.from_first = f32[8,128]{1,0:T(8,128)S(1)} collective-permute-done((f32[8,128]{1,0:T(8,128)S(1)}, f32[8,128]{1,0:T(8,128)S(1)}, u32[]{:S(2)}, u32[]{:S(2)}) %collective-permute-start.10) | collective-permute-done | bytes 4128 | tf_op jit(solution)/shard_map/ppermute | solution.py:513
  43.5 3.5 %collective-permute-done.11.from_second = f32[8,128]{1,0:T(8,128)S(1)} collective-permute-done((f32[8,128]{1,0:T(8,128)S(1)}, f32[8,128]{1,0:T(8,128)S(1)}, u32[]{:S(2)}, u32[]{:S(2)}) %collective-permute-start.11) | collective-permute-done | bytes 4128 | tf_op jit(solution)/shard_map/ppermute | solution.py:513
  47.0 1.0 %last.1 = (f32[2,2,8]{2,1,0:T(2,128)}, f32[2,2,8]{2,1,0:T(2,128)}) custom-call(f32[8,128]{1,0:T(8,128)S(1)} %pack_last.1.own, f32[8,128]{1,0:T(8,128)S(1)} %collective-permute-done.10.from_first, f32[8,128]{1,0:T(8,128)S(1)} %collective-permute-done.11.from_second, f32[2,8,128]{2,1,0:T(8,128)S(1)} %get-tuple-element.77.k4), custom_call_target="tpu_custom_call" | custom-call | tf_op jit(solution)/shard_map/last/pallas_call | solution.py:601
  (8 shorter events, 0.2 us)
Async XLA Ops:
  2.0 4.2 %collective-permute-start = (f32[32,8,128]{2,1,0:T(8,128)S(1)}, f32[32,8,128]{2,1,0:T(8,128)S(1)}, u32[]{:S(2)}, u32[]{:S(2)}) collective-permute-start(f32[32,8,128]{2,1,0:T(8,128)S(1)} %get-tuple-element.43.after.own_first), channel_id=1, source_target_pairs={{0,1},{1,2},{2,3},{3,4},{4,5},{5,6},{6,7},{7,8},{8,9},{9,10},{10,1... | collective-permute-start | bytes 393224 | tf_op jit(solution)/shard_map/ppermute | solution.py:513
  2.3 4.7 %collective-permute-start.1 = (f32[32,8,128]{2,1,0:T(8,128)S(1)}, f32[32,8,128]{2,1,0:T(8,128)S(1)}, u32[]{:S(2)}, u32[]{:S(2)}) collective-permute-start(f32[32,8,128]{2,1,0:T(8,128)S(1)} %get-tuple-element.44.own_second), channel_id=1, source_target_pairs={{1,0},{2,1},{3,2},{4,3},{5,4},{6,5},{7,6},{8,7},{9,8},{10,9},{11,1... | collective-permute-start | bytes 393224 | tf_op jit(solution)/shard_map/ppermute | solution.py:513
  7.0 8.2 %collective-permute-start.2 = (f32[7,40,128]{2,1,0:T(8,128)S(1)}, f32[7,40,128]{2,1,0:T(8,128)S(1)}, u32[]{:S(2)}, u32[]{:S(2)}) collective-permute-start(f32[7,40,128]{2,1,0:T(8,128)S(1)} %get-tuple-element.48), channel_id=1, source_target_pairs={{0,16},{1,0},{2,18},{3,2},{4,20},{5,4},{6,22},{7,6},{8,24},{9,8},{... | collective-permute-start | bytes 430088 | tf_op jit(solution)/shard_map/ppermute | solution.py:513
  11.8 5.7 %collective-permute-start.3 = (f32[7,40,128]{2,1,0:T(8,128)S(1)}, f32[7,40,128]{2,1,0:T(8,128)S(1)}, u32[]{:S(2)}, u32[]{:S(2)}) collective-permute-start(f32[7,40,128]{2,1,0:T(8,128)S(1)} %get-tuple-element.49), channel_id=1, source_target_pairs={{16,0},{0,1},{18,2},{2,3},{20,4},{4,5},{22,6},{6,7},{24,8},{8,9},{... | collective-permute-start | bytes 430088 | tf_op jit(solution)/shard_map/ppermute | solution.py:513
  18.0 5.4 %collective-permute-start.4 = (f32[16,16,128]{2,1,0:T(8,128)S(1)}, f32[16,16,128]{2,1,0:T(8,128)S(1)}, u32[]{:S(2)}, u32[]{:S(2)}) collective-permute-start(f32[16,16,128]{2,1,0:T(8,128)S(1)} %get-tuple-element.57.own), channel_id=1, source_target_pairs={{0,1},{1,2},{2,3},{3,4},{4,5},{5,6},{6,7},{7,8},{8,9},{9,10},{10,1... | collective-permute-start | bytes 393224 | tf_op jit(solution)/shard_map/ppermute | solution.py:513
  18.1 5.3 %collective-permute-start.5 = (f32[16,16,128]{2,1,0:T(8,128)S(1)}, f32[16,16,128]{2,1,0:T(8,128)S(1)}, u32[]{:S(2)}, u32[]{:S(2)}) collective-permute-start(f32[16,16,128]{2,1,0:T(8,128)S(1)} %get-tuple-element.57.own), channel_id=1, source_target_pairs={{1,0},{2,1},{3,2},{4,3},{5,4},{6,5},{7,6},{8,7},{9,8},{10,9},{11,1... | collective-permute-start | bytes 393224 | tf_op jit(solution)/shard_map/ppermute | solution.py:513
  23.5 7.6 %collective-permute-start.6 = (f32[14,48,128]{2,1,0:T(8,128)S(1)}, f32[14,48,128]{2,1,0:T(8,128)S(1)}, u32[]{:S(2)}, u32[]{:S(2)}) collective-permute-start(f32[14,48,128]{2,1,0:T(8,128)S(1)} %get-tuple-element.81), channel_id=1, source_target_pairs={{0,16},{1,0},{2,18},{3,2},{4,20},{5,4},{6,22},{7,6},{8,24},{9,8},{... | collective-permute-start | bytes 1032200 | tf_op jit(solution)/shard_map/ppermute | solution.py:513
  26.9 7.9 %collective-permute-start.7 = (f32[14,48,128]{2,1,0:T(8,128)S(1)}, f32[14,48,128]{2,1,0:T(8,128)S(1)}, u32[]{:S(2)}, u32[]{:S(2)}) collective-permute-start(f32[14,48,128]{2,1,0:T(8,128)S(1)} %get-tuple-element.80), channel_id=1, source_target_pairs={{16,0},{0,1},{18,2},{2,3},{20,4},{4,5},{22,6},{6,7},{24,8},{8,9},{... | collective-permute-start | bytes 1032200 | tf_op jit(solution)/shard_map/ppermute | solution.py:513
  36.1 2.5 %collective-permute-start.8 = (f32[8,128]{1,0:T(8,128)S(1)}, f32[8,128]{1,0:T(8,128)S(1)}, u32[]{:S(2)}, u32[]{:S(2)}) collective-permute-start(f32[8,128]{1,0:T(8,128)S(1)} %get-tuple-element.66.own), channel_id=1, source_target_pairs={{0,1},{1,2},{2,3},{3,4},{4,5},{5,6},{6,7},{7,8},{8,9},{9,10},{10,1... | collective-permute-start | bytes 12296 | tf_op jit(solution)/shard_map/ppermute | solution.py:513
  36.2 2.5 %collective-permute-start.9 = (f32[8,128]{1,0:T(8,128)S(1)}, f32[8,128]{1,0:T(8,128)S(1)}, u32[]{:S(2)}, u32[]{:S(2)}) collective-permute-start(f32[8,128]{1,0:T(8,128)S(1)} %get-tuple-element.66.own), channel_id=1, source_target_pairs={{1,0},{2,1},{3,2},{4,3},{5,4},{6,5},{7,6},{8,7},{9,8},{10,9},{11,1... | collective-permute-start | bytes 12296 | tf_op jit(solution)/shard_map/ppermute | solution.py:513
  38.7 4.8 %collective-permute-start.10 = (f32[8,128]{1,0:T(8,128)S(1)}, f32[8,128]{1,0:T(8,128)S(1)}, u32[]{:S(2)}, u32[]{:S(2)}) collective-permute-start(f32[8,128]{1,0:T(8,128)S(1)} %pack_last.1.own), channel_id=1, source_target_pairs={{0,16},{1,0},{2,18},{3,2},{4,20},{5,4},{6,22},{7,6},{8,24},{9,8},{... | collective-permute-start | bytes 12296 | tf_op jit(solution)/shard_map/ppermute | solution.py:513
  42.7 4.2 %collective-permute-start.11 = (f32[8,128]{1,0:T(8,128)S(1)}, f32[8,128]{1,0:T(8,128)S(1)}, u32[]{:S(2)}, u32[]{:S(2)}) collective-permute-start(f32[8,128]{1,0:T(8,128)S(1)} %pack_last.1.own), channel_id=1, source_target_pairs={{16,0},{0,1},{18,2},{2,3},{20,4},{4,5},{22,6},{6,7},{24,8},{8,9},{... | collective-permute-start | bytes 12296 | tf_op jit(solution)/shard_map/ppermute | solution.py:513

commit v9 on v8

--- a/solution.py
+++ b/solution.py
@@ -49,7 +49,7 @@
 
 
 def moves_up(axis):
-    return lax.axis_index(across_of(axis)) % 2 == 0
+    return lax.axis_index(across_of(axis)) // (2 if axis == "box" else 1) % 2 == 0
 
 
 def in_order(axis, first, second):
@@ -503,11 +503,12 @@
     route = []
     for source in range(sizes[0] * sizes[1]):
         at = list(divmod(source, sizes[1]))
-        step = 1 if at[1 - along] % 2 == 0 else -1
+        width = 2 if axis == "box" else 1
+        step = 1 if at[1 - along] // width % 2 == 0 else -1
         if 0 <= at[along] + step < sizes[along]:
             at[along] += step
         else:
-            at[1 - along] += step
+            at[1 - along] += step * width
         route.append((source, at[0] * sizes[1] + at[1]))
     inverse = [(target, source) for source, target in route]
     return lax.ppermute(first, names, route), lax.ppermute(second, names, inverse)

time: 48.2 us -> 48.3 us (level)
  the two profiles are of different devices: /device:TPU:101 before, /device:TPU:6 now
where the time goes in v9:
time: 48.3 us; the launch traced here: 48.1 us
  waiting for transfers between devices  28.3 us (59%)
  Pallas kernels  10 us (21%)
  starting transfers between devices  8.02 us (17%)
  other arithmetic  0.93 us (2%)
  between operations  0.74 us (2%)
    ppermute x6, waiting for transfers between devices, exchanged(): lax.ppermute(second, names, inverse)  18.3 us
    ppermute x6, waiting for transfers between devices, exchanged(): lax.ppermute(first, names, route)  10 us
    ppermute x6, starting transfers between devices, exchanged(): lax.ppermute(second, names, inverse)  5.71 us
    pallas_call x1, Pallas kernels, per_device(): call(fine_inner, [big] * 6 + [(16, 16, LANES)], [VMEM] * 3 + [HBM] * 3, s...  3.32 us
    ppermute x6, starting transfers between devices, exchanged(): lax.ppermute(first, names, route)  2.32 us
    pallas_call x1, Pallas kernels, per_device(): call(coarse_outer, [(8, 16, LANES), (4, 8, LANES), (2, 8, LANES), (8, LAN...  1.35 us
    pallas_call x1, Pallas kernels, per_device(): call(pack_rows, [tile, tile], [HBM] * 4, scratch=[pltpu.SMEM((1, 1, flags...  1.34 us
    pallas_call x1, Pallas kernels, per_device(): call(last_kernel, [(2, 2, 8), (2, 2, 8)], [VMEM] * 4, name='last')  1.03 us
  transfers between devices with their start and end apart: 12, of which 11 were waited for; matrix products, arithmetic and copies ran while one was open for 2% of the time, Pallas kernels for 12%

profile of v9, /device:TPU:6, one launch (start us, length us, event | category | flops | bytes accessed | tf_op | source)
XLA Modules:
  0.0 48.1 jit_solution(2043500119031719273)
XLA Ops:
  0.6 1.3 %pack_rows.1 = (f32[32,8,128]{2,1,0:T(8,128)S(1)}, f32[32,8,128]{2,1,0:T(8,128)S(1)}) custom-call(s32[1,1,4]{2,1,0:T(1,128)} %flags.1, f32[32,32,128]{2,1,0:T(8,128)} %guess.5, f32[32,32,128]{2,1,0:T(8,128)} %source.5, f32[32,32,128]{2,1,0:T(8,128)} %reaction.5), custom_call_target="tpu_custom_call" | custom-call | tf_op jit(solution)/shard_map/pack_rows/pallas_call | solution.py:540
  2.0 1.6 %collective-permute-start = (f32[32,8,128]{2,1,0:T(8,128)S(1)}, f32[32,8,128]{2,1,0:T(8,128)S(1)}, u32[]{:S(2)}, u32[]{:S(2)}) collective-permute-start(f32[32,8,128]{2,1,0:T(8,128)S(1)} %get-tuple-element.43.after.own_first), channel_id=1, source_target_pairs={{0,1},{1,2},{2,3},{3,4},{4,5},{5,6},{6,7},{7,8},{8,9},{9,10},{10,1... | collective-permute-start | bytes 393224 | tf_op jit(solution)/shard_map/ppermute | solution.py:514
  3.6 0.6 %collective-permute-start.1 = (f32[32,8,128]{2,1,0:T(8,128)S(1)}, f32[32,8,128]{2,1,0:T(8,128)S(1)}, u32[]{:S(2)}, u32[]{:S(2)}) collective-permute-start(f32[32,8,128]{2,1,0:T(8,128)S(1)} %get-tuple-element.44.own_second), channel_id=1, source_target_pairs={{1,0},{2,1},{3,2},{4,3},{5,4},{6,5},{7,6},{8,7},{9,8},{10,9},{11,1... | collective-permute-start | bytes 393224 | tf_op jit(solution)/shard_map/ppermute | solution.py:514
  4.1 0.9 %load_strips.1 = (f32[7,32,128]{2,1,0:T(8,128)S(1)}, f32[7,32,128]{2,1,0:T(8,128)S(1)}) custom-call(f32[32,8,128]{2,1,0:T(8,128)S(1)} %get-tuple-element.43.after.own_first, f32[32,32,128]{2,1,0:T(8,128)} %guess.5, f32[32,32,128]{2,1,0:T(8,128)} %source.5, f32[32,32,128]{2,1,0:T(8,128)} %reaction.5), custom_call_target="tpu_custom_call" | custom-call | tf_op jit(solution)/shard_map/load_strips/pallas_call | solution.py:548
  5.0 2.8 %collective-permute-done.from_first = f32[32,8,128]{2,1,0:T(8,128)S(1)} collective-permute-done((f32[32,8,128]{2,1,0:T(8,128)S(1)}, f32[32,8,128]{2,1,0:T(8,128)S(1)}, u32[]{:S(2)}, u32[]{:S(2)}) %collective-permute-start) | collective-permute-done | bytes 131104 | tf_op jit(solution)/shard_map/ppermute | solution.py:514
  7.8 2.8 %collective-permute-done.1.from_second = f32[32,8,128]{2,1,0:T(8,128)S(1)} collective-permute-done((f32[32,8,128]{2,1,0:T(8,128)S(1)}, f32[32,8,128]{2,1,0:T(8,128)S(1)}, u32[]{:S(2)}, u32[]{:S(2)}) %collective-permute-start.1) | collective-permute-done | bytes 131104 | tf_op jit(solution)/shard_map/ppermute | solution.py:514
  10.7 0.1 collective-permute-start.2
  10.8 0.5 %collective-permute-start.3 = (f32[7,40,128]{2,1,0:T(8,128)S(1)}, f32[7,40,128]{2,1,0:T(8,128)S(1)}, u32[]{:S(2)}, u32[]{:S(2)}) collective-permute-start(f32[7,40,128]{2,1,0:T(8,128)S(1)} %get-tuple-element.49), channel_id=1, source_target_pairs={{16,0},{17,1},{0,2},{1,3},{20,4},{21,5},{4,6},{5,7},{24,8},{25,9},... | collective-permute-start | bytes 430088 | tf_op jit(solution)/shard_map/ppermute | solution.py:514
  11.3 3.3 %fine_inner.1 = (f32[32,40,128]{2,1,0:T(8,128)S(1)}, f32[32,40,128]{2,1,0:T(8,128)S(1)}, f32[32,40,128]{2,1,0:T(8,128)S(1)}, f32[32,40,128]{2,1,0:T(8,128)S(1)},...) custom-call(f32[40,128]{1,0:T(8,128)S(1)} %get-tuple-element.47.mask_ref, ...), custom_call_target="tpu_custom_call" | custom-call | flops 8000000 | bytes 8000000 | tf_op jit(solution)/shard_map/fine_inner/pallas_call | solution.py:557
  14.7 2.8 %collective-permute-done.3.from_second = f32[7,40,128]{2,1,0:T(8,128)S(1)} collective-permute-done((f32[7,40,128]{2,1,0:T(8,128)S(1)}, f32[7,40,128]{2,1,0:T(8,128)S(1)}, u32[]{:S(2)}, u32[]{:S(2)}) %collective-permute-start.3) | collective-permute-done | bytes 143392 | tf_op jit(solution)/shard_map/ppermute | solution.py:514
  17.5 0.5 %fine_outer.1 = (f32[16,16,128]{2,1,0:T(8,128)S(1)}, f32[4,32,128]{2,1,0:T(8,128)S(1)}) custom-call(f32[40,128]{1,0:T(8,128)S(1)} %get-tuple-element.47.mask_ref, f32[7,40,128]{2,1,0:T(8,128)S(1)} %collective-permute-done.2.from_first, f32[7,40,128]{2,1,0:T(8,128)S(1)} %collective-permute-done.3.from_second, f32[32,40,128]{2,1,0:T(8,128)S(1)} %get-tuple-element.50.g, ...), custom_call_target="tpu_custom_call" | custom-call | tf_op jit(solution)/shard_map/fine_outer/pallas_call | solution.py:566
  18.0 0.4 collective-permute-start.4
  18.4 1.6 %collective-permute-start.5 = (f32[16,16,128]{2,1,0:T(8,128)S(1)}, f32[16,16,128]{2,1,0:T(8,128)S(1)}, u32[]{:S(2)}, u32[]{:S(2)}) collective-permute-start(f32[16,16,128]{2,1,0:T(8,128)S(1)} %get-tuple-element.57.own), channel_id=1, source_target_pairs={{1,0},{2,1},{3,2},{4,3},{5,4},{6,5},{7,6},{8,7},{9,8},{10,9},{11,1... | collective-permute-start | bytes 393224 | tf_op jit(solution)/shard_map/ppermute | solution.py:514
  20.1 0.8 %pad_maximum_fusion = f32[32,32,128]{2,1,0:T(8,128)} fusion(f32[2,32,128]{2,1,0:T(8,128)S(1)} %get-tuple-element.85, f32[28,32,128]{2,1,0:T(8,128)S(1)} %slice.16, f32[2,32,128]{2,1,0:T(8,128)S(1)} %get-tuple-element.84), kind=kLoop, calls=%fused_computation | loop fusion | flops 262144 | bytes 1048576 | tf_op jit(solution)/shard_map/concatenate | solution.py:573
  20.9 2.1 %collective-permute-done.4 = f32[16,16,128]{2,1,0:T(8,128)S(1)} collective-permute-done((f32[16,16,128]{2,1,0:T(8,128)S(1)}, f32[16,16,128]{2,1,0:T(8,128)S(1)}, u32[]{:S(2)}, u32[]{:S(2)}) %collective-permute-start.4) | collective-permute-done | bytes 131104 | tf_op jit(solution)/shard_map/ppermute | solution.py:514
  23.0 2.5 %collective-permute-done.5 = f32[16,16,128]{2,1,0:T(8,128)S(1)} collective-permute-done((f32[16,16,128]{2,1,0:T(8,128)S(1)}, f32[16,16,128]{2,1,0:T(8,128)S(1)}, u32[]{:S(2)}, u32[]{:S(2)}) %collective-permute-start.5) | collective-permute-done | bytes 131104 | tf_op jit(solution)/shard_map/ppermute | solution.py:514
  25.6 0.1 collective-permute-start.6
  25.7 0.5 %collective-permute-start.7 = (f32[14,48,128]{2,1,0:T(8,128)S(1)}, f32[14,48,128]{2,1,0:T(8,128)S(1)}, u32[]{:S(2)}, u32[]{:S(2)}) collective-permute-start(f32[14,48,128]{2,1,0:T(8,128)S(1)} %get-tuple-element.80), channel_id=1, source_target_pairs={{16,0},{17,1},{0,2},{1,3},{20,4},{21,5},{4,6},{5,7},{24,8},{25,9},... | collective-permute-start | bytes 1032200 | tf_op jit(solution)/shard_map/ppermute | solution.py:514
  26.2 0.6 %coarse_inner.1 = (f32[2,48,128]{2,1,0:T(8,128)S(1)}, f32[2,48,128]{2,1,0:T(8,128)S(1)}, f32[8,48,128]{2,1,0:T(8,128)S(1)}, f32[3,24,128]{2,1,0:T(8,128)S(1)}, f32[3,24,128]{2,1,0:T(8,128)S(1)}) custom-call(f32[16,16,128]{2,1,0:T(8,128)S(1)} %get-tuple-element.82.y_before, f32[16,16,128]{2,1,0:T(8,128)S(1)} %get-tuple-element.57.own, ...), custom_call_target="tpu_custom_call" | custom-call | flops 4000000 | bytes 4000000 | tf_op jit(solution)/shard_map/coarse_inner/pallas_call | solution.py:580
  26.8 3.7 %collective-permute-done.6.from_first = f32[14,48,128]{2,1,0:T(8,128)S(1)} collective-permute-done((f32[14,48,128]{2,1,0:T(8,128)S(1)}, f32[14,48,128]{2,1,0:T(8,128)S(1)}, u32[]{:S(2)}, u32[]{:S(2)}) %collective-permute-start.6) | collective-permute-done | bytes 344096 | tf_op jit(solution)/shard_map/ppermute | solution.py:514
  30.5 4.1 %collective-permute-done.7.from_second = f32[14,48,128]{2,1,0:T(8,128)S(1)} collective-permute-done((f32[14,48,128]{2,1,0:T(8,128)S(1)}, f32[14,48,128]{2,1,0:T(8,128)S(1)}, u32[]{:S(2)}, u32[]{:S(2)}) %collective-permute-start.7) | collective-permute-done | bytes 344096 | tf_op jit(solution)/shard_map/ppermute | solution.py:514
  34.6 1.3 %coarse_outer.1 = (f32[8,16,128]{2,1,0:T(8,128)S(1)}, f32[4,8,128]{2,1,0:T(8,128)S(1)}, f32[2,8,128]{2,1,0:T(8,128)S(1)}, f32[8,128]{1,0:T(8,128)S(1)}, f32[2,8,128]{2,1,0:T(8,128)S(1)}) custom-call(f32[14,48,128]{2,1,0:T(8,128)S(1)} %collective-permute-done.6.from_first, f32[14,48,128]{2,1,0:T(8,128)S(1)} %collective-permute-done.7.from_second, ...), custom_call_target="tpu_custom_call" | custom-call | tf_op jit(solution)/shard_map/coarse_outer/pallas_call | solution.py:588
  35.9 0.0 collective-permute-start.8
  36.0 2.0 %collective-permute-start.9 = (f32[8,128]{1,0:T(8,128)S(1)}, f32[8,128]{1,0:T(8,128)S(1)}, u32[]{:S(2)}, u32[]{:S(2)}) collective-permute-start(f32[8,128]{1,0:T(8,128)S(1)} %get-tuple-element.66.own), channel_id=1, source_target_pairs={{1,0},{2,1},{3,2},{4,3},{5,4},{6,5},{7,6},{8,7},{9,8},{10,9},{11,1... | collective-permute-start | bytes 12296 | tf_op jit(solution)/shard_map/ppermute | solution.py:514
  38.0 1.0 %unfold.1 = (f32[16,16,64]{2,1,0:T(8,128)}, f32[8,8,32]{2,1,0:T(8,128)}, f32[4,4,16]{2,1,0:T(4,128)}) custom-call(f32[8,16,128]{2,1,0:T(8,128)S(1)} %get-tuple-element.67.own1, f32[4,8,128]{2,1,0:T(8,128)S(1)} %get-tuple-element.68.own2, f32[2,8,128]{2,1,0:T(8,128)S(1)} %get-tuple-element.69.own3), custom_call_target="tpu_custom_call" | custom-call | flops 2000000 | bytes 2000000 | tf_op jit(solution)/shard_map/unfold/pallas_call | solution.py:595
  39.0 0.6 %collective-permute-done.8.from_first = f32[8,128]{1,0:T(8,128)S(1)} collective-permute-done((f32[8,128]{1,0:T(8,128)S(1)}, f32[8,128]{1,0:T(8,128)S(1)}, u32[]{:S(2)}, u32[]{:S(2)}) %collective-permute-start.8) | collective-permute-done | bytes 4128 | tf_op jit(solution)/shard_map/ppermute | solution.py:514
  39.6 2.2 %collective-permute-done.9.from_second = f32[8,128]{1,0:T(8,128)S(1)} collective-permute-done((f32[8,128]{1,0:T(8,128)S(1)}, f32[8,128]{1,0:T(8,128)S(1)}, u32[]{:S(2)}, u32[]{:S(2)}) %collective-permute-start.9) | collective-permute-done | bytes 4128 | tf_op jit(solution)/shard_map/ppermute | solution.py:514
  41.8 0.1 collective-permute-start.10
  41.9 0.5 %collective-permute-start.11 = (f32[8,128]{1,0:T(8,128)S(1)}, f32[8,128]{1,0:T(8,128)S(1)}, u32[]{:S(2)}, u32[]{:S(2)}) collective-permute-start(f32[8,128]{1,0:T(8,128)S(1)} %pack_last.1.own), channel_id=1, source_target_pairs={{16,0},{17,1},{0,2},{1,3},{20,4},{21,5},{4,6},{5,7},{24,8},{25,9},... | collective-permute-start | bytes 12296 | tf_op jit(solution)/shard_map/ppermute | solution.py:514
  42.4 0.8 %collective-permute-done.10.from_first = f32[8,128]{1,0:T(8,128)S(1)} collective-permute-done((f32[8,128]{1,0:T(8,128)S(1)}, f32[8,128]{1,0:T(8,128)S(1)}, u32[]{:S(2)}, u32[]{:S(2)}) %collective-permute-start.10) | collective-permute-done | bytes 4128 | tf_op jit(solution)/shard_map/ppermute | solution.py:514
  43.2 3.9 %collective-permute-done.11.from_second = f32[8,128]{1,0:T(8,128)S(1)} collective-permute-done((f32[8,128]{1,0:T(8,128)S(1)}, f32[8,128]{1,0:T(8,128)S(1)}, u32[]{:S(2)}, u32[]{:S(2)}) %collective-permute-start.11) | collective-permute-done | bytes 4128 | tf_op jit(solution)/shard_map/ppermute | solution.py:514
  47.1 1.0 %last.1 = (f32[2,2,8]{2,1,0:T(2,128)}, f32[2,2,8]{2,1,0:T(2,128)}) custom-call(f32[8,128]{1,0:T(8,128)S(1)} %pack_last.1.own, f32[8,128]{1,0:T(8,128)S(1)} %collective-permute-done.10.from_first, f32[8,128]{1,0:T(8,128)S(1)} %collective-permute-done.11.from_second, f32[2,8,128]{2,1,0:T(8,128)S(1)} %get-tuple-element.77.k4), custom_call_target="tpu_custom_call" | custom-call | tf_op jit(solution)/shard_map/last/pallas_call | solution.py:602
  (8 shorter events, 0.2 us)
Async XLA Ops:
  2.0 5.9 %collective-permute-start = (f32[32,8,128]{2,1,0:T(8,128)S(1)}, f32[32,8,128]{2,1,0:T(8,128)S(1)}, u32[]{:S(2)}, u32[]{:S(2)}) collective-permute-start(f32[32,8,128]{2,1,0:T(8,128)S(1)} %get-tuple-element.43.after.own_first), channel_id=1, source_target_pairs={{0,1},{1,2},{2,3},{3,4},{4,5},{5,6},{6,7},{7,8},{8,9},{9,10},{10,1... | collective-permute-start | bytes 393224 | tf_op jit(solution)/shard_map/ppermute | solution.py:514
  3.6 7.1 %collective-permute-start.1 = (f32[32,8,128]{2,1,0:T(8,128)S(1)}, f32[32,8,128]{2,1,0:T(8,128)S(1)}, u32[]{:S(2)}, u32[]{:S(2)}) collective-permute-start(f32[32,8,128]{2,1,0:T(8,128)S(1)} %get-tuple-element.44.own_second), channel_id=1, source_target_pairs={{1,0},{2,1},{3,2},{4,3},{5,4},{6,5},{7,6},{8,7},{9,8},{10,9},{11,1... | collective-permute-start | bytes 393224 | tf_op jit(solution)/shard_map/ppermute | solution.py:514
  10.7 4.0 %collective-permute-start.2 = (f32[7,40,128]{2,1,0:T(8,128)S(1)}, f32[7,40,128]{2,1,0:T(8,128)S(1)}, u32[]{:S(2)}, u32[]{:S(2)}) collective-permute-start(f32[7,40,128]{2,1,0:T(8,128)S(1)} %get-tuple-element.48), channel_id=1, source_target_pairs={{0,16},{1,17},{2,0},{3,1},{4,20},{5,21},{6,4},{7,5},{8,24},{9,25},... | collective-permute-start | bytes 430088 | tf_op jit(solution)/shard_map/ppermute | solution.py:514
  10.8 6.7 %collective-permute-start.3 = (f32[7,40,128]{2,1,0:T(8,128)S(1)}, f32[7,40,128]{2,1,0:T(8,128)S(1)}, u32[]{:S(2)}, u32[]{:S(2)}) collective-permute-start(f32[7,40,128]{2,1,0:T(8,128)S(1)} %get-tuple-element.49), channel_id=1, source_target_pairs={{16,0},{17,1},{0,2},{1,3},{20,4},{21,5},{4,6},{5,7},{24,8},{25,9},... | collective-permute-start | bytes 430088 | tf_op jit(solution)/shard_map/ppermute | solution.py:514
  18.0 5.0 %collective-permute-start.4 = (f32[16,16,128]{2,1,0:T(8,128)S(1)}, f32[16,16,128]{2,1,0:T(8,128)S(1)}, u32[]{:S(2)}, u32[]{:S(2)}) collective-permute-start(f32[16,16,128]{2,1,0:T(8,128)S(1)} %get-tuple-element.57.own), channel_id=1, source_target_pairs={{0,1},{1,2},{2,3},{3,4},{4,5},{5,6},{6,7},{7,8},{8,9},{9,10},{10,1... | collective-permute-start | bytes 393224 | tf_op jit(solution)/shard_map/ppermute | solution.py:514
  18.4 7.1 %collective-permute-start.5 = (f32[16,16,128]{2,1,0:T(8,128)S(1)}, f32[16,16,128]{2,1,0:T(8,128)S(1)}, u32[]{:S(2)}, u32[]{:S(2)}) collective-permute-start(f32[16,16,128]{2,1,0:T(8,128)S(1)} %get-tuple-element.57.own), channel_id=1, source_target_pairs={{1,0},{2,1},{3,2},{4,3},{5,4},{6,5},{7,6},{8,7},{9,8},{10,9},{11,1... | collective-permute-start | bytes 393224 | tf_op jit(solution)/shard_map/ppermute | solution.py:514
  25.6 4.9 %collective-permute-start.6 = (f32[14,48,128]{2,1,0:T(8,128)S(1)}, f32[14,48,128]{2,1,0:T(8,128)S(1)}, u32[]{:S(2)}, u32[]{:S(2)}) collective-permute-start(f32[14,48,128]{2,1,0:T(8,128)S(1)} %get-tuple-element.81), channel_id=1, source_target_pairs={{0,16},{1,17},{2,0},{3,1},{4,20},{5,21},{6,4},{7,5},{8,24},{9,25},... | collective-permute-start | bytes 1032200 | tf_op jit(solution)/shard_map/ppermute | solution.py:514
  25.7 8.9 %collective-permute-start.7 = (f32[14,48,128]{2,1,0:T(8,128)S(1)}, f32[14,48,128]{2,1,0:T(8,128)S(1)}, u32[]{:S(2)}, u32[]{:S(2)}) collective-permute-start(f32[14,48,128]{2,1,0:T(8,128)S(1)} %get-tuple-element.80), channel_id=1, source_target_pairs={{16,0},{17,1},{0,2},{1,3},{20,4},{21,5},{4,6},{5,7},{24,8},{25,9},... | collective-permute-start | bytes 1032200 | tf_op jit(solution)/shard_map/ppermute | solution.py:514
  35.9 3.6 %collective-permute-start.8 = (f32[8,128]{1,0:T(8,128)S(1)}, f32[8,128]{1,0:T(8,128)S(1)}, u32[]{:S(2)}, u32[]{:S(2)}) collective-permute-start(f32[8,128]{1,0:T(8,128)S(1)} %get-tuple-element.66.own), channel_id=1, source_target_pairs={{0,1},{1,2},{2,3},{3,4},{4,5},{5,6},{6,7},{7,8},{8,9},{9,10},{10,1... | collective-permute-start | bytes 12296 | tf_op jit(solution)/shard_map/ppermute | solution.py:514
  36.0 5.8 %collective-permute-start.9 = (f32[8,128]{1,0:T(8,128)S(1)}, f32[8,128]{1,0:T(8,128)S(1)}, u32[]{:S(2)}, u32[]{:S(2)}) collective-permute-start(f32[8,128]{1,0:T(8,128)S(1)} %get-tuple-element.66.own), channel_id=1, source_target_pairs={{1,0},{2,1},{3,2},{4,3},{5,4},{6,5},{7,6},{8,7},{9,8},{10,9},{11,1... | collective-permute-start | bytes 12296 | tf_op jit(solution)/shard_map/ppermute | solution.py:514
  41.8 1.4 %collective-permute-start.10 = (f32[8,128]{1,0:T(8,128)S(1)}, f32[8,128]{1,0:T(8,128)S(1)}, u32[]{:S(2)}, u32[]{:S(2)}) collective-permute-start(f32[8,128]{1,0:T(8,128)S(1)} %pack_last.1.own), channel_id=1, source_target_pairs={{0,16},{1,17},{2,0},{3,1},{4,20},{5,21},{6,4},{7,5},{8,24},{9,25},... | collective-permute-start | bytes 12296 | tf_op jit(solution)/shard_map/ppermute | solution.py:514
  41.9 5.2 %collective-permute-start.11 = (f32[8,128]{1,0:T(8,128)S(1)}, f32[8,128]{1,0:T(8,128)S(1)}, u32[]{:S(2)}, u32[]{:S(2)}) collective-permute-start(f32[8,128]{1,0:T(8,128)S(1)} %pack_last.1.own), channel_id=1, source_target_pairs={{16,0},{17,1},{0,2},{1,3},{20,4},{21,5},{4,6},{5,7},{24,8},{25,9},... | collective-permute-start | bytes 12296 | tf_op jit(solution)/shard_map/ppermute | solution.py:514
